TPU v7x, 32 devices: a whole 2x2x4 slice. The times are simulated.
32 devices in a mesh: ens: 2 (over core), gx: 4 (over y, x), gy: 4 (over z).
Axes of the slice: x: 2, y: 2, z: 4, core: 2. Of those that a mesh axis runs over, the one named last changes fastest.
Arguments:
- velocity: float32 [2, 2, 1024, 512], P('ens', None, 'gx', 'gy'), may hold values from -6 to 6
- targets: float32 [2, 2, 2, 1024, 512], P('ens', None, None, 'gx', 'gy'), may hold values from -6 to 6
- weight_one: bfloat16 [3, 3, 2, 64], replicated, may hold values from -1.5 to 1.5
- bias_one: float32 [64], replicated, may hold values from -3 to 3
- weight_two: bfloat16 [64, 64], replicated, may hold values from -0.75 to 0.75
- bias_two: float32 [64], replicated, may hold values from -3 to 3
- weight_three: bfloat16 [3, 3, 64, 6], replicated, may hold values from -0.25 to 0.25
Outputs:
- dir_weight_one: float32 [3, 3, 2, 64], replicated
- dir_bias_one: float32 [64], replicated
- dir_weight_two: float32 [64, 64], replicated
- dir_bias_two: float32 [64], replicated
- dir_weight_three: float32 [3, 3, 64, 6], replicated
- mean_loss: float32 [], replicated
- grad_velocity: float32 [2, 2, 1024, 512], P('ens', None, 'gx', 'gy')
All inputs are finite; a program needn't handle non-finite values.
Results may differ from a plain program's by a relative error of at most 0.0015.
Values sent between devices are 32-bit elements; how exact they have to be, the bound alone decides.
No kernel may reach another device: no remote copies, remote signals or barrier semaphores. Data moves between devices by JAX's collectives and lax.ppermute only.
A program may use at most 256 MiB of HBM per device.

v0:
```python
import jax
import jax.numpy as jnp
from jax import lax
from jax.sharding import PartitionSpec as P

SWEEPS = 16


TIME_STEP = 0.2
VISCOSITY = 0.05
DRAG_RATE = 0.1
FORCE_WAVES = 4.0
COEF_SCALE = 0.1
EPSILON = 1e-06
RIM_WIDTH = 4
OUTER_WEIGHT = -1.0 / 16.0
INNER_WEIGHT = 9.0 / 16.0
TWO_PI = 6.283185307179586


def with_halo(value, sides, width):
    for axis, dim in sides:
        size, length = (lax.axis_size(axis), value.shape[dim])
        up = [(i, (i + 1) % size) for i in range(size)]
        down = [(j, i) for i, j in up]
        last = lax.slice_in_dim(value, length - width, length, axis=dim)
        initial = lax.slice_in_dim(value, 0, width, axis=dim)
        before = lax.ppermute(last, axis, up)
        after = lax.ppermute(initial, axis, down)
        value = jnp.concatenate([before, value, after], axis=dim)
    return value


def passed_along(block, axis, distance):
    devices = range(lax.axis_size(axis))
    route = [((i - distance) % len(devices), i) for i in devices]
    return lax.ppermute(block, axis, route)


def silu_slope(values):
    logistic = jax.nn.sigmoid(values)
    return logistic * (1.0 + values * (1.0 - logistic))


def tap_offsets(width):
    offsets = []
    for offset_row in range(3):
        for offset_col in range(3):
            offsets.append(offset_row * width + offset_col)
    return offsets


def network(padded, weight_one, bias_one, weight_two, bias_two, weight_three):
    height = padded.shape[1]
    width = padded.shape[2]
    flat_in = padded.astype(jnp.bfloat16).reshape(padded.shape[0], height * width)
    len_one = (height - 2) * width - 2
    len_two = (height - 4) * width - 4
    offsets = tap_offsets(width)
    columns = jnp.concatenate([flat_in[:, start : start + len_one] for start in offsets], axis=0)
    kernel_one = weight_one.reshape(-1, weight_one.shape[3])
    pre_one = (
        jnp.einsum("kh,kp->hp", kernel_one, columns, preferred_element_type=jnp.float32)
        + bias_one[:, None]
    )
    hidden_one = jax.nn.silu(pre_one).astype(jnp.bfloat16)
    pre_two = (
        jnp.einsum("hg,hp->gp", weight_two, hidden_one, preferred_element_type=jnp.float32)
        + bias_two[:, None]
    )
    hidden_two = jax.nn.silu(pre_two).astype(jnp.bfloat16)
    kernel_three = weight_three.reshape(9, weight_three.shape[2], weight_three.shape[3])
    tap_terms = jnp.einsum(
        "khn,hp->knp", kernel_three, hidden_two, preferred_element_type=jnp.float32
    )
    summed = tap_terms[0, :, 0:len_two]
    for tap_index in range(1, 9):
        start = offsets[tap_index]
        summed = summed + tap_terms[tap_index, :, start : start + len_two]
    flat_coef = COEF_SCALE * summed
    grid_coef = jnp.pad(flat_coef, ((0, 0), (0, 4))).reshape(flat_coef.shape[0], height - 4, width)
    coefficients = grid_coef[:, :, : width - 4]
    return (
        columns,
        kernel_one,
        pre_one,
        hidden_one,
        pre_two,
        hidden_two,
        kernel_three,
        coefficients,
    )


def network_backward(saved_values, weight_two, grad_coef):
    columns, kernel_one, pre_one, hidden_one, pre_two, hidden_two, kernel_three, coefficients = (
        saved_values
    )
    height = coefficients.shape[1] + 4
    width = coefficients.shape[2] + 4
    len_one = hidden_two.shape[1]
    len_two = (height - 4) * width - 4
    spare = len_one - len_two
    offsets = tap_offsets(width)
    grid_taps = (COEF_SCALE * grad_coef).astype(jnp.bfloat16)
    grid_taps = jnp.pad(grid_taps, ((0, 0), (0, 0), (0, 4)))
    grad_taps = grid_taps.reshape(grid_taps.shape[0], (height - 4) * width)[:, :len_two]
    three_parts = []
    spread = []
    for tap_index in range(9):
        start = offsets[tap_index]
        window = hidden_two[:, start : start + len_two]
        three_parts.append(
            jnp.einsum("hp,np->hn", window, grad_taps, preferred_element_type=jnp.float32)
        )
        spread.append(jnp.pad(grad_taps, ((0, 0), (start, spare - start))))
    grad_three = jnp.stack(three_parts).reshape(3, 3, hidden_two.shape[0], grad_taps.shape[0])
    spread_taps = jnp.stack(spread)
    grad_hidden_two = jnp.einsum(
        "khn,knp->hp", kernel_three, spread_taps, preferred_element_type=jnp.float32
    )
    grad_pre_two = (grad_hidden_two * silu_slope(pre_two)).astype(jnp.bfloat16)
    grad_two = jnp.einsum("hp,gp->hg", hidden_one, grad_pre_two, preferred_element_type=jnp.float32)
    grad_bias_two = jnp.sum(grad_pre_two, axis=1, dtype=jnp.float32)
    grad_hidden_one = jnp.einsum(
        "hg,gp->hp", weight_two, grad_pre_two, preferred_element_type=jnp.float32
    )
    grad_pre_one = (grad_hidden_one * silu_slope(pre_one)).astype(jnp.bfloat16)
    channels = columns.shape[0] // 9
    grad_one = jnp.einsum(
        "kp,hp->kh", columns, grad_pre_one, preferred_element_type=jnp.float32
    ).reshape(3, 3, channels, grad_pre_one.shape[0])
    grad_bias_one = jnp.sum(grad_pre_one, axis=1, dtype=jnp.float32)
    grad_input = None
    grad_columns = jnp.einsum(
        "kh,hp->kp", kernel_one, grad_pre_one, preferred_element_type=jnp.float32
    )
    in_spare = height * width - len_one
    flat_input = None
    for tap_index in range(9):
        start = offsets[tap_index]
        term = jnp.pad(
            grad_columns[tap_index * channels : (tap_index + 1) * channels],
            ((0, 0), (start, in_spare - start)),
        )
        flat_input = term if flat_input is None else flat_input + term
    grad_input = flat_input.reshape(channels, height, width)
    return (grad_input, (grad_one, grad_bias_one, grad_two, grad_bias_two, grad_three))


def advect(padded, coefficients, forcing):
    current = padded[:, 1:-1, 1:-1]
    span_rows = current.shape[1] - 6
    span_cols = current.shape[2] - 6
    across = current[:, :, 2 : span_cols + 4]
    cell_one = across[:, 0 : span_rows + 3]
    cell_two = across[:, 1 : span_rows + 4]
    cell_three = across[:, 2 : span_rows + 5]
    cell_four = across[:, 3 : span_rows + 6]
    adjust_one = coefficients[0, 0 : span_rows + 3, 1 : span_cols + 3]
    adjust_two = coefficients[1, 0 : span_rows + 3, 1 : span_cols + 3]
    adjust_three = coefficients[2, 0 : span_rows + 3, 1 : span_cols + 3]
    face_value = (
        (OUTER_WEIGHT + adjust_one) * cell_one
        + (INNER_WEIGHT + adjust_two) * cell_two
        + (INNER_WEIGHT + adjust_three) * cell_three
        + (OUTER_WEIGHT - adjust_one - adjust_two - adjust_three) * cell_four
    )
    face_speed = 0.5 * (cell_two[0] + cell_three[0])
    flux_rows = face_speed * face_value
    change = flux_rows[:, 1:] - flux_rows[:, :-1]
    along_cols = current[:, 2 : span_rows + 4, :]
    cell_one = along_cols[:, :, 0 : span_cols + 3]
    cell_two = along_cols[:, :, 1 : span_cols + 4]
    cell_three = along_cols[:, :, 2 : span_cols + 5]
    cell_four = along_cols[:, :, 3 : span_cols + 6]
    adjust_one = coefficients[3, 1 : span_rows + 3, 0 : span_cols + 3]
    adjust_two = coefficients[4, 1 : span_rows + 3, 0 : span_cols + 3]
    adjust_three = coefficients[5, 1 : span_rows + 3, 0 : span_cols + 3]
    face_value = (
        (OUTER_WEIGHT + adjust_one) * cell_one
        + (INNER_WEIGHT + adjust_two) * cell_two
        + (INNER_WEIGHT + adjust_three) * cell_three
        + (OUTER_WEIGHT - adjust_one - adjust_two - adjust_three) * cell_four
    )
    face_speed = 0.5 * (cell_two[1] + cell_three[1])
    flux_cols = face_speed * face_value
    change = change + (flux_cols[:, :, 1:] - flux_cols[:, :, :-1])
    center = current[:, 2 : span_rows + 4, 2 : span_cols + 4]
    laplace = (
        current[:, 1 : span_rows + 3, 2 : span_cols + 4]
        + current[:, 3 : span_rows + 5, 2 : span_cols + 4]
        + current[:, 2 : span_rows + 4, 1 : span_cols + 3]
        + current[:, 2 : span_rows + 4, 3 : span_cols + 5]
        - 4.0 * center
    )
    return (
        center
        - TIME_STEP * change
        + TIME_STEP * (VISCOSITY * laplace - DRAG_RATE * center + forcing)
    )


def neighbours(field_in):
    return (
        field_in[:, 2:, 1:-1]
        + field_in[:, :-2, 1:-1]
        + field_in[:, 1:-1, 2:]
        + field_in[:, 1:-1, :-2]
    )


def divergence(extended):
    return 0.5 * (
        extended[0:1, 2:, 1:-1]
        - extended[0:1, :-2, 1:-1]
        + extended[1:2, 1:-1, 2:]
        - extended[1:2, 1:-1, :-2]
    )


def state_rim(current):
    return with_halo(current, (("gx", 1), ("gy", 2)), RIM_WIDTH)


def edge_rim(field_in):
    return with_halo(field_in, (("gx", 1), ("gy", 2)), 1)


def pressure_push(pressure):
    extended = edge_rim(pressure)
    return jnp.concatenate(
        [
            0.5 * (extended[:, 2:, 1:-1] - extended[:, :-2, 1:-1]),
            0.5 * (extended[:, 1:-1, 2:] - extended[:, 1:-1, :-2]),
        ],
        axis=0,
    )


def pressure_solve(divergence_field):
    initial = -0.25 * divergence_field

    def one_sweep(sweep_index, pressure):
        return 0.25 * neighbours(edge_rim(pressure)) - 0.25 * divergence_field

    return lax.fori_loop(0, SWEEPS, one_sweep, initial)


def pressure_adjoint(grad_pressure):
    zero_div = jnp.zeros_like(grad_pressure)

    def one_sweep(sweep_index, carried):
        cotangent, grad_div = carried
        grad_div = grad_div - 0.25 * cotangent
        return (0.25 * neighbours(edge_rim(cotangent)), grad_div)

    cotangent, grad_div = lax.fori_loop(0, SWEEPS, one_sweep, (grad_pressure, zero_div))
    return grad_div - 0.25 * cotangent


def step_forward(padded, weights, forcing):
    saved_values = network(padded, weights[0], weights[1], weights[2], weights[3], weights[4])
    provisional = advect(padded, saved_values[-1], forcing)
    pressure = pressure_solve(divergence(provisional))
    return provisional[:, 1:-1, 1:-1] - pressure_push(pressure)


def step_backward(padded, weights, forcing, grad_state):
    grad_pressure = divergence(edge_rim(grad_state))
    grad_div = pressure_adjoint(grad_pressure)
    saved_values = network(padded, weights[0], weights[1], weights[2], weights[3], weights[4])

    def advect_inputs(padded_in, coef_in):
        return advect(padded_in, coef_in, forcing)

    provisional, advect_pull = jax.vjp(advect_inputs, padded, saved_values[-1])
    unused, divergence_pull = jax.vjp(divergence, provisional)
    grad_provisional = divergence_pull(grad_div)[0]
    grad_provisional = grad_provisional.at[:, 1:-1, 1:-1].add(grad_state)
    grad_padded, grad_coef = advect_pull(grad_provisional)
    grad_input, step_grads = network_backward(saved_values, weights[2], grad_coef)
    grad_padded = grad_padded + grad_input
    return (grad_padded, step_grads)


def fold_rims(grad_padded):
    low_rim = grad_padded[:, :, :RIM_WIDTH]
    high_rim = grad_padded[:, :, -RIM_WIDTH:]
    middle = grad_padded[:, :, RIM_WIDTH:-RIM_WIDTH]
    from_next = passed_along(low_rim, "gy", -1)
    from_prev = passed_along(high_rim, "gy", 1)
    middle = middle.at[:, :, :RIM_WIDTH].add(from_prev)
    middle = middle.at[:, :, -RIM_WIDTH:].add(from_next)
    low_rim = middle[:, :RIM_WIDTH, :]
    high_rim = middle[:, -RIM_WIDTH:, :]
    result = middle[:, RIM_WIDTH:-RIM_WIDTH, :]
    from_next = passed_along(low_rim, "gx", -1)
    from_prev = passed_along(high_rim, "gx", 1)
    result = result.at[:, :RIM_WIDTH, :].add(from_prev)
    result = result.at[:, -RIM_WIDTH:, :].add(from_next)
    return result


def make_forcing(span_rows, span_cols):
    total_cols = span_cols * lax.axis_size("gy")
    col_ids = lax.axis_index("gy") * span_cols + jnp.arange(span_cols + 2, dtype=jnp.int32) - 1
    phase_angle = col_ids.astype(jnp.float32) * (TWO_PI * FORCE_WAVES / total_cols)
    force_row = jnp.broadcast_to(jnp.sin(phase_angle)[None, :], (span_rows + 2, span_cols + 2))
    return jnp.stack([force_row, jnp.zeros_like(force_row)])


def normalize(flat_grads, lengths):
    pieces = []
    offset = 0
    for length in lengths:
        segment = flat_grads[offset : offset + length]
        pieces.append(segment * (1.0 / jnp.sqrt(jnp.mean(jnp.square(segment)) + EPSILON)))
        offset += length
    return pieces


def shards(velocity, targets, weight_one, bias_one, weight_two, bias_two, weight_three):
    weights = (weight_one, bias_one, weight_two, bias_two, weight_three)
    current = velocity[0]
    goal_fields = targets[0]
    step_count = goal_fields.shape[0]
    span_rows = current.shape[1]
    span_cols = current.shape[2]
    forcing = make_forcing(span_rows, span_cols)
    history = [current]
    kept_padded = []
    local_loss = jnp.zeros((), jnp.float32)
    for step_index in range(step_count):
        padded = state_rim(current)
        kept_padded.append(padded)
        current = step_forward(padded, weights, forcing)
        history.append(current)
        local_loss = local_loss + 0.5 * jnp.sum(jnp.square(current - goal_fields[step_index]))
    grad_state = jnp.zeros_like(current)
    grad_sums = None
    for step_index in range(step_count - 1, -1, -1):
        grad_state = grad_state + (history[step_index + 1] - goal_fields[step_index])
        padded = state_rim(history[step_index])
        grad_padded, step_grads = step_backward(padded, weights, forcing, grad_state)
        if grad_sums is None:
            grad_sums = step_grads
        else:
            grad_sums = jax.tree.map(jnp.add, grad_sums, step_grads)
        grad_state = fold_rims(grad_padded)
    lengths = [int(tensor.size) for tensor in grad_sums]
    flat_grads = jnp.concatenate([tensor.reshape(-1) for tensor in grad_sums])
    device_count = lax.axis_size(("ens", "gx", "gy"))
    loss_scale = 1.0 / float(step_count * 2 * span_rows * span_cols * device_count)
    total_grads, total_loss = lax.psum((flat_grads, local_loss), ("ens", "gx", "gy"))
    pieces = normalize(total_grads, lengths)
    outputs = [piece.reshape(tensor.shape) for piece, tensor in zip(pieces, grad_sums)]
    mean_loss = total_loss * loss_scale
    return (outputs[0], outputs[1], outputs[2], outputs[3], outputs[4], mean_loss, grad_state[None])


def solution(mesh):
    return jax.shard_map(
        shards,
        mesh=mesh,
        in_specs=(
            P("ens", None, "gx", "gy"),
            P("ens", None, None, "gx", "gy"),
            P(),
            P(),
            P(),
            P(),
            P(),
        ),
        out_specs=(P(), P(), P(), P(), P(), P(), P("ens", None, "gx", "gy")),
        check_vma=False,
    )
```

profile of v0, /device:TPU:0, one launch (start us, length us, event | category | flops | bytes accessed | tf_op | source)
XLA Modules:
  0.0 1468.4 jit_solution(1928468684055226869)
XLA Ops:
  13.7 6.6 collective-permute-done.18
  26.8 7.7 concatenate.199
  34.5 5.4 multiply_convert_fusion.3
  40.0 5.5 multiply_convert_fusion.2
  47.6 6.8 convolution_bitcast_fusion.1
  54.4 25.4 %fusion.177 = f32[1,6,35356]{2,0,1:T(1,128)S(1)} fusion(f32[9,6,35630]{2,0,1:T(8,128)} %convolution_bitcast_fusion.1), kind=kLoop, calls=%fused_computation.182 | loop fusion | flops 1909224 | bytes 8485440 | tf_op jit(solution)/shard_map/mul | solution.py:80
  86.2 224.3 %while.56 = (s32[]{:T(128)}, f32[1,256,128]{2,1,0:T(8,128)S(1)}, f32[1,256,128]{2,1,0:T(8,128)S(1)}, s32[]{:T(128)}) while((s32[]{:T(128)}, f32[1,256,128]{2,1,0:T(8,128)S(1)}, f32[1,256,128]{2,1,0:T(8,128)S(1)}, s32[]{:T(128)}) %tuple.294), condition=%wide.region_1.2_spmd, body=%wide.region_0.1_spmd.sunk | while | flops 524802 | bytes 941381 | solution.py:247
  152.5 3.9 collective-permute-done.2
  207.4 4.5 collective-permute-done.2
  263.5 4.3 collective-permute-done.2
  292.1 3.7 collective-permute-done.2
  321.4 4.2 collective-permute-done.23
  331.5 3.8 collective-permute-start.27
  335.3 4.6 collective-permute-done.26
  343.9 8.6 concatenate.210
  352.6 5.5 multiply_convert_fusion.1
  358.0 5.5 multiply_convert_fusion
  365.6 6.9 convolution_bitcast_fusion
  372.5 24.9 %fusion.176 = f32[1,6,35356]{2,0,1:T(1,128)S(1)} fusion(f32[9,6,35630]{2,0,1:T(8,128)} %convolution_bitcast_fusion), kind=kLoop, calls=%fused_computation.173 | loop fusion | flops 1909224 | bytes 8485440 | tf_op jit(solution)/shard_map/mul | solution.py:80
  406.5 228.1 %while.57 = (s32[]{:T(128)}, f32[1,256,128]{2,1,0:T(8,128)S(1)}, f32[1,256,128]{2,1,0:T(8,128)S(1)}, s32[]{:T(128)}) while((s32[]{:T(128)}, f32[1,256,128]{2,1,0:T(8,128)S(1)}, f32[1,256,128]{2,1,0:T(8,128)S(1)}, s32[]{:T(128)}) %tuple.297), condition=%wide.region_3.4_spmd, body=%wide.region_2.3_spmd.sunk | while | flops 524802 | bytes 941381 | solution.py:247
  414.0 3.8 collective-permute-start.7
  434.5 4.5 collective-permute-start.4
  447.5 3.9 collective-permute-done.6
  502.5 4.3 collective-permute-done.6
  568.7 4.0 collective-permute-start.7
  602.5 4.5 collective-permute-done.6
  645.0 4.3 collective-permute-done.31
  660.6 8.3 collective-permute-done.34
  670.0 228.1 %while.58 = (s32[]{:T(128)}, f32[1,256,128]{2,1,0:T(8,128)S(1)}, f32[1,256,128]{2,1,0:T(8,128)S(1)}, s32[]{:T(128)}, s32[]{:T(128)}) while((s32[]{:T(128)}, f32[1,256,128]{2,1,0:T(8,128)S(1)}, f32[1,256,128]{2,1,0:T(8,128)S(1)}, s32[]{:T(128)}, s32[]{:T(128)}) %tuple.300), condition=%wide.region_5.6_spmd.clone, body=%wide.region_4.5_spmd.clone.sunk | while | flops 557571 | bytes 1072471 | solution.py:258
  708.6 4.6 collective-permute-done.10
  899.3 3.9 scatter-add.34
  914.0 3.7 fusion.71
  917.7 5.0 pad_bitcast_fusion.9
  936.1 35.7 %stack.133 = bf16[9,6,35630]{2,0,1:T(8,128)(2,1)} concatenate(bf16[1,6,35630]{2,0,1:T(2,128)(2,1)S(1)} %copy.212, bf16[1,6,35630]{2,0,1:T(2,128)(2,1)} %copy.213, bf16[1,6,35630]{2,0,1:T(2,128)(2,1)} %copy.214, bf16[1,6,35630]{2,0,1:T(2,128)(2,1)} %copy.215, bf16[1,6,35630]{2,0,1:T(2,128)(2,1)} %copy.216, bf16[1,6,35630]{2,0,1:T(2,128)(2,1)} %copy.217, ...), dimensions={0} | concatenate | bytes 7696080 | tf_op jit(solution)/shard_map/stack | solution.py:118
  971.8 8.6 convert_reduce_fusion.1
  982.5 7.4 convert_reduce_fusion.3
  1022.9 4.5 fusion.107
  1045.7 5.9 collective-permute-done.43
  1051.8 212.0 %while.59 = (s32[]{:T(128)}, f32[1,256,128]{2,1,0:T(8,128)S(1)}, f32[1,256,128]{2,1,0:T(8,128)S(1)}, s32[]{:T(128)}, s32[]{:T(128)}) while((s32[]{:T(128)}, f32[1,256,128]{2,1,0:T(8,128)S(1)}, f32[1,256,128]{2,1,0:T(8,128)S(1)}, s32[]{:T(128)}, s32[]{:T(128)}) %tuple.303), condition=%wide.region_17.18_spmd.clone, body=%wide.region_16.17_spmd.clone.sunk | while | flops 557571 | bytes 1072471 | solution.py:258
  1060.5 4.0 collective-permute-done.14
  1265.0 4.0 scatter-add.41
  1278.5 4.4 fusion.125
  1294.9 36.9 %stack.143 = bf16[9,6,35630]{2,0,1:T(8,128)(2,1)} concatenate(bf16[1,6,35630]{2,0,1:T(2,128)(2,1)S(1)} %copy.222, bf16[1,6,35630]{2,0,1:T(2,128)(2,1)S(1)} %copy.223, bf16[1,6,35630]{2,0,1:T(2,128)(2,1)S(1)} %copy.224, bf16[1,6,35630]{2,0,1:T(2,128)(2,1)S(1)} %copy.225, bf16[1,6,35630]{2,0,1:T(2,128)(2,1)} %copy.226, bf16[1,6,35630]{2,0,1:T(2,128)(2,1)} %copy.227, ...), dimensions={0} | concatenate | bytes 7696080 | tf_op jit(solution)/shard_map/stack | solution.py:118
  1331.8 8.1 convert_reduce_fusion
  1339.9 9.2 convert_reduce_fusion.2
  1375.1 5.0 convolution_add_fusion.4
  1380.3 4.1 convolution_add_fusion.5
  1384.6 39.2 %all-reduce.105 = (f32[8832]{0:T(1024)S(1)}, f32[]{:T(128)}) all-reduce(f32[8832]{0:T(1024)S(1)} %concatenate.229, f32[]{:T(128)S(6)} %add.889), channel_id=1, replica_groups=mesh['ens'=2,'gx'=4,'gy'=4] {'ens','gx','gy'}, use_global_device_ids=true, to_apply=%region_30.31 | all-reduce | flops 8833 | bytes 70664 | tf_op jit(solution)/shard_map/psum | solution.py:355
  (1266 shorter events, 1086.3 us)
Async XLA Ops:
  9.0 11.3 collective-permute-start.18
  10.7 12.3 collective-permute-start.19
  132.6 7.2 collective-permute-start.2
  133.8 8.9 collective-permute-start.3
  148.6 7.7 collective-permute-start.2
  189.8 8.2 collective-permute-start.3
  203.6 8.4 collective-permute-start.2
  245.6 8.1 collective-permute-start.3
  259.6 8.2 collective-permute-start.2
  274.8 7.4 collective-permute-start.3
  288.2 7.6 collective-permute-start.2
  288.8 7.4 collective-permute-start.3
  331.4 8.5 collective-permute-start.26
  331.5 9.4 collective-permute-start.27
  414.0 7.3 collective-permute-start.7
  443.6 7.8 collective-permute-start.6
  483.9 7.2 collective-permute-start.7
  498.6 8.1 collective-permute-start.6
  499.7 7.3 collective-permute-start.7
  539.9 7.2 collective-permute-start.7
  553.5 7.5 collective-permute-start.6
  555.9 7.3 collective-permute-start.7
  568.1 7.6 collective-permute-start.6
  568.7 7.6 collective-permute-start.7
  581.2 7.9 collective-permute-start.6
  582.8 8.6 collective-permute-start.7
  598.6 8.3 collective-permute-start.6
  599.4 7.9 collective-permute-start.7
  657.3 11.6 collective-permute-start.34
  657.4 11.5 collective-permute-start.35
  676.8 7.2 collective-permute-start.10
  691.0 7.3 collective-permute-start.11
  704.3 8.9 collective-permute-start.10
  705.2 9.3 collective-permute-start.11
  721.3 7.2 collective-permute-start.10
  777.5 7.2 collective-permute-start.10
  791.9 7.2 collective-permute-start.10
  819.7 7.2 collective-permute-start.10
  833.8 7.2 collective-permute-start.10
  862.4 7.2 collective-permute-start.10
  875.9 7.2 collective-permute-start.10
  1005.9 14.2 collective-permute-start.36
  1006.9 14.0 collective-permute-start.37
  1022.3 7.5 collective-permute-start.38
  1040.6 11.0 collective-permute-start.43
  1056.6 7.9 collective-permute-start.14
  1440.3 11.3 collective-permute-start.44
  1445.3 10.0 collective-permute-start.45
  (339 other events, 2128.8 us)
where the time goes:
time: 1480 us; the launch traced here: 1470 us
  waiting for transfers between devices  542 us (37%)
  starting transfers between devices  435 us (29%)
  local copies, waits for them, and re-layouts  181 us (12%)
  matrix products  131 us (9%)
  other arithmetic  128 us (9%)
  blocking collectives  39.2 us (3%)
    ppermute x140, waiting for transfers between devices, with_halo(): before = lax.ppermute(last, axis, up)  364 us
    ppermute x140, starting transfers between devices, with_halo(): after = lax.ppermute(initial, axis, down)  262 us
    ppermute x140, waiting for transfers between devices, with_halo(): after = lax.ppermute(initial, axis, down)  168 us
    ppermute x140, starting transfers between devices, with_halo(): before = lax.ppermute(last, axis, up)  159 us
    another operation x22, local copies, waits for them, and re-layouts, network_backward(): spread_taps = jnp.stack(spread)  103 us
    mul x2, other arithmetic, network(): flat_coef = COEF_SCALE * summed  50.4 us
    dot_general x18, matrix products, network_backward(): jnp.einsum('hp,np->hn', window, grad_taps, preferred_element_type=jnp.flo...  47.5 us
    psum x1, blocking collectives, shards(): lax.psum((flat_grads, local_loss), ('ens', 'gx', 'gy'))  39.2 us
  transfers between devices with their start and end apart: 288, of which 279 were waited for; matrix products, arithmetic and copies ran while one was open for 2% of the time, Pallas kernels for 0%

commit v1 on v0

v1 whole, which is shorter than its diff:
```python
import functools

import jax
import jax.numpy as jnp
import numpy as np
from jax import lax
from jax.experimental import pallas as pl
from jax.experimental.pallas import tpu as pltpu
from jax.sharding import PartitionSpec as P

SWEEPS = 16
TIME_STEP = 0.2
VISCOSITY = 0.05
DRAG_RATE = 0.1
FORCE_WAVES = 4.0
COEF_SCALE = 0.1
EPSILON = 1e-06
OUTER_WEIGHT = -1.0 / 16.0
INNER_WEIGHT = 9.0 / 16.0
TWO_PI = 6.283185307179586

TOP = 40
LEFT = 64
CHUNK_ROWS = 16
LEAD = 384
BF16 = jnp.bfloat16
F32 = jnp.float32


def passed_along(block, axis, distance):
    size = lax.axis_size(axis)
    route = [(i, (i + distance) % size) for i in range(size)]
    return lax.ppermute(block, axis, route)


def exchange(own, rim):
    before = passed_along(own[:, -rim:], "gx", 1)
    after = passed_along(own[:, :rim], "gx", -1)
    tall = jnp.concatenate([before, own, after], axis=1)
    left = passed_along(jnp.swapaxes(tall[:, :, -rim:], 1, 2), "gy", 1)
    right = passed_along(jnp.swapaxes(tall[:, :, :rim], 1, 2), "gy", -1)
    wide = jnp.concatenate([jnp.swapaxes(left, 1, 2), tall, jnp.swapaxes(right, 1, 2)], axis=2)
    return jnp.pad(wide, ((0, 0), (TOP - rim, TOP - rim), (LEFT - rim, LEFT - rim)))


def total_over(value, axis):
    size = lax.axis_size(axis)
    if size <= 4:
        moved = [passed_along(value, axis, distance) for distance in range(1, size)]
        for other in moved:
            value = value + other
        return value
    return lax.psum(value, axis)


def at(field, rows, cols):
    if rows:
        field = pltpu.roll(field, (-rows) % field.shape[0], 0)
    if cols:
        field = pltpu.roll(field, (-cols) % field.shape[1], 1)
    return field


def project(first, second, work_ref, rhs_ref):
    quarter = -0.125 * (at(first, 1, 0) - at(first, -1, 0) + at(second, 0, 1) - at(second, 0, -1))
    rhs_ref[...] = quarter
    work_ref[...] = quarter

    def sweep(index, carried):
        p = work_ref[...]
        near = at(p, 1, 0) + at(p, -1, 0) + at(p, 0, 1) + at(p, 0, -1)
        work_ref[...] = 0.25 * near + rhs_ref[...]
        return carried

    lax.fori_loop(0, SWEEPS, sweep, 0)
    p = work_ref[...]
    return (
        first - 0.5 * (at(p, 1, 0) - at(p, -1, 0)),
        second - 0.5 * (at(p, 0, 1) - at(p, 0, -1)),
    )


def project_kernel(in_ref, out_ref, work_ref, rhs_ref):
    first, second = project(in_ref[0], in_ref[1], work_ref, rhs_ref)
    out_ref[0] = first
    out_ref[1] = second


def last_kernel(rows, cols, in_ref, goal_ref, out_ref, loss_ref, work_ref, rhs_ref):
    first, second = project(in_ref[0], in_ref[1], work_ref, rhs_ref)
    first = first - goal_ref[0]
    second = second - goal_ref[1]
    row = lax.broadcasted_iota(jnp.int32, first.shape, 0)
    col = lax.broadcasted_iota(jnp.int32, first.shape, 1)
    own = (row >= TOP) & (row < TOP + rows) & (col >= LEFT) & (col < LEFT + cols)
    square = jnp.where(own, first * first + second * second, 0.0)
    loss_ref[...] = jnp.sum(square, axis=0, keepdims=True)
    out_ref[0] = first
    out_ref[1] = second
    first, second = project(out_ref[0], out_ref[1], work_ref, rhs_ref)
    out_ref[0] = first
    out_ref[1] = second


def faces(field, c0, c1, c2, move):
    return (
        (OUTER_WEIGHT + c0) * move(field, -1)
        + (INNER_WEIGHT + c1) * field
        + (INNER_WEIGHT + c2) * move(field, 1)
        + (OUTER_WEIGHT - c0 - c1 - c2) * move(field, 2)
    )


def by_row(field, distance):
    return at(field, distance, 0)


def by_col(field, distance):
    return at(field, 0, distance)


def advect_kernel(v_ref, c_ref, force_ref, out_ref):
    speed_rows = 0.5 * (v_ref[0] + by_row(v_ref[0], 1))
    speed_cols = 0.5 * (v_ref[1] + by_col(v_ref[1], 1))
    for comp in range(2):
        q = v_ref[comp]
        flux = speed_rows * faces(q, c_ref[0], c_ref[1], c_ref[2], by_row)
        change = flux - by_row(flux, -1)
        flux = speed_cols * faces(q, c_ref[3], c_ref[4], c_ref[5], by_col)
        change = change + (flux - by_col(flux, -1))
        laplace = by_row(q, 1) + by_row(q, -1) + by_col(q, 1) + by_col(q, -1) - 4.0 * q
        drive = VISCOSITY * laplace - DRAG_RATE * q
        if comp == 0:
            drive = drive + force_ref[...]
        out_ref[comp] = q - TIME_STEP * change + TIME_STEP * drive


def advect_back_kernel(v_ref, c_ref, g_ref, taps_ref, out_ref):
    for axis in range(2):
        move = by_row if axis == 0 else by_col
        speed = 0.5 * (v_ref[axis] + move(v_ref[axis], 1))
        c0 = c_ref[3 * axis]
        c1 = c_ref[3 * axis + 1]
        c2 = c_ref[3 * axis + 2]
        grads = []
        grad_speed = None
        taps = None
        for comp in range(2):
            q = v_ref[comp]
            g = g_ref[comp]
            grad_flux = TIME_STEP * (move(g, 1) - g)
            term = grad_flux * faces(q, c0, c1, c2, move)
            grad_speed = term if grad_speed is None else grad_speed + term
            grad_face = grad_flux * speed
            behind = move(q, -1)
            ahead = move(q, 1)
            far = move(q, 2)
            new = (grad_face * (behind - far), grad_face * (q - far), grad_face * (ahead - far))
            taps = new if taps is None else tuple(a + b for a, b in zip(taps, new))
            grads.append(
                move(grad_face * (OUTER_WEIGHT + c0), 1)
                + grad_face * (INNER_WEIGHT + c1)
                + move(grad_face * (INNER_WEIGHT + c2), -1)
                + move(grad_face * (OUTER_WEIGHT - c0 - c1 - c2), -2)
            )
        grads[axis] = grads[axis] + 0.5 * (grad_speed + move(grad_speed, -1))
        for number in range(3):
            taps_ref[3 * axis + number] = COEF_SCALE * taps[number]
        for comp in range(2):
            if axis == 0:
                out_ref[comp] = grads[comp]
            else:
                g = g_ref[comp]
                near = by_row(g, 1) + by_row(g, -1) + by_col(g, 1) + by_col(g, -1) - 4.0 * g
                out_ref[comp] = (
                    out_ref[comp]
                    + grads[comp]
                    + g
                    + TIME_STEP * (VISCOSITY * near - DRAG_RATE * g)
                )


def tap_offsets(wide):
    return [row * wide + col for row in range(3) for col in range(3)]


def shifted(block, offset, length):
    if offset:
        block = pltpu.roll(block, block.shape[1] - offset, 1)
    return block[:, :length]


def gather_columns(x_ref, cols_ref, start, chunk, offsets):
    window = x_ref[:, pl.ds(start, chunk + LEAD)]
    for tap, offset in enumerate(offsets):
        cols_ref[2 * tap : 2 * tap + 2, :] = shifted(window, offset, chunk)[:2]


def product(left, right):
    return lax.dot_general(left, right, (((1,), (0,)), ((), ())), preferred_element_type=F32)


def product_over_cells(left, right):
    return lax.dot_general(left, right, (((1,), (1,)), ((), ())), preferred_element_type=F32)


def network_kernel(chunk, offsets, x_ref, w1_ref, b1_ref, w2_ref, b2_ref, w3_ref, out_ref, cols_ref, terms_ref):
    step = pl.program_id(0)
    start = pl.multiple_of(step * chunk, 128)

    @pl.when(step == 0)
    def _():
        cols_ref[...] = jnp.zeros_like(cols_ref)
        terms_ref[...] = jnp.zeros_like(terms_ref)

    gather_columns(x_ref, cols_ref, start, chunk, offsets)
    half = product(w1_ref[...], cols_ref[...].astype(BF16)) + b1_ref[...]
    hidden = (half * jnp.tanh(half) + half).astype(BF16)
    half = product(w2_ref[...], hidden) + b2_ref[...]
    hidden = (half * jnp.tanh(half) + half).astype(BF16)
    terms_ref[:, :LEAD] = terms_ref[:, chunk:]
    terms_ref[:, LEAD:] = product(w3_ref[...], hidden)
    total = None
    for tap, offset in enumerate(offsets):
        term = shifted(terms_ref[8 * tap : 8 * tap + 8, :], offset, chunk)
        total = term if total is None else total + term
    out_ref[...] = COEF_SCALE * total


def network_back_kernel(
    chunk, offsets, x_ref, taps_ref, own_ref, w1_ref, b1_ref, w2_ref, b2_ref, w1b_ref, w2b_ref, w3b_ref,
    out_ref, d1_ref, d2_ref, d3_ref, cols_ref, spread_ref, terms_ref,
):
    step = pl.program_id(0)
    start = pl.multiple_of(step * chunk, 128)

    @pl.when(step == 0)
    def _():
        cols_ref[...] = jnp.zeros_like(cols_ref)
        spread_ref[...] = jnp.zeros_like(spread_ref)
        terms_ref[...] = jnp.zeros_like(terms_ref)
        d1_ref[...] = jnp.zeros_like(d1_ref)
        d2_ref[...] = jnp.zeros_like(d2_ref)
        d3_ref[...] = jnp.zeros_like(d3_ref)

    own = own_ref[:, pl.ds(start, chunk)]
    gather_columns(x_ref, cols_ref, start, chunk, offsets)
    cols_ref[18:19, :] = jnp.ones((1, chunk), F32)
    window = taps_ref[:, pl.ds(start, chunk + LEAD)]
    for tap, offset in enumerate(offsets):
        spread_ref[8 * tap : 8 * tap + 8, :] = shifted(window, LEAD - offset, chunk)
    cols = cols_ref[...]
    half = product(w1_ref[...], cols.astype(BF16)) + b1_ref[...]
    bend = jnp.tanh(half)
    hidden_one = (half * bend + half).astype(BF16)
    slope_one = (0.5 + 0.5 * bend) * (1.0 + half * (1.0 - bend))
    half = product(w2_ref[...], hidden_one) + b2_ref[...]
    bend = jnp.tanh(half)
    hidden_two = (half * bend + half).astype(BF16)
    slope_two = (0.5 + 0.5 * bend) * (1.0 + half * (1.0 - bend))
    spread = spread_ref[...].astype(BF16)
    grad_two = (product(w3b_ref[...], spread) * slope_two).astype(BF16)
    grad_one = (product(w2b_ref[...], grad_two) * slope_one).astype(BF16)
    mask = own.astype(BF16)
    d3_ref[...] += product_over_cells(spread, hidden_two * mask)
    d2_ref[...] += product_over_cells(hidden_one, grad_two * mask)
    d1_ref[...] += product_over_cells((cols * own).astype(BF16), jnp.concatenate([grad_one, grad_two], axis=0))
    terms_ref[:, :LEAD] = terms_ref[:, chunk:]
    terms_ref[:, LEAD:] = product(w1b_ref[...], grad_one)
    total = None
    for tap, offset in enumerate(offsets):
        term = shifted(terms_ref[8 * tap : 8 * tap + 8, :], LEAD - offset, chunk)
        total = term if total is None else total + term
    out_ref[...] = total


def whole(shape):
    return pl.BlockSpec(shape, lambda *step: (0,) * len(shape))


def shards(velocity, targets, weight_one, bias_one, weight_two, bias_two, weight_three):
    rows, cols = velocity.shape[2], velocity.shape[3]
    step_count = targets.shape[1]
    frame = (rows + 2 * TOP, cols + 2 * LEFT)
    wide = cols + 8
    chunk = CHUNK_ROWS * wide
    chunks = -(-(rows + 8) // CHUNK_ROWS)
    length = chunks * chunk
    offsets = tap_offsets(wide)
    hid = weight_two.shape[0]
    nout = weight_three.shape[3]
    params = pltpu.CompilerParams(vmem_limit_bytes=56 << 20)

    def grid_call(kernel, outs, *args, scratch=()):
        return pl.pallas_call(
            kernel,
            out_shape=[jax.ShapeDtypeStruct(shape, F32) for shape in outs],
            scratch_shapes=[pltpu.VMEM(shape, F32) for shape in scratch],
            compiler_params=params,
        )(*args)

    w1 = weight_one.reshape(18, hid)
    w1_half = jnp.pad((0.5 * w1.astype(F32)).astype(BF16).T, ((0, 0), (0, 14)))
    w2_half = (0.5 * weight_two.astype(F32)).astype(BF16).T
    b1_half = 0.5 * bias_one[:, None]
    b2_half = 0.5 * bias_two[:, None]
    w3 = jnp.pad(weight_three.reshape(9, hid, nout), ((0, 0), (0, 0), (0, 8 - nout)))
    w3_out = jnp.transpose(w3, (0, 2, 1)).reshape(72, hid)
    w3_back = jnp.pad(jnp.transpose(w3, (1, 0, 2)).reshape(hid, 72), ((0, 0), (0, 8)))
    w1_back = jnp.pad(weight_one.reshape(9, 2, hid), ((0, 0), (0, 6), (0, 0))).reshape(72, hid)

    place = np.arange(length)
    place_row, place_col = place // wide, place % wide
    own_cells = (place_row >= 3) & (place_row < 3 + rows) & (place_col >= 3) & (place_col < 3 + cols)
    own_row = jnp.asarray(own_cells[None, :], F32)

    total_cols = cols * lax.axis_size("gy")
    col_ids = lax.axis_index("gy") * cols + jnp.arange(frame[1], dtype=jnp.int32) - LEFT
    forcing = jnp.sin(col_ids.astype(F32) * (TWO_PI * FORCE_WAVES / total_cols))[None, :]

    def flat_velocity(v):
        cells = v[:, TOP - 4 : TOP + rows + 4, LEFT - 4 : LEFT + cols + 4]
        cells = cells.astype(BF16).astype(F32).reshape(2, (rows + 8) * wide)
        return jnp.pad(cells, ((0, 0), (0, length + LEAD - (rows + 8) * wide)))

    def network(x):
        flat = pl.pallas_call(
            functools.partial(network_kernel, chunk, offsets),
            grid=(chunks,),
            in_specs=[
                whole((2, length + LEAD)),
                whole((hid, 32)),
                whole((hid, 1)),
                whole((hid, hid)),
                whole((hid, 1)),
                whole((72, hid)),
            ],
            out_specs=pl.BlockSpec((8, chunk), lambda step: (0, step)),
            out_shape=jax.ShapeDtypeStruct((8, length), F32),
            scratch_shapes=[pltpu.VMEM((32, chunk), F32), pltpu.VMEM((72, chunk + LEAD), F32)],
            compiler_params=params,
        )(x, w1_half, b1_half, w2_half, b2_half, w3_out)
        used = rows + 4
        cells = flat[:nout, LEAD : LEAD + used * wide].reshape(nout, used, wide)
        return jnp.pad(cells, ((0, 0), (TOP - 2, frame[0] - (TOP - 2) - used), (LEFT - 2, frame[1] - (LEFT - 2) - wide)))

    def network_back(x, taps):
        used = rows + 4
        cells = taps[:, TOP - 2 : TOP - 2 + used, LEFT - 2 : LEFT - 2 + wide].astype(BF16).astype(F32)
        cells = cells.reshape(nout, used * wide)
        cells = jnp.pad(cells, ((0, 8 - nout), (LEAD, length - used * wide)))
        flat, d1, d2, d3 = pl.pallas_call(
            functools.partial(network_back_kernel, chunk, offsets),
            grid=(chunks,),
            in_specs=[
                whole((2, length + LEAD)),
                whole((8, length + LEAD)),
                whole((1, length)),
                whole((hid, 32)),
                whole((hid, 1)),
                whole((hid, hid)),
                whole((hid, 1)),
                whole((72, hid)),
                whole((hid, hid)),
                whole((hid, 80)),
            ],
            out_specs=[
                pl.BlockSpec((8, chunk), lambda step: (0, step)),
                whole((32, 2 * hid)),
                whole((hid, hid)),
                whole((80, hid)),
            ],
            out_shape=[
                jax.ShapeDtypeStruct((8, length), F32),
                jax.ShapeDtypeStruct((32, 2 * hid), F32),
                jax.ShapeDtypeStruct((hid, hid), F32),
                jax.ShapeDtypeStruct((80, hid), F32),
            ],
            scratch_shapes=[
                pltpu.VMEM((32, chunk), F32),
                pltpu.VMEM((80, chunk), F32),
                pltpu.VMEM((72, chunk + LEAD), F32),
            ],
            compiler_params=params,
        )(x, cells, own_row, w1_half, b1_half, w2_half, b2_half, w1_back, weight_two, w3_back)
        grad_in = flat[:2, : (rows + 8) * wide].reshape(2, rows + 8, wide)[:, 4 : 4 + rows, 4 : 4 + cols]
        grad_three = d3[:72].reshape(9, 8, hid)[:, :nout].transpose(0, 2, 1)
        pieces = [d1[:18, :hid], d1[18, :hid], d2, d1[18, hid:], grad_three]
        return grad_in, jnp.concatenate([piece.reshape(-1) for piece in pieces])

    def own(framed):
        return framed[:, TOP : TOP + rows, LEFT : LEFT + cols]

    pair = (2,) + frame
    first = exchange(jnp.concatenate([velocity[0], targets[0, step_count - 1]], axis=0), 24)
    current = first[:2]
    last_goal = first[2:]
    loss = jnp.zeros((), F32)
    kept = []
    errors = []
    for step_index in range(step_count):
        x = flat_velocity(current)
        coefs = network(x)
        (provisional,) = grid_call(advect_kernel, [pair], current, coefs, forcing)
        kept.append((current, x, coefs))
        if step_index < step_count - 1:
            framed = exchange(own(provisional), 24)
            (current,) = grid_call(project_kernel, [pair], framed, scratch=[frame, frame])
            error = own(current) - targets[0, step_index]
            errors.append(error)
            loss = loss + jnp.sum(jnp.square(error))
        else:
            framed = exchange(own(provisional), 40)
            grad, squares = grid_call(
                functools.partial(last_kernel, rows, cols), [pair, (1, frame[1])], framed, last_goal,
                scratch=[frame, frame],
            )
            loss = loss + jnp.sum(squares)
    sums = None
    for step_index in range(step_count - 1, -1, -1):
        if step_index < step_count - 1:
            framed = exchange(grad_own + errors[step_index], 24)
            (grad,) = grid_call(project_kernel, [pair], framed, scratch=[frame, frame])
        current, x, coefs = kept[step_index]
        taps, moved = grid_call(advect_back_kernel, [(nout,) + frame, pair], current, coefs, grad)
        grad_in, step_sums = network_back(x, taps)
        grad_own = own(moved) + grad_in
        sums = step_sums if sums is None else sums + step_sums

    flat_sums = jnp.concatenate([sums, 0.5 * loss[None]])
    count = flat_sums.shape[0]
    tall = -(-count // 1024) * 8
    flat_sums = jnp.pad(flat_sums, (0, tall * 128 - count)).reshape(tall, 128)
    for axis in ("ens", "gx", "gy"):
        flat_sums = total_over(flat_sums, axis)
    flat_sums = flat_sums.reshape(-1)
    outputs = []
    offset = 0
    for shape in (weight_one.shape, bias_one.shape, weight_two.shape, bias_two.shape, weight_three.shape):
        size = int(np.prod(shape))
        segment = flat_sums[offset : offset + size]
        scaled = segment * (1.0 / jnp.sqrt(jnp.mean(jnp.square(segment)) + EPSILON))
        outputs.append(scaled.reshape(shape))
        offset += size
    device_count = lax.axis_size(("ens", "gx", "gy"))
    mean_loss = flat_sums[offset] * (1.0 / float(step_count * 2 * rows * cols * device_count))
    return (*outputs, mean_loss, grad_own[None])


def solution(mesh):
    return jax.shard_map(
        shards,
        mesh=mesh,
        in_specs=(P("ens", None, "gx", "gy"), P("ens", None, None, "gx", "gy"), P(), P(), P(), P(), P()),
        out_specs=(P(), P(), P(), P(), P(), P(), P("ens", None, "gx", "gy")),
        check_vma=False,
    )
```

time: 1480 us -> 278 us (0.19)
  waiting for transfers between devices: 542 us -> 37.9 us
  starting transfers between devices: 435 us -> 37.4 us
  local copies, waits for them, and re-layouts: 181 us -> 40.1 us
  Pallas kernels: 0 us -> 132 us
  matrix products: 131 us -> 0 us
  other arithmetic: 128 us -> 21.1 us
  blocking collectives: 39.2 us -> 0 us
    ppermute x280 -> x0, waiting for transfers between devices: 532 us -> none  [the longest x140 364 us: with_halo(): before = lax.ppermute(last, axis, up)]
    ppermute x280 -> x0, starting transfers between devices: 421 us -> none  [the longest x140 262 us: with_halo(): after = lax.ppermute(initial, axis, down)]
    pallas_call x0 -> x11, Pallas kernels: none -> 132 us  [the longest x2 53 us: network_back(): pl.pallas_call(functools.partial(network_back_kernel, chunk, offsets), gr...]
    dot_general x34 -> x0, matrix products: 131 us -> none  [the longest x18 47.5 us: network_backward(): jnp.einsum('hp,np->hn', window, grad_taps, preferred_element_type=jnp.flo...]
    another operation x23 -> x0, local copies, waits for them, and re-layouts: 103 us -> none  [the longest x22 103 us: network_backward(): spread_taps = jnp.stack(spread)]
    mul x34 -> x6, other arithmetic: 72.8 us -> 2.53 us  [the longest x4 1.21 us: shards(): scaled = segment * (1.0 / jnp.sqrt(jnp.mean(jnp.square(segment)) + EPSILON))]
    psum x1 -> x0, blocking collectives: 39.2 us -> none  [shards(): lax.psum((flat_grads, local_loss), ('ens', 'gx', 'gy'))]
    ppermute x8 -> x23, waiting for transfers between devices: 10.3 us -> 37.9 us  [passed_along(): return lax.ppermute(block, axis, route)]
  transfers between devices with their start and end apart: 288 -> 23, of which waited for: 279 -> 17; matrix products, arithmetic and copies ran while one was open for 2% -> 6% of each run, Pallas kernels for 0% -> 0%
where the time goes in v1:
time: 278 us; the launch traced here: 276 us
  Pallas kernels  132 us (47%)
  local copies, waits for them, and re-layouts  40.1 us (14%)
  waiting for transfers between devices  37.9 us (14%)
  starting transfers between devices  37.4 us (13%)
  other arithmetic  21.1 us (8%)
  between operations  7.46 us (3%)
    pallas_call x2, Pallas kernels, network_back(): pl.pallas_call(functools.partial(network_back_kernel, chunk, offsets), gr...  53 us
    pallas_call x7, Pallas kernels, grid_call(): pl.pallas_call(kernel, out_shape=[jax.ShapeDtypeStruct(shape, F32) for sh...  46.4 us
    ppermute x23, waiting for transfers between devices, passed_along(): return lax.ppermute(block, axis, route)  37.9 us
    ppermute x23, starting transfers between devices, passed_along(): return lax.ppermute(block, axis, route)  37.4 us
    pallas_call x2, Pallas kernels, network(): pl.pallas_call(functools.partial(network_kernel, chunk, offsets), grid=(c...  33 us
  transfers between devices with their start and end apart: 23, of which 17 were waited for; matrix products, arithmetic and copies ran while one was open for 6% of the time, Pallas kernels for 0%

profile of v1, /device:TPU:0, one launch (start us, length us, event | category | flops | bytes accessed | tf_op | source)
XLA Modules:
  0.0 276.3 jit_solution(18014381828476353537)
XLA Ops:
  2.4 3.0 %collective-permute-start = (f32[4,24,128]{2,1,0:T(8,128)S(1)}, f32[4,24,128]{2,1,0:T(8,128)S(1)}, u32[]{:S(2)}, u32[]{:S(2)}) collective-permute-start(f32[4,24,128]{2,1,0:T(8,128)S(1)} %get-tuple-element.61), channel_id=1, source_target_pairs={{0,4},{4,8},{8,12},{12,0},{1,5},{5,9},{9,13},{13,1},{2,6},{6,10},{... | collective-permute-start | bytes 147464 | tf_op jit(solution)/shard_map/ppermute | solution.py:33
  10.4 2.0 collective-permute-start.2
  12.6 2.1 collective-permute-start.3
  21.5 1.5 pad_slice_fusion
  24.4 16.5 %shard_map.135 = f32[8,36992]{1,0:T(8,128)} custom-call(f32[2,37376]{1,0:T(2,128)} %pad_convert_fusion.3.x_ref, bf16[64,32]{1,0:T(8,128)(2,1)} %pad.67.w1_ref, f32[64,1]{1,0:T(8,128)} %copy.47.b1_ref, bf16[64,64]{1,0:T(8,128)(2,1)} %fusion.7.w2_ref, f32[64,1]{1,0:T(8,128)} %copy.48.b2_ref, bf16[72,64]{1,0:T(8,128)(2,1)} %get-tuple-element.74.w3_ref), custom_call_target="tpu_custom_call" | custom-call | tf_op jit(solution)/shard_map/pallas_call | solution.py:327
  40.9 1.3 slice.226
  43.3 1.9 pad.69.c_ref
  45.1 4.3 %shard_map.136 = f32[2,336,256]{2,1,0:T(8,128)} custom-call(f32[2,336,256]{2,1,0:T(8,128)} %get-tuple-element.52.v_ref, f32[6,336,256]{2,1,0:T(8,128)} %pad.69.c_ref, f32[1,256]{1,0:T(1,128)} %multiply_sine_fusion.force_ref), custom_call_target="tpu_custom_call" | custom-call | tf_op jit(solution)/shard_map/pallas_call | solution.py:295
  50.3 1.3 collective-permute-start.4
  51.6 1.7 collective-permute-start.5
  56.5 3.0 %collective-permute-start.7 = (f32[2,24,304]{1,2,0:T(8,128)S(1)}, f32[2,24,304]{1,2,0:T(8,128)S(1)}, u32[]{:S(2)}, u32[]{:S(2)}) collective-permute-start(f32[2,24,304]{1,2,0:T(8,128)S(1)} %get-tuple-element.68), channel_id=1, source_target_pairs={{0,3},{1,0},{2,1},{3,2},{4,7},{5,4},{6,5},{7,6},{8,11},{9,8},{10,9... | collective-permute-start | bytes 175112 | tf_op jit(solution)/shard_map/ppermute | solution.py:33
  59.4 8.3 %collective-permute-done.6 = f32[2,24,304]{1,2,0:T(8,128)S(1)} collective-permute-done((f32[2,24,304]{1,2,0:T(8,128)S(1)}, f32[2,24,304]{1,2,0:T(8,128)S(1)}, u32[]{:S(2)}, u32[]{:S(2)}) %collective-permute-start.6) | collective-permute-done | bytes 58400 | tf_op jit(solution)/shard_map/ppermute | solution.py:33
  67.7 2.8 collective-permute-done.7
  70.5 1.4 select_maximum_fusion.8.in_ref
  71.8 6.6 %shard_map.137.v_ref = f32[2,336,256]{2,1,0:T(8,128)} custom-call(f32[2,336,256]{2,1,0:T(8,128)} %select_maximum_fusion.8.in_ref), custom_call_target="tpu_custom_call" | custom-call | tf_op jit(solution)/shard_map/pallas_call | solution.py:295
  78.5 1.2 slice.310
  81.1 16.5 %shard_map.138 = f32[8,36992]{1,0:T(8,128)} custom-call(f32[2,37376]{1,0:T(2,128)} %pad_convert_fusion.2.x_ref, bf16[64,32]{1,0:T(8,128)(2,1)} %pad.67.w1_ref, f32[64,1]{1,0:T(8,128)} %copy.47.b1_ref, bf16[64,64]{1,0:T(8,128)(2,1)} %fusion.7.w2_ref, f32[64,1]{1,0:T(8,128)} %copy.48.b2_ref, bf16[72,64]{1,0:T(8,128)(2,1)} %get-tuple-element.74.w3_ref), custom_call_target="tpu_custom_call" | custom-call | tf_op jit(solution)/shard_map/pallas_call | solution.py:327
  97.5 1.3 slice.233
  99.9 1.8 pad.73.c_ref
  101.7 4.3 %shard_map.139 = f32[2,336,256]{2,1,0:T(8,128)} custom-call(f32[2,336,256]{2,1,0:T(8,128)} %shard_map.137.v_ref, f32[6,336,256]{2,1,0:T(8,128)} %pad.73.c_ref, f32[1,256]{1,0:T(1,128)} %multiply_sine_fusion.force_ref), custom_call_target="tpu_custom_call" | custom-call | tf_op jit(solution)/shard_map/pallas_call | solution.py:295
  107.0 2.4 collective-permute-start.8
  112.0 1.5 collective-permute-done.9
  114.2 3.3 %collective-permute-start.11 = (f32[2,40,336]{1,2,0:T(8,128)S(1)}, f32[2,40,336]{1,2,0:T(8,128)S(1)}, u32[]{:S(2)}, u32[]{:S(2)}) collective-permute-start(f32[2,40,336]{1,2,0:T(8,128)S(1)} %get-tuple-element.64), channel_id=1, source_target_pairs={{0,3},{1,0},{2,1},{3,2},{4,7},{5,4},{6,5},{7,6},{8,11},{9,8},{10,9... | collective-permute-start | bytes 322568 | tf_op jit(solution)/shard_map/ppermute | solution.py:33
  118.1 8.2 %collective-permute-done.10 = f32[2,40,336]{1,2,0:T(8,128)S(1)} collective-permute-done((f32[2,40,336]{1,2,0:T(8,128)S(1)}, f32[2,40,336]{1,2,0:T(8,128)S(1)}, u32[]{:S(2)}, u32[]{:S(2)}) %collective-permute-start.10) | collective-permute-done | bytes 107552 | tf_op jit(solution)/shard_map/ppermute | solution.py:33
  126.4 2.1 collective-permute-done.11
  128.5 1.4 select_maximum_fusion.4.in_ref
  129.9 11.7 %shard_map.140 = (f32[2,336,256]{2,1,0:T(8,128)}, f32[1,256]{1,0:T(1,128)}) custom-call(f32[2,336,256]{2,1,0:T(8,128)} %select_maximum_fusion.4.in_ref, f32[2,336,256]{2,1,0:T(8,128)} %get-tuple-element.51.goal_ref), custom_call_target="tpu_custom_call" | custom-call | tf_op jit(solution)/shard_map/pallas_call | solution.py:295
  141.6 6.4 %shard_map.141 = (f32[6,336,256]{2,1,0:T(8,128)}, f32[2,336,256]{2,1,0:T(8,128)}) custom-call(f32[2,336,256]{2,1,0:T(8,128)} %shard_map.137.v_ref, f32[6,336,256]{2,1,0:T(8,128)} %pad.73.c_ref, f32[2,336,256]{2,1,0:T(8,128)} %get-tuple-element.21.g_ref), custom_call_target="tpu_custom_call" | custom-call | tf_op jit(solution)/shard_map/pallas_call | solution.py:295
  148.0 1.8 slice.309
  152.0 26.5 %shard_map.142 = (f32[8,36992]{1,0:T(8,128)}, f32[32,128]{1,0:T(8,128)}, f32[64,64]{1,0:T(8,128)}, f32[80,64]{1,0:T(8,128)}) custom-call(f32[2,37376]{1,0:T(2,128)} %pad_convert_fusion.2.x_ref, f32[8,37376]{1,0:T(8,128)} %pad_convert_fusion.1.taps_ref, f32[1,36992]{1,0:T(1,128)} %constant.45.clone.own_ref, bf16[64,32]{1,0:T(8,128)(2,1)} %pad.67.w1_ref, ...), custom_call_target="tpu_custom_call" | custom-call | tf_op jit(solution)/shard_map/pallas_call | solution.py:352
  178.5 1.3 slice.198
  180.4 2.1 fusion.5
  182.5 1.2 collective-permute-start.12
  183.7 1.7 collective-permute-start.13
  185.4 1.8 collective-permute-done.12
  188.6 3.0 %collective-permute-start.15 = (f32[2,24,304]{1,2,0:T(8,128)S(1)}, f32[2,24,304]{1,2,0:T(8,128)S(1)}, u32[]{:S(2)}, u32[]{:S(2)}) collective-permute-start(f32[2,24,304]{1,2,0:T(8,128)S(1)} %get-tuple-element.66), channel_id=1, source_target_pairs={{0,3},{1,0},{2,1},{3,2},{4,7},{5,4},{6,5},{7,6},{8,11},{9,8},{10,9... | collective-permute-start | bytes 175112 | tf_op jit(solution)/shard_map/ppermute | solution.py:33
  194.2 5.1 %collective-permute-done.14 = f32[2,24,304]{1,2,0:T(8,128)S(1)} collective-permute-done((f32[2,24,304]{1,2,0:T(8,128)S(1)}, f32[2,24,304]{1,2,0:T(8,128)S(1)}, u32[]{:S(2)}, u32[]{:S(2)}) %collective-permute-start.14) | collective-permute-done | bytes 58400 | tf_op jit(solution)/shard_map/ppermute | solution.py:33
  199.3 2.2 collective-permute-done.15
  201.5 1.3 select_maximum_fusion.in_ref
  202.8 6.7 %shard_map.143.g_ref = f32[2,336,256]{2,1,0:T(8,128)} custom-call(f32[2,336,256]{2,1,0:T(8,128)} %select_maximum_fusion.in_ref), custom_call_target="tpu_custom_call" | custom-call | tf_op jit(solution)/shard_map/pallas_call | solution.py:295
  209.5 6.4 %shard_map.144 = (f32[6,336,256]{2,1,0:T(8,128)}, f32[2,336,256]{2,1,0:T(8,128)}) custom-call(f32[2,336,256]{2,1,0:T(8,128)} %get-tuple-element.52.v_ref, f32[6,336,256]{2,1,0:T(8,128)} %pad.69.c_ref, f32[2,336,256]{2,1,0:T(8,128)} %shard_map.143.g_ref), custom_call_target="tpu_custom_call" | custom-call | tf_op jit(solution)/shard_map/pallas_call | solution.py:295
  215.9 1.8 slice.308
  219.8 26.5 %shard_map.145 = (f32[8,36992]{1,0:T(8,128)}, f32[32,128]{1,0:T(8,128)}, f32[64,64]{1,0:T(8,128)}, f32[80,64]{1,0:T(8,128)}) custom-call(f32[2,37376]{1,0:T(2,128)} %pad_convert_fusion.3.x_ref, f32[8,37376]{1,0:T(8,128)} %pad_convert_fusion.taps_ref, f32[1,36992]{1,0:T(1,128)} %constant.45.clone.own_ref, bf16[64,32]{1,0:T(8,128)(2,1)} %pad.67.w1_ref, ...), custom_call_target="tpu_custom_call" | custom-call | tf_op jit(solution)/shard_map/pallas_call | solution.py:352
  251.3 1.8 collective-permute-start.17
  255.0 1.3 slice.221
  258.6 2.1 collective-permute-start.21
  260.8 2.3 collective-permute-start.22
  263.0 1.9 fusion.4
  (123 shorter events, 50.3 us)
Async XLA Ops:
  0.6 9.2 %copy-start = (f32[1,2,256,128]{3,2,1,0:T(8,128)S(1)}, f32[1,2,256,128]{3,2,1,0:T(8,128)}, u32[]{:S(2)}) copy-start(f32[1,2,256,128]{3,2,1,0:T(8,128)} %param.8) | copy-start | bytes 786436
  2.4 7.4 %collective-permute-start = (f32[4,24,128]{2,1,0:T(8,128)S(1)}, f32[4,24,128]{2,1,0:T(8,128)S(1)}, u32[]{:S(2)}, u32[]{:S(2)}) collective-permute-start(f32[4,24,128]{2,1,0:T(8,128)S(1)} %get-tuple-element.61), channel_id=1, source_target_pairs={{0,4},{4,8},{8,12},{12,0},{1,5},{5,9},{9,13},{13,1},{2,6},{6,10},{... | collective-permute-start | bytes 147464 | tf_op jit(solution)/shard_map/ppermute | solution.py:33
  5.4 4.5 %collective-permute-start.1 = (f32[4,24,128]{2,1,0:T(8,128)S(1)}, f32[4,24,128]{2,1,0:T(8,128)S(1)}, u32[]{:S(2)}, u32[]{:S(2)}) collective-permute-start(f32[4,24,128]{2,1,0:T(8,128)S(1)} %get-tuple-element.62), channel_id=1, source_target_pairs={{0,12},{4,0},{8,4},{12,8},{1,13},{5,1},{9,5},{13,9},{2,14},{6,2},{... | collective-permute-start | bytes 147464 | tf_op jit(solution)/shard_map/ppermute | solution.py:33
  10.1 7.4 %copy-start.4 = (bf16[3,3,64,6]{2,3,1,0:T(8,128)(2,1)S(1)}, bf16[3,3,64,6]{2,3,1,0:T(8,128)(2,1)}, u32[]{:S(2)}) copy-start(bf16[3,3,64,6]{2,3,1,0:T(8,128)(2,1)} %param.14) | copy-start | bytes 20740
  10.4 8.8 %collective-permute-start.2 = (f32[4,24,304]{2,1,0:T(8,128)S(1)}, f32[4,24,304]{2,1,0:T(8,128)S(1)}, u32[]{:S(2)}, u32[]{:S(2)}) collective-permute-start(f32[4,24,304]{2,1,0:T(8,128)S(1)} %copy.41), channel_id=1, source_target_pairs={{0,1},{1,2},{2,3},{3,0},{4,5},{5,6},{6,7},{7,4},{8,9},{9,10},{10,1... | collective-permute-start | bytes 350216 | tf_op jit(solution)/shard_map/ppermute | solution.py:33
  12.6 7.9 %collective-permute-start.3 = (f32[4,24,304]{2,1,0:T(8,128)S(1)}, f32[4,24,304]{2,1,0:T(8,128)S(1)}, u32[]{:S(2)}, u32[]{:S(2)}) collective-permute-start(f32[4,24,304]{2,1,0:T(8,128)S(1)} %copy.43), channel_id=1, source_target_pairs={{0,3},{1,0},{2,1},{3,2},{4,7},{5,4},{6,5},{7,6},{8,11},{9,8},{10,9... | collective-permute-start | bytes 350216 | tf_op jit(solution)/shard_map/ppermute | solution.py:33
  50.3 4.7 %collective-permute-start.4 = (f32[2,24,128]{2,1,0:T(8,128)S(1)}, f32[2,24,128]{2,1,0:T(8,128)S(1)}, u32[]{:S(2)}, u32[]{:S(2)}) collective-permute-start(f32[2,24,128]{2,1,0:T(8,128)S(1)} %get-tuple-element.57), channel_id=1, source_target_pairs={{0,4},{4,8},{8,12},{12,0},{1,5},{5,9},{9,13},{13,1},{2,6},{6,10},{... | collective-permute-start | bytes 73736 | tf_op jit(solution)/shard_map/ppermute | solution.py:33
  51.6 3.8 %collective-permute-start.5 = (f32[2,24,128]{2,1,0:T(8,128)S(1)}, f32[2,24,128]{2,1,0:T(8,128)S(1)}, u32[]{:S(2)}, u32[]{:S(2)}) collective-permute-start(f32[2,24,128]{2,1,0:T(8,128)S(1)} %get-tuple-element.58), channel_id=1, source_target_pairs={{0,12},{4,0},{8,4},{12,8},{1,13},{5,1},{9,5},{13,9},{2,14},{6,2},{... | collective-permute-start | bytes 73736 | tf_op jit(solution)/shard_map/ppermute | solution.py:33
  55.6 12.2 %collective-permute-start.6 = (f32[2,24,304]{1,2,0:T(8,128)S(1)}, f32[2,24,304]{1,2,0:T(8,128)S(1)}, u32[]{:S(2)}, u32[]{:S(2)}) collective-permute-start(f32[2,24,304]{1,2,0:T(8,128)S(1)} %get-tuple-element.67), channel_id=1, source_target_pairs={{0,1},{1,2},{2,3},{3,0},{4,5},{5,6},{6,7},{7,4},{8,9},{9,10},{10,1... | collective-permute-start | bytes 175112 | tf_op jit(solution)/shard_map/ppermute | solution.py:33
  56.5 14.0 %collective-permute-start.7 = (f32[2,24,304]{1,2,0:T(8,128)S(1)}, f32[2,24,304]{1,2,0:T(8,128)S(1)}, u32[]{:S(2)}, u32[]{:S(2)}) collective-permute-start(f32[2,24,304]{1,2,0:T(8,128)S(1)} %get-tuple-element.68), channel_id=1, source_target_pairs={{0,3},{1,0},{2,1},{3,2},{4,7},{5,4},{6,5},{7,6},{8,11},{9,8},{10,9... | collective-permute-start | bytes 175112 | tf_op jit(solution)/shard_map/ppermute | solution.py:33
  107.0 5.0 %collective-permute-start.8 = (f32[2,40,128]{2,1,0:T(8,128)S(1)}, f32[2,40,128]{2,1,0:T(8,128)S(1)}, u32[]{:S(2)}, u32[]{:S(2)}) collective-permute-start(f32[2,40,128]{2,1,0:T(8,128)S(1)} %get-tuple-element.55), channel_id=1, source_target_pairs={{0,4},{4,8},{8,12},{12,0},{1,5},{5,9},{9,13},{13,1},{2,6},{6,10},{... | collective-permute-start | bytes 122888 | tf_op jit(solution)/shard_map/ppermute | solution.py:33
  109.5 4.0 %collective-permute-start.9 = (f32[2,40,128]{2,1,0:T(8,128)S(1)}, f32[2,40,128]{2,1,0:T(8,128)S(1)}, u32[]{:S(2)}, u32[]{:S(2)}) collective-permute-start(f32[2,40,128]{2,1,0:T(8,128)S(1)} %get-tuple-element.56), channel_id=1, source_target_pairs={{0,12},{4,0},{8,4},{12,8},{1,13},{5,1},{9,5},{13,9},{2,14},{6,2},{... | collective-permute-start | bytes 122888 | tf_op jit(solution)/shard_map/ppermute | solution.py:33
  110.7 6.8 %copy-start.5 = (bf16[3,3,2,64]{3,2,1,0:T(2,128)(2,1)S(1)}, bf16[3,3,2,64]{3,2,1,0:T(2,128)(2,1)}, u32[]{:S(2)}) copy-start(bf16[3,3,2,64]{3,2,1,0:T(2,128)(2,1)} %param.10) | copy-start | bytes 6916
  113.7 12.7 %collective-permute-start.10 = (f32[2,40,336]{1,2,0:T(8,128)S(1)}, f32[2,40,336]{1,2,0:T(8,128)S(1)}, u32[]{:S(2)}, u32[]{:S(2)}) collective-permute-start(f32[2,40,336]{1,2,0:T(8,128)S(1)} %get-tuple-element.63), channel_id=1, source_target_pairs={{0,1},{1,2},{2,3},{3,0},{4,5},{5,6},{6,7},{7,4},{8,9},{9,10},{10,1... | collective-permute-start | bytes 322568 | tf_op jit(solution)/shard_map/ppermute | solution.py:33
  114.2 14.3 %collective-permute-start.11 = (f32[2,40,336]{1,2,0:T(8,128)S(1)}, f32[2,40,336]{1,2,0:T(8,128)S(1)}, u32[]{:S(2)}, u32[]{:S(2)}) collective-permute-start(f32[2,40,336]{1,2,0:T(8,128)S(1)} %get-tuple-element.64), channel_id=1, source_target_pairs={{0,3},{1,0},{2,1},{3,2},{4,7},{5,4},{6,5},{7,6},{8,11},{9,8},{10,9... | collective-permute-start | bytes 322568 | tf_op jit(solution)/shard_map/ppermute | solution.py:33
  152.0 28.4 %copy-start.1 = (f32[1,2,2,256,128]{4,3,2,1,0:T(8,128)S(1)}, f32[1,2,2,256,128]{4,3,2,1,0:T(8,128)}, u32[]{:S(2)}) copy-start(f32[1,2,2,256,128]{4,3,2,1,0:T(8,128)} %param.9) | copy-start | bytes 1572868
  179.8 5.6 %copy-start.2 = (f32[80,64]{1,0:T(8,128)S(1)}, f32[80,64]{1,0:T(8,128)}, u32[]{:S(2)}) copy-start(f32[80,64]{1,0:T(8,128)} %get-tuple-element.25) | copy-start | bytes 61444
  182.5 9.1 %copy-start.6 = (f32[32,128]{1,0:T(8,128)S(1)}, f32[32,128]{1,0:T(8,128)}, u32[]{:S(2)}) copy-start(f32[32,128]{1,0:T(8,128)} %get-tuple-element.23) | copy-start | bytes 49156
  182.5 4.7 %collective-permute-start.12 = (f32[2,24,128]{2,1,0:T(8,128)S(1)}, f32[2,24,128]{2,1,0:T(8,128)S(1)}, u32[]{:S(2)}, u32[]{:S(2)}) collective-permute-start(f32[2,24,128]{2,1,0:T(8,128)S(1)} %get-tuple-element.69), channel_id=1, source_target_pairs={{0,4},{4,8},{8,12},{12,0},{1,5},{5,9},{9,13},{13,1},{2,6},{6,10},{... | collective-permute-start | bytes 73736 | tf_op jit(solution)/shard_map/ppermute | solution.py:33
  183.7 3.8 %collective-permute-start.13 = (f32[2,24,128]{2,1,0:T(8,128)S(1)}, f32[2,24,128]{2,1,0:T(8,128)S(1)}, u32[]{:S(2)}, u32[]{:S(2)}) collective-permute-start(f32[2,24,128]{2,1,0:T(8,128)S(1)} %get-tuple-element.70), channel_id=1, source_target_pairs={{0,12},{4,0},{8,4},{12,8},{1,13},{5,1},{9,5},{13,9},{2,14},{6,2},{... | collective-permute-start | bytes 73736 | tf_op jit(solution)/shard_map/ppermute | solution.py:33
  185.4 6.7 %copy-start.3 = (f32[64,64]{1,0:T(8,128)S(1)}, f32[64,64]{1,0:T(8,128)}, u32[]{:S(2)}) copy-start(f32[64,64]{1,0:T(8,128)} %get-tuple-element.24) | copy-start | bytes 49156
  185.4 6.8 %copy-start.7 = (f32[1,256]{1,0:T(1,128)S(1)}, f32[1,256]{1,0:T(1,128)}, u32[]{:S(2)}) copy-start(f32[1,256]{1,0:T(1,128)} %get-tuple-element.32) | copy-start | bytes 3076
  187.7 11.6 %collective-permute-start.14 = (f32[2,24,304]{1,2,0:T(8,128)S(1)}, f32[2,24,304]{1,2,0:T(8,128)S(1)}, u32[]{:S(2)}, u32[]{:S(2)}) collective-permute-start(f32[2,24,304]{1,2,0:T(8,128)S(1)} %get-tuple-element.65), channel_id=1, source_target_pairs={{0,1},{1,2},{2,3},{3,0},{4,5},{5,6},{6,7},{7,4},{8,9},{9,10},{10,1... | collective-permute-start | bytes 175112 | tf_op jit(solution)/shard_map/ppermute | solution.py:33
  188.6 12.9 %collective-permute-start.15 = (f32[2,24,304]{1,2,0:T(8,128)S(1)}, f32[2,24,304]{1,2,0:T(8,128)S(1)}, u32[]{:S(2)}, u32[]{:S(2)}) collective-permute-start(f32[2,24,304]{1,2,0:T(8,128)S(1)} %get-tuple-element.66), channel_id=1, source_target_pairs={{0,3},{1,0},{2,1},{3,2},{4,7},{5,4},{6,5},{7,6},{8,11},{9,8},{10,9... | collective-permute-start | bytes 175112 | tf_op jit(solution)/shard_map/ppermute | solution.py:33
  250.0 1.3 collective-permute-start.16
  251.3 5.5 %collective-permute-start.17 = (f32[72,128]{1,0:T(8,128)S(1)}, f32[72,128]{1,0:T(8,128)S(1)}, u32[]{:S(2)}, u32[]{:S(2)}) collective-permute-start(f32[72,128]{1,0:T(8,128)S(1)} %fusion.12), channel_id=1, source_target_pairs={{0,4},{4,8},{8,12},{12,0},{1,5},{5,9},{9,13},{13,1},{2,6},{6,10},{... | collective-permute-start | bytes 110600 | tf_op jit(solution)/shard_map/ppermute | solution.py:33
  253.1 4.0 %collective-permute-start.18 = (f32[72,128]{1,0:T(8,128)S(1)}, f32[72,128]{1,0:T(8,128)S(1)}, u32[]{:S(2)}, u32[]{:S(2)}) collective-permute-start(f32[72,128]{1,0:T(8,128)S(1)} %fusion.12), channel_id=1, source_target_pairs={{0,8},{4,12},{8,0},{12,4},{1,9},{5,13},{9,1},{13,5},{2,10},{6,14},... | collective-permute-start | bytes 110600 | tf_op jit(solution)/shard_map/ppermute | solution.py:33
  254.0 4.0 %collective-permute-start.19 = (f32[72,128]{1,0:T(8,128)S(1)}, f32[72,128]{1,0:T(8,128)S(1)}, u32[]{:S(2)}, u32[]{:S(2)}) collective-permute-start(f32[72,128]{1,0:T(8,128)S(1)} %fusion.12), channel_id=1, source_target_pairs={{0,12},{4,0},{8,4},{12,8},{1,13},{5,1},{9,5},{13,9},{2,14},{6,2},{... | collective-permute-start | bytes 110600 | tf_op jit(solution)/shard_map/ppermute | solution.py:33
  258.0 7.0 %collective-permute-start.20 = (f32[72,128]{1,0:T(8,128)S(1)}, f32[72,128]{1,0:T(8,128)S(1)}, u32[]{:S(2)}, u32[]{:S(2)}) collective-permute-start(f32[72,128]{1,0:T(8,128)S(1)} %add_add_fusion.1), channel_id=1, source_target_pairs={{0,1},{1,2},{2,3},{3,0},{4,5},{5,6},{6,7},{7,4},{8,9},{9,10},{10,1... | collective-permute-start | bytes 110600 | tf_op jit(solution)/shard_map/ppermute | solution.py:33
  258.6 6.4 %collective-permute-start.21 = (f32[72,128]{1,0:T(8,128)S(1)}, f32[72,128]{1,0:T(8,128)S(1)}, u32[]{:S(2)}, u32[]{:S(2)}) collective-permute-start(f32[72,128]{1,0:T(8,128)S(1)} %add_add_fusion.1), channel_id=1, source_target_pairs={{0,2},{1,3},{2,0},{3,1},{4,6},{5,7},{6,4},{7,5},{8,10},{9,11},{10,... | collective-permute-start | bytes 110600 | tf_op jit(solution)/shard_map/ppermute | solution.py:33
  260.8 4.2 %collective-permute-start.22 = (f32[72,128]{1,0:T(8,128)S(1)}, f32[72,128]{1,0:T(8,128)S(1)}, u32[]{:S(2)}, u32[]{:S(2)}) collective-permute-start(f32[72,128]{1,0:T(8,128)S(1)} %add_add_fusion.1), channel_id=1, source_target_pairs={{0,3},{1,0},{2,1},{3,2},{4,7},{5,4},{6,5},{7,6},{8,11},{9,8},{10,9... | collective-permute-start | bytes 110600 | tf_op jit(solution)/shard_map/ppermute | solution.py:33

commit v2 on v1

v2 whole, which is shorter than its diff:
```python
import functools

import jax
import jax.numpy as jnp
import numpy as np
from jax import lax
from jax.experimental import pallas as pl
from jax.experimental.pallas import tpu as pltpu
from jax.sharding import PartitionSpec as P

SWEEPS = 16
TIME_STEP = 0.2
VISCOSITY = 0.05
DRAG_RATE = 0.1
FORCE_WAVES = 4.0
COEF_SCALE = 0.1
EPSILON = 1e-06
OUTER_WEIGHT = -1.0 / 16.0
INNER_WEIGHT = 9.0 / 16.0
TWO_PI = 6.283185307179586

TOP = 40
LEFT = 64
CHUNK_ROWS = 16
LEAD = 384
GUARD = 8
BF16 = jnp.bfloat16
F32 = jnp.float32


def passed_along(block, axis, distance):
    size = lax.axis_size(axis)
    route = [(i, (i + distance) % size) for i in range(size)]
    return lax.ppermute(block, axis, route)


def exchange(own, rim):
    before = passed_along(own[:, -rim:], "gx", 1)
    after = passed_along(own[:, :rim], "gx", -1)
    tall = jnp.concatenate([before, own, after], axis=1)
    left = passed_along(jnp.swapaxes(tall[:, :, -rim:], 1, 2), "gy", 1)
    right = passed_along(jnp.swapaxes(tall[:, :, :rim], 1, 2), "gy", -1)
    wide = jnp.concatenate([jnp.swapaxes(left, 1, 2), tall, jnp.swapaxes(right, 1, 2)], axis=2)
    return jnp.pad(wide, ((0, 0), (TOP - rim, TOP - rim), (LEFT - rim, LEFT - rim)))


def total_over(value, axis):
    size = lax.axis_size(axis)
    if size <= 4:
        moved = [passed_along(value, axis, distance) for distance in range(1, size)]
        for other in moved:
            value = value + other
        return value
    return lax.psum(value, axis)


def at(field, rows, cols):
    if rows:
        field = pltpu.roll(field, (-rows) % field.shape[0], 0)
    if cols:
        field = pltpu.roll(field, (-cols) % field.shape[1], 1)
    return field


def project(first, second, buffers, rhs_ref, rim):
    height = first.shape[0]
    quarter = -0.125 * (at(first, 1, 0) - at(first, -1, 0) + at(second, 0, 1) - at(second, 0, -1))
    for half in range(2):
        part = quarter[:, 128 * half : 128 * half + 128]
        rhs_ref[half] = part
        for buffer in range(2):
            buffers[buffer, half, :GUARD] = jnp.zeros((GUARD, 128), F32)
            buffers[buffer, half, GUARD + height :] = jnp.zeros((GUARD, 128), F32)
            buffers[buffer, half, GUARD : GUARD + height] = part
    lane = lax.broadcasted_iota(jnp.int32, (8, 128), 1)
    at_start = lane == 0
    at_end = lane == 127

    def one_sweep(source, target):
        for row in range(TOP - rim, height - TOP + rim, 8):
            here = [buffers[source, half, GUARD + row : GUARD + row + 8] for half in range(2)]
            ahead = [pltpu.roll(part, 127, 1) for part in here]
            behind = [pltpu.roll(part, 1, 1) for part in here]
            for half in range(2):
                above = buffers[source, half, GUARD + row - 1 : GUARD + row + 7]
                below = buffers[source, half, GUARD + row + 1 : GUARD + row + 9]
                east = jnp.where(at_end, ahead[1 - half], ahead[half])
                west = jnp.where(at_start, behind[1 - half], behind[half])
                near = (above + below) + (east + west)
                buffers[target, half, GUARD + row : GUARD + row + 8] = 0.25 * near + rhs_ref[half, row : row + 8]

    def two_sweeps(index, carried):
        one_sweep(0, 1)
        one_sweep(1, 0)
        return carried

    lax.fori_loop(0, SWEEPS // 2, two_sweeps, 0)
    p = jnp.concatenate([buffers[0, half, GUARD : GUARD + height] for half in range(2)], axis=1)
    above = jnp.concatenate([buffers[0, half, GUARD - 1 : GUARD - 1 + height] for half in range(2)], axis=1)
    below = jnp.concatenate([buffers[0, half, GUARD + 1 : GUARD + 1 + height] for half in range(2)], axis=1)
    return first - 0.5 * (below - above), second - 0.5 * (at(p, 0, 1) - at(p, 0, -1))


def faces(field, c0, c1, c2, move):
    return (
        (OUTER_WEIGHT + c0) * move(field, -1)
        + (INNER_WEIGHT + c1) * field
        + (INNER_WEIGHT + c2) * move(field, 1)
        + (OUTER_WEIGHT - c0 - c1 - c2) * move(field, 2)
    )


def by_row(field, distance):
    return at(field, distance, 0)


def by_col(field, distance):
    return at(field, 0, distance)


def advect(v, coefs, forcing):
    speed_rows = 0.5 * (v[0] + by_row(v[0], 1))
    speed_cols = 0.5 * (v[1] + by_col(v[1], 1))
    results = []
    for comp in range(2):
        q = v[comp]
        flux = speed_rows * faces(q, coefs[0], coefs[1], coefs[2], by_row)
        change = flux - by_row(flux, -1)
        flux = speed_cols * faces(q, coefs[3], coefs[4], coefs[5], by_col)
        change = change + (flux - by_col(flux, -1))
        laplace = by_row(q, 1) + by_row(q, -1) + by_col(q, 1) + by_col(q, -1) - 4.0 * q
        drive = VISCOSITY * laplace - DRAG_RATE * q
        if comp == 0:
            drive = drive + forcing
        results.append(q - TIME_STEP * change + TIME_STEP * drive)
    return results


def advect_back(v, coefs, g, keep_taps):
    results = [None, None]
    for axis in range(2):
        move = by_row if axis == 0 else by_col
        speed = 0.5 * (v[axis] + move(v[axis], 1))
        c0, c1, c2 = coefs[3 * axis : 3 * axis + 3]
        grads = []
        grad_speed = None
        taps = None
        for comp in range(2):
            q = v[comp]
            grad_flux = TIME_STEP * (move(g[comp], 1) - g[comp])
            term = grad_flux * faces(q, c0, c1, c2, move)
            grad_speed = term if grad_speed is None else grad_speed + term
            grad_face = grad_flux * speed
            behind = move(q, -1)
            ahead = move(q, 1)
            far = move(q, 2)
            new = (grad_face * (behind - far), grad_face * (q - far), grad_face * (ahead - far))
            taps = new if taps is None else tuple(a + b for a, b in zip(taps, new))
            grads.append(
                move(grad_face * (OUTER_WEIGHT + c0), 1)
                + grad_face * (INNER_WEIGHT + c1)
                + move(grad_face * (INNER_WEIGHT + c2), -1)
                + move(grad_face * (OUTER_WEIGHT - c0 - c1 - c2), -2)
            )
        grads[axis] = grads[axis] + 0.5 * (grad_speed + move(grad_speed, -1))
        for number in range(3):
            keep_taps(3 * axis + number, COEF_SCALE * taps[number])
        for comp in range(2):
            results[comp] = grads[comp] if axis == 0 else results[comp] + grads[comp]
    for comp in range(2):
        near = by_row(g[comp], 1) + by_row(g[comp], -1) + by_col(g[comp], 1) + by_col(g[comp], -1)
        drive = VISCOSITY * (near - 4.0 * g[comp]) - DRAG_RATE * g[comp]
        results[comp] = results[comp] + g[comp] + TIME_STEP * drive
    return results


class Plan:
    def __init__(self, rows, cols, rim):
        self.rows, self.cols, self.rim = rows, cols, rim
        self.wide = -(-(cols + 2 * rim + 4) // 8) * 8
        self.chunk = CHUNK_ROWS * self.wide
        self.chunks = -(-(rows + 2 * rim + 2) // CHUNK_ROWS)
        self.offsets = [row * self.wide + col for row in range(3) for col in range(3)]
        self.in_row, self.in_lane = TOP - rim - 2, LEFT - rim - 2
        self.out_row, self.out_lane = TOP - rim, LEFT - rim
        self.window = -(-(CHUNK_ROWS + 2) * self.wide // 128) * 128


def rounded(field):
    return field.astype(BF16).astype(F32)


def shifted(block, offset, length):
    if offset % block.shape[1]:
        block = pltpu.roll(block, (-offset) % block.shape[1], 1)
    return block[:, :length]


def lay_rows(source_ref, first_row, lane, wide, target_ref):
    lanes = lax.broadcasted_iota(jnp.int32, (8, 128), 1)
    tiles = {}
    for number in range(CHUNK_ROWS + 2):
        place = pl.ds(pl.multiple_of(8 * (first_row + number), 8), 8)
        block = jnp.concatenate([source_ref[half, place] for half in range(2)], axis=1)
        start = number * wide
        tile, offset = start // 128, start % 128
        block = pltpu.roll(block, (offset - lane) % 256, 1)
        for part in range(-(-(offset + wide) // 128)):
            piece = block[:, 128 * (part % 2) : 128 * (part % 2) + 128]
            if part == 0 and offset:
                piece = jnp.where(lanes < offset, tiles[tile], piece)
            tiles[tile + part] = piece
    for tile in range(target_ref.shape[1] // 128):
        target_ref[:, 128 * tile : 128 * tile + 128] = tiles[tile]


def split_rows(flat, target_ref, first_row, lane, wide):
    for number in range(CHUNK_ROWS):
        start = number * wide
        tile, offset = start // 128, start % 128
        parts = max(2, -(-(offset + wide) // 128))
        if tile + parts > flat.shape[1] // 128:
            tile, offset = tile - 1, offset + 128
        block = flat[:, 128 * tile : 128 * (tile + parts)]
        block = shifted(block, offset - lane, 256)
        place = pl.ds(pl.multiple_of(8 * (first_row + number), 8), 8)
        for half in range(2):
            target_ref[half, place] = block[:, 128 * half : 128 * half + 128]


def channel(ref, number, first_row, rows):
    place = pl.ds(8 * first_row + number, rows, stride=8)
    return jnp.concatenate([ref[half, place] for half in range(2)], axis=1)


def keep_channel(ref, number, first_row, field):
    place = pl.ds(8 * first_row + number, field.shape[0], stride=8)
    for half in range(2):
        ref[half, place] = field[:, 128 * half : 128 * half + 128]


def keep_inputs(v, inputs_ref):
    inputs_ref[...] = jnp.zeros_like(inputs_ref)
    for comp in range(2):
        field = rounded(v[comp])
        for col in range(3):
            keep_channel(inputs_ref, 2 * col + comp, 0, by_col(field, col))
    keep_channel(inputs_ref, 6, 0, jnp.ones_like(v[0]))


def product(left, right):
    return lax.dot_general(left, right, (((1,), (0,)), ((), ())), preferred_element_type=F32)


def product_over_cells(left, right):
    return lax.dot_general(left, right, (((1,), (1,)), ((), ())), preferred_element_type=F32)


def columns(plan, step, inputs_ref, window_ref):
    lay_rows(inputs_ref, plan.in_row + CHUNK_ROWS * step, plan.in_lane, plan.wide, window_ref)
    window = window_ref[...]
    parts = [shifted(window, row * plan.wide, plan.chunk) for row in range(3)]
    return jnp.concatenate(parts + [jnp.zeros((8, plan.chunk), F32)], axis=0)


def add_taps(terms_ref, offsets, length):
    total = None
    for tap, offset in enumerate(offsets):
        term = shifted(terms_ref[8 * tap : 8 * tap + 8, :], offset, length)
        total = term if total is None else total + term
    return total


def network(plan, inputs_ref, weight_refs, coefs_ref, window_ref, terms_ref):
    w1_ref, b1_ref, w2_ref, b2_ref, w3_ref = weight_refs
    terms_ref[...] = jnp.zeros_like(terms_ref)
    lag = LEAD - 2 * plan.wide

    def one_chunk(step, carried):
        cols = columns(plan, step, inputs_ref, window_ref).astype(BF16)
        half = product(w1_ref[...], cols) + b1_ref[...]
        hidden = (half * jnp.tanh(half) + half).astype(BF16)
        half = product(w2_ref[...], hidden) + b2_ref[...]
        hidden = (half * jnp.tanh(half) + half).astype(BF16)
        terms_ref[:, :LEAD] = terms_ref[:, plan.chunk :]
        terms_ref[:, LEAD:] = product(w3_ref[...], hidden)
        total = COEF_SCALE * add_taps(terms_ref, [offset + lag for offset in plan.offsets], plan.chunk)
        split_rows(total, coefs_ref, plan.out_row - 2 + CHUNK_ROWS * step, plan.out_lane, plan.wide)
        return carried

    lax.fori_loop(0, plan.chunks, one_chunk, 0)


def network_back(plan, inputs_ref, taps_ref, weight_refs, place_ref, grads_ref, sums_ref, window_ref, terms_ref):
    w1_ref, b1_ref, w2_ref, b2_ref, w1b_ref, w2b_ref, w3b_ref = weight_refs
    terms_ref[...] = jnp.zeros_like(terms_ref)

    def one_chunk(step, carried):
        row = place_ref[...] + CHUNK_ROWS * step
        own = jnp.where((row >= plan.rim + 1) & (row < plan.rim + 1 + plan.rows), 1.0, 0.0)
        mask = own.astype(BF16)
        cols = columns(plan, step, inputs_ref, window_ref)
        half = product(w1_ref[...], cols.astype(BF16)) + b1_ref[...]
        bend = jnp.tanh(half)
        hidden_one = (half * bend + half).astype(BF16)
        slope_one = (0.5 + 0.5 * bend) * (1.0 + half * (1.0 - bend))
        half = product(w2_ref[...], hidden_one) + b2_ref[...]
        bend = jnp.tanh(half)
        hidden_two = (half * bend + half).astype(BF16)
        slope_two = (0.5 + 0.5 * bend) * (1.0 + half * (1.0 - bend))
        lay_rows(taps_ref, plan.out_row - 2 + CHUNK_ROWS * step, plan.out_lane, plan.wide, window_ref)
        window = window_ref[...]
        parts = [shifted(window, 2 * plan.wide - offset, plan.chunk) for offset in plan.offsets]
        spread = jnp.concatenate(parts + [jnp.zeros((8, plan.chunk), F32)], axis=0).astype(BF16)
        grad_two = (product(w3b_ref[...], spread) * slope_two).astype(BF16)
        grad_one = (product(w2b_ref[...], grad_two) * slope_one).astype(BF16)
        sums_ref[:80, :64] += product_over_cells(spread, hidden_two * mask)
        sums_ref[:64, 64:] += product_over_cells(hidden_one, grad_two * mask)
        both = jnp.concatenate([grad_one, grad_two], axis=0)
        sums_ref[80:, :] += product_over_cells((cols * own).astype(BF16), both)
        terms_ref[:, :LEAD] = terms_ref[:, plan.chunk :]
        terms_ref[:, LEAD:] = product(w1b_ref[...], grad_one)
        total = add_taps(terms_ref, [LEAD - offset for offset in plan.offsets], plan.chunk)
        split_rows(total, grads_ref, plan.in_row + CHUNK_ROWS * step, plan.in_lane, plan.wide)
        return carried

    lax.fori_loop(0, plan.chunks, one_chunk, 0)


def own_part(field, rows, cols, first_row):
    return pltpu.roll(field[TOP - first_row : TOP - first_row + rows], 256 - LEFT, 1)[:, :cols]


def lane_sums(squares):
    return jnp.sum(squares, axis=0, keepdims=True)


def first_kernel(plan, v_ref, goal_ref, force_ref, w1, b1, w2, b2, w3, v_out, coefs_ref, error_ref, loss_ref,
                 inputs_ref, window_ref, terms_ref, frame_ref, buffers, rhs_ref):
    keep_inputs([v_ref[0], v_ref[1]], inputs_ref)
    coefs_ref[...] = jnp.zeros_like(coefs_ref)
    network(plan, inputs_ref, (w1, b1, w2, b2, w3), coefs_ref, window_ref, terms_ref)
    height = v_ref.shape[1]
    result = advect(
        [v_ref[0], v_ref[1]], [channel(coefs_ref, number, 0, height) for number in range(6)], force_ref[...]
    )
    for comp in range(2):
        frame_ref[comp] = result[comp]
    result = project(frame_ref[0], frame_ref[1], buffers, rhs_ref, 24)
    loss = None
    for comp in range(2):
        v_out[comp] = result[comp]
        error = own_part(result[comp], plan.rows, plan.cols, 0) - goal_ref[comp]
        error_ref[comp] = error
        square = lane_sums(error * error)
        loss = square if loss is None else loss + square
    loss_ref[...] = loss


def second_kernel(plan, v_ref, force_ref, w1, b1, w2, b2, w3, out_ref, coefs_ref, inputs_ref, window_ref, terms_ref):
    keep_inputs([v_ref[0], v_ref[1]], inputs_ref)
    coefs_ref[...] = jnp.zeros_like(coefs_ref)
    network(plan, inputs_ref, (w1, b1, w2, b2, w3), coefs_ref, window_ref, terms_ref)
    low, tall = TOP - 8, plan.rows + 16
    v = [v_ref[comp, low : low + tall] for comp in range(2)]
    result = advect(v, [channel(coefs_ref, number, low, tall) for number in range(6)], force_ref[...])
    for comp in range(2):
        out_ref[comp] = own_part(result[comp], plan.rows, plan.cols, low)


def back_kernel(plan, last, in_ref, goal_ref, extra_ref, before_ref, v_ref, coefs_ref, place_ref,
                w1, b1, w2, b2, w1b, w2b, w3b, out_ref, sums_ref,
                inputs_ref, taps_ref, grads_ref, window_ref, terms_ref, frame_ref, buffers, rhs_ref):
    rows, cols = plan.rows, plan.cols
    sums_ref[...] = before_ref[...]
    first, second = project(in_ref[0], in_ref[1], buffers, rhs_ref, TOP if last else 24)
    if last:
        errors = (first - goal_ref[0], second - goal_ref[1])
        for error in errors:
            mine = own_part(error, rows, cols, 0)
            sums_ref[111:112, :] += lane_sums(mine * mine)
        for comp in range(2):
            frame_ref[comp] = errors[comp]
        first, second = project(frame_ref[0], frame_ref[1], buffers, rhs_ref, 24)
    frame_ref[0] = first
    frame_ref[1] = second
    keep_inputs([v_ref[0], v_ref[1]], inputs_ref)
    taps_ref[...] = jnp.zeros_like(taps_ref)
    low, tall = TOP - 8, rows + 16
    result = advect_back(
        [v_ref[comp, low : low + tall] for comp in range(2)],
        [channel(coefs_ref, number, low, tall) for number in range(6)],
        [frame_ref[comp, low : low + tall] for comp in range(2)],
        lambda number, field: keep_channel(taps_ref, number, low, rounded(field)),
    )
    for comp in range(2):
        frame_ref[comp, low : low + tall] = result[comp]
    weight_refs = (w1, b1, w2, b2, w1b, w2b, w3b)
    network_back(plan, inputs_ref, taps_ref, weight_refs, place_ref, grads_ref, sums_ref, window_ref, terms_ref)
    for comp in range(2):
        field = frame_ref[comp, low : low + tall] + channel(grads_ref, comp, low, tall)
        total = own_part(field, rows, cols, low)
        out_ref[comp] = total + extra_ref[comp] if last else total


def scaled(piece, count):
    return piece * (1.0 / jnp.sqrt(jnp.sum(piece * piece) / count + EPSILON))


def finish_kernel(loss_scale, in_ref, w1_ref, b1_ref, w2_ref, b2_ref, w3_ref, loss_ref):
    one = jnp.concatenate([in_ref[80 + 8 * row : 86 + 8 * row, :64] for row in range(3)], axis=0)
    w1_ref[...] = scaled(one, one.size)
    b1_ref[...] = scaled(in_ref[86:87, :64], 64)
    b2_ref[...] = scaled(in_ref[86:87, 64:], 64)
    w2_ref[...] = scaled(in_ref[:64, 64:], 64 * 64)
    w3_ref[...] = scaled(in_ref[:72, :64], 54 * 64)
    loss_ref[...] = (0.5 * loss_scale) * jnp.sum(in_ref[111:112, :], axis=1, keepdims=True)


def shards(velocity, targets, weight_one, bias_one, weight_two, bias_two, weight_three):
    rows, cols = velocity.shape[2], velocity.shape[3]
    step_count = targets.shape[1]
    height = rows + 2 * TOP
    frame = (height, cols + 2 * LEFT)
    pair = (2,) + frame
    own_pair = (2, rows, cols)
    packed = (2, 8 * height, 128)
    sums_shape = (112, 128)
    hid = weight_two.shape[0]
    nout = weight_three.shape[3]
    near = Plan(rows, cols, 2)
    far = Plan(rows, cols, 23)

    def call(kernel, outs, scratch, *args):
        return pl.pallas_call(
            kernel,
            out_shape=[jax.ShapeDtypeStruct(shape, F32) for shape in outs],
            scratch_shapes=[pltpu.VMEM(shape, F32) for shape in scratch],
            compiler_params=pltpu.CompilerParams(vmem_limit_bytes=60 << 20),
        )(*args)

    def net_scratch(plan):
        return [(8, plan.window), (72, plan.chunk + LEAD)]

    sweep_scratch = [pair, (2, 2, height + 2 * GUARD, 128), (2, height, 128)]

    w1 = jnp.pad(weight_one.reshape(3, 6, hid), ((0, 1), (0, 2), (0, 0))).reshape(32, hid)
    w1_half = (0.5 * w1.astype(F32)).astype(BF16).T
    w2_half = (0.5 * weight_two.astype(F32)).astype(BF16).T
    b1_half = 0.5 * bias_one[:, None]
    b2_half = 0.5 * bias_two[:, None]
    w3 = jnp.pad(weight_three.reshape(9, hid, nout), ((0, 0), (0, 0), (0, 8 - nout)))
    w3_out = jnp.transpose(w3, (0, 2, 1)).reshape(72, hid)
    w3_back = jnp.pad(jnp.transpose(w3, (1, 0, 2)).reshape(hid, 72), ((0, 0), (0, 8)))
    w1_back = jnp.pad(weight_one.reshape(9, 2, hid), ((0, 0), (0, 6), (0, 0))).reshape(72, hid)
    forward_weights = (w1_half, b1_half, w2_half, b2_half, w3_out)
    backward_weights = (w1_half, b1_half, w2_half, b2_half, w1_back, weight_two, w3_back)

    lane = np.arange(near.chunk)
    place_row, place_col = lane // near.wide, lane % near.wide
    mine = (place_col >= near.rim + 1) & (place_col < near.rim + 1 + cols)
    place = jnp.asarray(np.where(mine, place_row, -10 * height)[None, :], jnp.int32)

    total_cols = cols * lax.axis_size("gy")
    col_ids = lax.axis_index("gy") * cols + jnp.arange(frame[1], dtype=jnp.int32) - LEFT
    forcing = jnp.sin(col_ids.astype(F32) * (TWO_PI * FORCE_WAVES / total_cols))[None, :]

    both = exchange(jnp.concatenate([velocity[0], targets[0, step_count - 1]], axis=0), 32)
    v_first = both[:2]
    v_second, coefs_first, error_first, loss_first = call(
        functools.partial(first_kernel, far),
        [pair, packed, own_pair, (1, cols)],
        [packed] + net_scratch(far) + sweep_scratch,
        v_first, targets[0, 0], forcing, *forward_weights,
    )
    provisional, coefs_second = call(
        functools.partial(second_kernel, near),
        [own_pair, packed],
        [packed] + net_scratch(near),
        v_second, forcing, *forward_weights,
    )
    back_scratch = [packed, packed, packed] + net_scratch(near) + sweep_scratch
    start_sums = jnp.pad(loss_first, ((111, 0), (0, 128 - cols)))
    framed = exchange(provisional, 40)
    grad, sums = call(
        functools.partial(back_kernel, near, True), [own_pair, sums_shape], back_scratch,
        framed, both[2:], error_first, start_sums, v_second, coefs_second, place, *backward_weights,
    )
    framed = exchange(grad, 24)
    grad, sums = call(
        functools.partial(back_kernel, near, False), [own_pair, sums_shape], back_scratch,
        framed, forcing, forcing, sums, v_first, coefs_first, place, *backward_weights,
    )
    for axis in ("ens", "gx", "gy"):
        sums = total_over(sums, axis)
    device_count = lax.axis_size(("ens", "gx", "gy"))
    loss_scale = 1.0 / float(step_count * 2 * rows * cols * device_count)
    d1, db1, d2, db2, d3, loss = call(
        functools.partial(finish_kernel, loss_scale),
        [(18, hid), (1, hid), (hid, hid), (1, hid), (72, hid), (1, 1)], [], sums,
    )
    return (
        d1.reshape(weight_one.shape),
        db1[0],
        d2,
        db2[0],
        d3.reshape(9, 8, hid)[:, :nout].transpose(0, 2, 1).reshape(weight_three.shape),
        loss[0, 0],
        grad[None],
    )


def solution(mesh):
    return jax.shard_map(
        shards,
        mesh=mesh,
        in_specs=(P("ens", None, "gx", "gy"), P("ens", None, None, "gx", "gy"), P(), P(), P(), P(), P()),
        out_specs=(P(), P(), P(), P(), P(), P(), P("ens", None, "gx", "gy")),
        check_vma=False,
    )
```

time: 278 us -> 218 us (0.78)
  local copies, waits for them, and re-layouts: 40.1 us -> 14.1 us
  other arithmetic: 21.1 us -> 7.22 us
  starting transfers between devices: 37.4 us -> 30.5 us
  between operations: 7.46 us -> 0.8 us
  Pallas kernels: 132 us -> 126 us
    slice x18 -> x3, local copies, waits for them, and re-layouts: 17.4 us -> 2.73 us  [the longest x2 1.57 us: exchange(): after = passed_along(own[:, :rim], 'gx', -1)]
    reshape x16 -> x2, local copies, waits for them, and re-layouts: 8.43 us -> 1.33 us  [the longest x1 1.31 us: shards(): d1.reshape(weight_one.shape)]
    ppermute x23 -> x19, starting transfers between devices: 37.4 us -> 30.5 us  [passed_along(): return lax.ppermute(block, axis, route)]
    pallas_call x11 -> x5, Pallas kernels: 132 us -> 126 us  [call(): pl.pallas_call(kernel, out_shape=[jax.ShapeDtypeStruct(shape, F32) for sh...]
    pad x4 -> x0, other arithmetic: 3.89 us -> none  [the longest x2 2.23 us: network_back(): cells = jnp.pad(cells, ((0, 8 - nout), (LEAD, length - used * wide)))]
    pad x3 -> x1, local copies, waits for them, and re-layouts: 4.27 us -> 0.64 us  [shards(): start_sums = jnp.pad(loss_first, ((111, 0), (0, 128 - cols)))]
    reduce_sum x5 -> x0, other arithmetic: 3.16 us -> none  [the longest x4 2.55 us: shards(): scaled = segment * (1.0 / jnp.sqrt(jnp.mean(jnp.square(segment)) + EPSILON))]
    ppermute x23 -> x19, waiting for transfers between devices: 37.9 us -> 38.9 us  [passed_along(): return lax.ppermute(block, axis, route)]
  transfers between devices with their start and end apart: 23 -> 19, of which waited for: 17 -> 17; matrix products, arithmetic and copies ran while one was open for 6% -> 4% of each run, Pallas kernels for 0% -> 0%
where the time goes in v2:
time: 218 us
  Pallas kernels  126 us (58%)
  waiting for transfers between devices  38.9 us (18%)
  starting transfers between devices  30.5 us (14%)
  local copies, waits for them, and re-layouts  14.1 us (6%)
  other arithmetic  7.22 us (3%)
    pallas_call x5, Pallas kernels, call(): pl.pallas_call(kernel, out_shape=[jax.ShapeDtypeStruct(shape, F32) for sh...  126 us
    ppermute x19, waiting for transfers between devices, passed_along(): return lax.ppermute(block, axis, route)  38.9 us
    ppermute x19, starting transfers between devices, passed_along(): return lax.ppermute(block, axis, route)  30.5 us
  transfers between devices with their start and end apart: 19, of which 17 were waited for; matrix products, arithmetic and copies ran while one was open for 4% of the time, Pallas kernels for 0%

profile of v2, /device:TPU:0, one launch (start us, length us, event | category | flops | bytes accessed | tf_op | source)
XLA Modules:
  0.0 217.9 jit_solution(7475566195633276307)
XLA Ops:
  0.7 1.8 slice_bitcast_fusion.6
  2.5 0.8 pad_maximum_fusion.2
  3.3 3.0 %collective-permute-start = (f32[4,32,128]{2,1,0:T(8,128)S(1)}, f32[4,32,128]{2,1,0:T(8,128)S(1)}, u32[]{:S(2)}, u32[]{:S(2)}) collective-permute-start(f32[4,32,128]{2,1,0:T(8,128)S(1)} %get-tuple-element.45), channel_id=1, source_target_pairs={{0,4},{4,8},{8,12},{12,0},{1,5},{5,9},{9,13},{13,1},{2,6},{6,10},{... | collective-permute-start | bytes 196616 | tf_op jit(solution)/shard_map/ppermute | solution.py:34
  6.3 1.0 collective-permute-start.1
  8.1 1.6 collective-permute-done
  9.6 1.4 collective-permute-done.1
  11.5 1.6 collective-permute-start.2
  13.4 2.3 %collective-permute-start.3 = (f32[4,32,320]{2,1,0:T(8,128)S(1)}, f32[4,32,320]{2,1,0:T(8,128)S(1)}, u32[]{:S(2)}, u32[]{:S(2)}) collective-permute-start(f32[4,32,320]{2,1,0:T(8,128)S(1)} %copy.40), channel_id=1, source_target_pairs={{0,3},{1,0},{2,1},{3,2},{4,7},{5,4},{6,5},{7,6},{8,11},{9,8},{10,9... | collective-permute-start | bytes 491528 | tf_op jit(solution)/shard_map/ppermute | solution.py:34
  19.0 2.2 %collective-permute-done.2 = f32[4,32,320]{2,1,0:T(8,128)S(1)} collective-permute-done((f32[4,32,320]{2,1,0:T(8,128)S(1)}, f32[4,32,320]{2,1,0:T(8,128)S(1)}, u32[]{:S(2)}, u32[]{:S(2)}) %collective-permute-start.2) | collective-permute-done | bytes 163872 | tf_op jit(solution)/shard_map/ppermute | solution.py:34
  21.5 1.7 collective-permute-done.3
  23.4 0.9 select_maximum_fusion
  24.3 1.2 fusion.9
  25.4 27.8 %shard_map.135 = (f32[2,336,256]{2,1,0:T(8,128)}, f32[2,2688,128]{2,1,0:T(8,128)}, f32[2,256,128]{2,1,0:T(8,128)}, f32[1,128]{1,0:T(1,128)}) custom-call(f32[2,336,256]{2,1,0:T(8,128)} %get-tuple-element.40.v_ref, f32[2,256,128]{2,1,0:T(8,128)} %get-tuple-element.43.goal_ref, f32[1,256]{1,0:T(1,128)} %multiply_sine_fusion.force_ref.goal_ref.extra_ref, ...), custom_call_target="tpu_custom_call" | custom-call | tf_op jit(solution)/shard_map/pallas_call | solution.py:435
  53.2 20.4 %shard_map.136 = (f32[2,256,128]{2,1,0:T(8,128)}, f32[2,2688,128]{2,1,0:T(8,128)}) custom-call(f32[2,336,256]{2,1,0:T(8,128)} %get-tuple-element.23.v_ref, f32[1,256]{1,0:T(1,128)} %multiply_sine_fusion.force_ref.goal_ref.extra_ref, bf16[64,32]{1,0:T(8,128)(2,1)} %bitcast.59, f32[64,1]{1,0:T(8,128)} %copy.44.b1, bf16[64,64]{1,0:T(8,128)(2,1)} %fusion.7.w2, ...), custom_call_target="tpu_custom_call" | custom-call | tf_op jit(solution)/shard_map/pallas_call | solution.py:435
  73.6 0.8 fusion.11
  74.4 2.1 collective-permute-start.4
  77.2 0.8 collective-permute-start.5
  78.0 1.5 collective-permute-done.4
  79.5 1.0 constant_dynamic-update-slice_fusion.1
  81.4 0.9 collective-permute-start.6
  82.3 3.0 %collective-permute-start.7 = (f32[2,40,336]{1,2,0:T(8,128)S(1)}, f32[2,40,336]{1,2,0:T(8,128)S(1)}, u32[]{:S(2)}, u32[]{:S(2)}) collective-permute-start(f32[2,40,336]{1,2,0:T(8,128)S(1)} %get-tuple-element.48), channel_id=1, source_target_pairs={{0,3},{1,0},{2,1},{3,2},{4,7},{5,4},{6,5},{7,6},{8,11},{9,8},{10,9... | collective-permute-start | bytes 322568 | tf_op jit(solution)/shard_map/ppermute | solution.py:34
  86.5 7.7 %collective-permute-done.6 = f32[2,40,336]{1,2,0:T(8,128)S(1)} collective-permute-done((f32[2,40,336]{1,2,0:T(8,128)S(1)}, f32[2,40,336]{1,2,0:T(8,128)S(1)}, u32[]{:S(2)}, u32[]{:S(2)}) %collective-permute-start.6) | collective-permute-done | bytes 107552 | tf_op jit(solution)/shard_map/ppermute | solution.py:34
  94.2 3.5 %collective-permute-done.7 = f32[2,40,336]{1,2,0:T(8,128)S(1)} collective-permute-done((f32[2,40,336]{1,2,0:T(8,128)S(1)}, f32[2,40,336]{1,2,0:T(8,128)S(1)}, u32[]{:S(2)}, u32[]{:S(2)}) %collective-permute-start.7) | collective-permute-done | bytes 107552 | tf_op jit(solution)/shard_map/ppermute | solution.py:34
  97.7 1.4 select_maximum_fusion.7.in_ref
  99.2 40.3 %shard_map.137 = (f32[2,256,128]{2,1,0:T(8,128)}, f32[112,128]{1,0:T(8,128)}) custom-call(f32[2,336,256]{2,1,0:T(8,128)} %select_maximum_fusion.7.in_ref, f32[2,336,256]{2,1,0:T(8,128)} %get-tuple-element.39.goal_ref, f32[2,256,128]{2,1,0:T(8,128)} %get-tuple-element.25.extra_ref, f32[112,128]{1,0:T(8,128)} %pad.36.before_ref, ...), custom_call_target="tpu_custom_call" | custom-call | tf_op jit(solution)/shard_map/pallas_call | solution.py:435
  140.2 1.9 collective-permute-start.8
  142.1 1.1 collective-permute-start.9
  143.2 1.8 collective-permute-done.8
  145.0 1.0 constant_dynamic-update-slice_fusion.4
  146.7 3.3 %collective-permute-start.11 = (f32[2,24,304]{1,2,0:T(8,128)S(1)}, f32[2,24,304]{1,2,0:T(8,128)S(1)}, u32[]{:S(2)}, u32[]{:S(2)}) collective-permute-start(f32[2,24,304]{1,2,0:T(8,128)S(1)} %get-tuple-element.50), channel_id=1, source_target_pairs={{0,3},{1,0},{2,1},{3,2},{4,7},{5,4},{6,5},{7,6},{8,11},{9,8},{10,9... | collective-permute-start | bytes 175112 | tf_op jit(solution)/shard_map/ppermute | solution.py:34
  150.0 8.2 %collective-permute-done.10 = f32[2,24,304]{1,2,0:T(8,128)S(1)} collective-permute-done((f32[2,24,304]{1,2,0:T(8,128)S(1)}, f32[2,24,304]{1,2,0:T(8,128)S(1)}, u32[]{:S(2)}, u32[]{:S(2)}) %collective-permute-start.10) | collective-permute-done | bytes 58400 | tf_op jit(solution)/shard_map/ppermute | solution.py:34
  158.2 1.8 collective-permute-done.11
  160.0 1.3 select_maximum_fusion.5.in_ref
  161.3 35.9 %shard_map.138 = (f32[2,256,128]{2,1,0:T(8,128)}, f32[112,128]{1,0:T(8,128)}) custom-call(f32[2,336,256]{2,1,0:T(8,128)} %select_maximum_fusion.5.in_ref, f32[1,256]{1,0:T(1,128)} %multiply_sine_fusion.force_ref.goal_ref.extra_ref, f32[1,256]{1,0:T(1,128)} %multiply_sine_fusion.force_ref.goal_ref.extra_ref, f32[112,128]{1,0:T(8,128)} %get-tuple-element.29.before_ref, ...), custom_call_target="tpu_custom_call" | custom-call | tf_op jit(solution)/shard_map/pallas_call | solution.py:435
  197.2 1.4 collective-permute-done.12
  198.6 0.8 add.60
  199.5 1.3 collective-permute-start.13
  200.7 0.8 collective-permute-start.14
  201.6 1.8 collective-permute-start.15
  203.4 1.4 collective-permute-done.13
  204.8 0.8 collective-permute-done.14
  205.8 0.8 collective-permute-start.16
  206.6 1.9 collective-permute-start.17
  208.5 2.3 %collective-permute-start.18 = (f32[112,128]{1,0:T(8,128)S(1)}, f32[112,128]{1,0:T(8,128)S(1)}, u32[]{:S(2)}, u32[]{:S(2)}) collective-permute-start(f32[112,128]{1,0:T(8,128)S(1)} %add_add_fusion.1), channel_id=1, source_target_pairs={{0,3},{1,0},{2,1},{3,2},{4,7},{5,4},{6,5},{7,6},{8,11},{9,8},{10,9... | collective-permute-start | bytes 172040 | tf_op jit(solution)/shard_map/ppermute | solution.py:34
  210.9 1.6 collective-permute-done.16
  212.4 1.5 collective-permute-done.17
  214.6 2.0 shard_map.139
  216.6 1.3 reshape.73
  (50 shorter events, 10.5 us)
Async XLA Ops:
  0.6 10.4 %copy-start = (f32[1,2,256,128]{3,2,1,0:T(8,128)S(1)}, f32[1,2,256,128]{3,2,1,0:T(8,128)}, u32[]{:S(2)}) copy-start(f32[1,2,256,128]{3,2,1,0:T(8,128)} %param.8) | copy-start | bytes 786436
  0.6 6.7 %copy-start.5 = (f32[64]{0:T(128)S(1)}, f32[64]{0:T(128)}, u32[]{:S(2)}) copy-start(f32[64]{0:T(128)} %param.11) | copy-start | bytes 772
  0.7 6.7 %copy-start.6 = (f32[64]{0:T(128)S(1)}, f32[64]{0:T(128)}, u32[]{:S(2)}) copy-start(f32[64]{0:T(128)} %param.13) | copy-start | bytes 772
  0.7 6.7 %copy-start.1 = (bf16[64,64]{1,0:T(8,128)(2,1)S(1)}, bf16[64,64]{1,0:T(8,128)(2,1)}, u32[]{:S(2)}) copy-start(bf16[64,64]{1,0:T(8,128)(2,1)} %w2b.3) | copy-start | bytes 24580
  0.7 7.4 %copy-start.3 = (bf16[3,3,2,64]{3,2,1,0:T(2,128)(2,1)S(1)}, bf16[3,3,2,64]{3,2,1,0:T(2,128)(2,1)}, u32[]{:S(2)}) copy-start(bf16[3,3,2,64]{3,2,1,0:T(2,128)(2,1)} %param.10) | copy-start | bytes 6916
  3.3 6.3 %collective-permute-start = (f32[4,32,128]{2,1,0:T(8,128)S(1)}, f32[4,32,128]{2,1,0:T(8,128)S(1)}, u32[]{:S(2)}, u32[]{:S(2)}) collective-permute-start(f32[4,32,128]{2,1,0:T(8,128)S(1)} %get-tuple-element.45), channel_id=1, source_target_pairs={{0,4},{4,8},{8,12},{12,0},{1,5},{5,9},{9,13},{13,1},{2,6},{6,10},{... | collective-permute-start | bytes 196616 | tf_op jit(solution)/shard_map/ppermute | solution.py:34
  6.3 4.7 %collective-permute-start.1 = (f32[4,32,128]{2,1,0:T(8,128)S(1)}, f32[4,32,128]{2,1,0:T(8,128)S(1)}, u32[]{:S(2)}, u32[]{:S(2)}) collective-permute-start(f32[4,32,128]{2,1,0:T(8,128)S(1)} %get-tuple-element.46), channel_id=1, source_target_pairs={{0,12},{4,0},{8,4},{12,8},{1,13},{5,1},{9,5},{13,9},{2,14},{6,2},{... | collective-permute-start | bytes 196616 | tf_op jit(solution)/shard_map/ppermute | solution.py:34
  11.3 7.1 %copy-start.2 = (bf16[3,3,64,6]{2,3,1,0:T(8,128)(2,1)S(1)}, bf16[3,3,64,6]{2,3,1,0:T(8,128)(2,1)}, u32[]{:S(2)}) copy-start(bf16[3,3,64,6]{2,3,1,0:T(8,128)(2,1)} %param.14) | copy-start | bytes 20740
  11.5 9.7 %collective-permute-start.2 = (f32[4,32,320]{2,1,0:T(8,128)S(1)}, f32[4,32,320]{2,1,0:T(8,128)S(1)}, u32[]{:S(2)}, u32[]{:S(2)}) collective-permute-start(f32[4,32,320]{2,1,0:T(8,128)S(1)} %copy.38), channel_id=1, source_target_pairs={{0,1},{1,2},{2,3},{3,0},{4,5},{5,6},{6,7},{7,4},{8,9},{9,10},{10,1... | collective-permute-start | bytes 491528 | tf_op jit(solution)/shard_map/ppermute | solution.py:34
  13.4 9.7 %collective-permute-start.3 = (f32[4,32,320]{2,1,0:T(8,128)S(1)}, f32[4,32,320]{2,1,0:T(8,128)S(1)}, u32[]{:S(2)}, u32[]{:S(2)}) collective-permute-start(f32[4,32,320]{2,1,0:T(8,128)S(1)} %copy.40), channel_id=1, source_target_pairs={{0,3},{1,0},{2,1},{3,2},{4,7},{5,4},{6,5},{7,6},{8,11},{9,8},{10,9... | collective-permute-start | bytes 491528 | tf_op jit(solution)/shard_map/ppermute | solution.py:34
  53.2 32.6 %copy-start.4 = (f32[1,128]{1,0:T(1,128)S(1)}, f32[1,128]{1,0:T(1,128)}, u32[]{:S(2)}) copy-start(f32[1,128]{1,0:T(1,128)} %get-tuple-element.26) | copy-start | bytes 1540
  74.4 5.1 %collective-permute-start.4 = (f32[2,40,128]{2,1,0:T(8,128)S(1)}, f32[2,40,128]{2,1,0:T(8,128)S(1)}, u32[]{:S(2)}, u32[]{:S(2)}) collective-permute-start(f32[2,40,128]{2,1,0:T(8,128)S(1)} %get-tuple-element.54), channel_id=1, source_target_pairs={{0,4},{4,8},{8,12},{12,0},{1,5},{5,9},{9,13},{13,1},{2,6},{6,10},{... | collective-permute-start | bytes 122888 | tf_op jit(solution)/shard_map/ppermute | solution.py:34
  77.2 4.0 %collective-permute-start.5 = (f32[2,40,128]{2,1,0:T(8,128)S(1)}, f32[2,40,128]{2,1,0:T(8,128)S(1)}, u32[]{:S(2)}, u32[]{:S(2)}) collective-permute-start(f32[2,40,128]{2,1,0:T(8,128)S(1)} %get-tuple-element.53), channel_id=1, source_target_pairs={{0,12},{4,0},{8,4},{12,8},{1,13},{5,1},{9,5},{13,9},{2,14},{6,2},{... | collective-permute-start | bytes 122888 | tf_op jit(solution)/shard_map/ppermute | solution.py:34
  81.4 12.9 %collective-permute-start.6 = (f32[2,40,336]{1,2,0:T(8,128)S(1)}, f32[2,40,336]{1,2,0:T(8,128)S(1)}, u32[]{:S(2)}, u32[]{:S(2)}) collective-permute-start(f32[2,40,336]{1,2,0:T(8,128)S(1)} %get-tuple-element.47), channel_id=1, source_target_pairs={{0,1},{1,2},{2,3},{3,0},{4,5},{5,6},{6,7},{7,4},{8,9},{9,10},{10,1... | collective-permute-start | bytes 322568 | tf_op jit(solution)/shard_map/ppermute | solution.py:34
  82.3 15.5 %collective-permute-start.7 = (f32[2,40,336]{1,2,0:T(8,128)S(1)}, f32[2,40,336]{1,2,0:T(8,128)S(1)}, u32[]{:S(2)}, u32[]{:S(2)}) collective-permute-start(f32[2,40,336]{1,2,0:T(8,128)S(1)} %get-tuple-element.48), channel_id=1, source_target_pairs={{0,3},{1,0},{2,1},{3,2},{4,7},{5,4},{6,5},{7,6},{8,11},{9,8},{10,9... | collective-permute-start | bytes 322568 | tf_op jit(solution)/shard_map/ppermute | solution.py:34
  140.2 4.7 %collective-permute-start.8 = (f32[2,24,128]{2,1,0:T(8,128)S(1)}, f32[2,24,128]{2,1,0:T(8,128)S(1)}, u32[]{:S(2)}, u32[]{:S(2)}) collective-permute-start(f32[2,24,128]{2,1,0:T(8,128)S(1)} %get-tuple-element.52), channel_id=1, source_target_pairs={{0,4},{4,8},{8,12},{12,0},{1,5},{5,9},{9,13},{13,1},{2,6},{6,10},{... | collective-permute-start | bytes 73736 | tf_op jit(solution)/shard_map/ppermute | solution.py:34
  142.1 3.9 %collective-permute-start.9 = (f32[2,24,128]{2,1,0:T(8,128)S(1)}, f32[2,24,128]{2,1,0:T(8,128)S(1)}, u32[]{:S(2)}, u32[]{:S(2)}) collective-permute-start(f32[2,24,128]{2,1,0:T(8,128)S(1)} %get-tuple-element.51), channel_id=1, source_target_pairs={{0,12},{4,0},{8,4},{12,8},{1,13},{5,1},{9,5},{13,9},{2,14},{6,2},{... | collective-permute-start | bytes 73736 | tf_op jit(solution)/shard_map/ppermute | solution.py:34
  146.1 12.1 %collective-permute-start.10 = (f32[2,24,304]{1,2,0:T(8,128)S(1)}, f32[2,24,304]{1,2,0:T(8,128)S(1)}, u32[]{:S(2)}, u32[]{:S(2)}) collective-permute-start(f32[2,24,304]{1,2,0:T(8,128)S(1)} %get-tuple-element.49), channel_id=1, source_target_pairs={{0,1},{1,2},{2,3},{3,0},{4,5},{5,6},{6,7},{7,4},{8,9},{9,10},{10,1... | collective-permute-start | bytes 175112 | tf_op jit(solution)/shard_map/ppermute | solution.py:34
  146.7 13.3 %collective-permute-start.11 = (f32[2,24,304]{1,2,0:T(8,128)S(1)}, f32[2,24,304]{1,2,0:T(8,128)S(1)}, u32[]{:S(2)}, u32[]{:S(2)}) collective-permute-start(f32[2,24,304]{1,2,0:T(8,128)S(1)} %get-tuple-element.50), channel_id=1, source_target_pairs={{0,3},{1,0},{2,1},{3,2},{4,7},{5,4},{6,5},{7,6},{8,11},{9,8},{10,9... | collective-permute-start | bytes 175112 | tf_op jit(solution)/shard_map/ppermute | solution.py:34
  197.2 1.5 collective-permute-start.12
  199.5 5.3 %collective-permute-start.13 = (f32[112,128]{1,0:T(8,128)S(1)}, f32[112,128]{1,0:T(8,128)S(1)}, u32[]{:S(2)}, u32[]{:S(2)}) collective-permute-start(f32[112,128]{1,0:T(8,128)S(1)} %add.60), channel_id=1, source_target_pairs={{0,4},{4,8},{8,12},{12,0},{1,5},{5,9},{9,13},{13,1},{2,6},{6,10},{... | collective-permute-start | bytes 172040 | tf_op jit(solution)/shard_map/ppermute | solution.py:34
  200.7 4.8 %collective-permute-start.14 = (f32[112,128]{1,0:T(8,128)S(1)}, f32[112,128]{1,0:T(8,128)S(1)}, u32[]{:S(2)}, u32[]{:S(2)}) collective-permute-start(f32[112,128]{1,0:T(8,128)S(1)} %add.60), channel_id=1, source_target_pairs={{0,8},{4,12},{8,0},{12,4},{1,9},{5,13},{9,1},{13,5},{2,10},{6,14},... | collective-permute-start | bytes 172040 | tf_op jit(solution)/shard_map/ppermute | solution.py:34
  201.6 4.2 %collective-permute-start.15 = (f32[112,128]{1,0:T(8,128)S(1)}, f32[112,128]{1,0:T(8,128)S(1)}, u32[]{:S(2)}, u32[]{:S(2)}) collective-permute-start(f32[112,128]{1,0:T(8,128)S(1)} %add.60), channel_id=1, source_target_pairs={{0,12},{4,0},{8,4},{12,8},{1,13},{5,1},{9,5},{13,9},{2,14},{6,2},{... | collective-permute-start | bytes 172040 | tf_op jit(solution)/shard_map/ppermute | solution.py:34
  205.8 6.7 %collective-permute-start.16 = (f32[112,128]{1,0:T(8,128)S(1)}, f32[112,128]{1,0:T(8,128)S(1)}, u32[]{:S(2)}, u32[]{:S(2)}) collective-permute-start(f32[112,128]{1,0:T(8,128)S(1)} %add_add_fusion.1), channel_id=1, source_target_pairs={{0,1},{1,2},{2,3},{3,0},{4,5},{5,6},{6,7},{7,4},{8,9},{9,10},{10,1... | collective-permute-start | bytes 172040 | tf_op jit(solution)/shard_map/ppermute | solution.py:34
  206.6 7.3 %collective-permute-start.17 = (f32[112,128]{1,0:T(8,128)S(1)}, f32[112,128]{1,0:T(8,128)S(1)}, u32[]{:S(2)}, u32[]{:S(2)}) collective-permute-start(f32[112,128]{1,0:T(8,128)S(1)} %add_add_fusion.1), channel_id=1, source_target_pairs={{0,2},{1,3},{2,0},{3,1},{4,6},{5,7},{6,4},{7,5},{8,10},{9,11},{10,... | collective-permute-start | bytes 172040 | tf_op jit(solution)/shard_map/ppermute | solution.py:34
  208.5 5.4 %collective-permute-start.18 = (f32[112,128]{1,0:T(8,128)S(1)}, f32[112,128]{1,0:T(8,128)S(1)}, u32[]{:S(2)}, u32[]{:S(2)}) collective-permute-start(f32[112,128]{1,0:T(8,128)S(1)} %add_add_fusion.1), channel_id=1, source_target_pairs={{0,3},{1,0},{2,1},{3,2},{4,7},{5,4},{6,5},{7,6},{8,11},{9,8},{10,9... | collective-permute-start | bytes 172040 | tf_op jit(solution)/shard_map/ppermute | solution.py:34

commit v3 on v2

--- a/solution.py
+++ b/solution.py
@@ -34,14 +34,49 @@
     return lax.ppermute(block, axis, route)
 
 
-def exchange(own, rim):
-    before = passed_along(own[:, -rim:], "gx", 1)
-    after = passed_along(own[:, :rim], "gx", -1)
-    tall = jnp.concatenate([before, own, after], axis=1)
-    left = passed_along(jnp.swapaxes(tall[:, :, -rim:], 1, 2), "gy", 1)
-    right = passed_along(jnp.swapaxes(tall[:, :, :rim], 1, 2), "gy", -1)
-    wide = jnp.concatenate([jnp.swapaxes(left, 1, 2), tall, jnp.swapaxes(right, 1, 2)], axis=2)
-    return jnp.pad(wide, ((0, 0), (TOP - rim, TOP - rim), (LEFT - rim, LEFT - rim)))
+def exchange(owns, sides):
+    rim, rows = sides[0].shape[1:]
+    right = passed_along(sides[0], "gy", -1)
+    left = passed_along(sides[1], "gy", 1)
+    edges = []
+    for first, tile, distance in ((rows - rim, rows - 128, 1), (0, 0, -1)):
+        mine = jnp.concatenate([own[:, first : first + rim] for own in owns], axis=0)
+        parts = [mine] + [part[:, :, tile : tile + 128] for part in (left, right)]
+        edges.append(passed_along(jnp.concatenate(parts, axis=1), "gx", distance))
+    return [left, right] + edges
+
+
+def side_strips(field, rim):
+    turned = field.T
+    return turned[:rim], turned[turned.shape[0] - rim :]
+
+
+def spread_out(middle, left, right, rows):
+    rim = left.shape[0]
+    lanes = left.shape[1]
+    before = jnp.concatenate([jnp.zeros((LEFT - rim, lanes), F32), left, jnp.zeros((128 - LEFT, lanes), F32)], axis=0).T
+    after = jnp.concatenate([jnp.zeros((LEFT, lanes), F32), right, jnp.zeros((128 - LEFT - rim, lanes), F32)], axis=0).T
+    turned = pltpu.roll(middle, LEFT, 1)
+    first_half = lax.broadcasted_iota(jnp.int32, middle.shape, 1) < LEFT
+    return jnp.concatenate(
+        [jnp.where(first_half, before[rows], turned), jnp.where(first_half, turned, after[rows])], axis=1
+    )
+
+
+def build_frame(own, pieces, comp, target_ref, target):
+    left_ref, right_ref, above_ref, below_ref = pieces
+    rim = left_ref.shape[1]
+    rows = own.shape[0]
+    if rim < TOP:
+        target_ref[target, : TOP - rim] = jnp.zeros((TOP - rim, 256), F32)
+        target_ref[target, TOP + rows + rim :] = jnp.zeros((TOP - rim, 256), F32)
+    target_ref[target, TOP : TOP + rows] = spread_out(
+        own, left_ref[comp], right_ref[comp], slice(0, rows)
+    )
+    for ref, first, kept in ((above_ref, TOP - rim, slice(128 - rim, 128)), (below_ref, TOP + rows, slice(0, rim))):
+        target_ref[target, first : first + rim] = spread_out(
+            ref[comp, :rim], ref[comp, rim : 2 * rim], ref[comp, 2 * rim :], kept
+        )
 
 
 def total_over(value, axis):
@@ -291,16 +326,17 @@
     lax.fori_loop(0, plan.chunks, one_chunk, 0)
 
 
-def network_back(plan, inputs_ref, taps_ref, weight_refs, place_ref, grads_ref, sums_ref, window_ref, terms_ref):
+def network_back(plan, inputs_ref, taps_ref, weight_refs, place_ref, grads_ref, sums_ref, cross_ref, window_ref, terms_ref):
     w1_ref, b1_ref, w2_ref, b2_ref, w1b_ref, w2b_ref, w3b_ref = weight_refs
     terms_ref[...] = jnp.zeros_like(terms_ref)
+    cross_ref[...] = jnp.zeros_like(cross_ref)
 
     def one_chunk(step, carried):
         row = place_ref[...] + CHUNK_ROWS * step
         own = jnp.where((row >= plan.rim + 1) & (row < plan.rim + 1 + plan.rows), 1.0, 0.0)
         mask = own.astype(BF16)
-        cols = columns(plan, step, inputs_ref, window_ref)
-        half = product(w1_ref[...], cols.astype(BF16)) + b1_ref[...]
+        cols = columns(plan, step, inputs_ref, window_ref).astype(BF16)
+        half = product(w1_ref[...], cols) + b1_ref[...]
         bend = jnp.tanh(half)
         hidden_one = (half * bend + half).astype(BF16)
         slope_one = (0.5 + 0.5 * bend) * (1.0 + half * (1.0 - bend))
@@ -314,10 +350,9 @@
         spread = jnp.concatenate(parts + [jnp.zeros((8, plan.chunk), F32)], axis=0).astype(BF16)
         grad_two = (product(w3b_ref[...], spread) * slope_two).astype(BF16)
         grad_one = (product(w2b_ref[...], grad_two) * slope_one).astype(BF16)
-        sums_ref[:80, :64] += product_over_cells(spread, hidden_two * mask)
-        sums_ref[:64, 64:] += product_over_cells(hidden_one, grad_two * mask)
-        both = jnp.concatenate([grad_one, grad_two], axis=0)
-        sums_ref[80:, :] += product_over_cells((cols * own).astype(BF16), both)
+        left = jnp.concatenate([spread, hidden_one, cols], axis=0)
+        right = jnp.concatenate([hidden_two * mask, grad_two * mask, grad_one * mask], axis=0)
+        cross_ref[...] += product_over_cells(left, right)
         terms_ref[:, :LEAD] = terms_ref[:, plan.chunk :]
         terms_ref[:, LEAD:] = product(w1b_ref[...], grad_one)
         total = add_taps(terms_ref, [LEAD - offset for offset in plan.offsets], plan.chunk)
@@ -325,6 +360,13 @@
         return carried
 
     lax.fori_loop(0, plan.chunks, one_chunk, 0)
+    for tap in range(9):
+        taken = 144 + 8 * (tap // 3) + 2 * (tap % 3)
+        sums_ref[8 * tap : 8 * tap + 6, :64] += cross_ref[8 * tap : 8 * tap + 6, :64]
+        sums_ref[8 * tap + 6 : 8 * tap + 8, :64] += cross_ref[taken : taken + 2, 128:192]
+    sums_ref[:64, 64:] += cross_ref[80:144, 64:128]
+    sums_ref[64:65, 64:] += cross_ref[150:151, 128:192]
+    sums_ref[65:66, 64:] += cross_ref[150:151, 64:128]
 
 
 def own_part(field, rows, cols, first_row):
@@ -335,8 +377,39 @@
     return jnp.sum(squares, axis=0, keepdims=True)
 
 
-def first_kernel(plan, v_ref, goal_ref, force_ref, w1, b1, w2, b2, w3, v_out, coefs_ref, error_ref, loss_ref,
-                 inputs_ref, window_ref, terms_ref, frame_ref, buffers, rhs_ref):
+def strips_kernel(v_ref, goals_ref, low_ref, high_ref):
+    rim = low_ref.shape[1]
+    for number in range(4):
+        field = v_ref[number] if number < 2 else goals_ref[goals_ref.shape[0] - 1, number - 2]
+        low_ref[number], high_ref[number] = side_strips(field, rim)
+
+
+def weights_kernel(w1_in, b1_in, w2_in, b2_in, w3_in, w1, b1, w2, b2, w3, w1b, w3b):
+    hid = b1_in.shape[1]
+    ahead, wide, back = [], [], []
+    for row in range(3):
+        parts = [w1_in[row, col].astype(F32) for col in range(3)]
+        ahead += parts + [jnp.zeros((2, hid), F32)]
+        for col in range(3):
+            wide += [parts[col], jnp.zeros((6, hid), F32)]
+            back += [w3_in[row, col].astype(F32), jnp.zeros((2, hid), F32)]
+    ahead = jnp.concatenate(ahead + [jnp.zeros((8, hid), F32)], axis=0)
+    back = jnp.concatenate(back, axis=0)
+    w1[...] = (0.5 * ahead).T.astype(BF16)
+    w1b[...] = jnp.concatenate(wide, axis=0).astype(BF16)
+    w2[...] = (0.5 * w2_in[...].astype(F32)).T.astype(BF16)
+    w3[...] = back.astype(BF16)
+    w3b[...] = jnp.concatenate([back, jnp.zeros((8, hid), F32)], axis=0).T.astype(BF16)
+    for source, target in ((b1_in, b1), (b2_in, b2)):
+        target[...] = jnp.broadcast_to(0.5 * source[...], (8, hid)).T[:, :1]
+
+
+def first_kernel(plan, left, right, above, below, own_ref, goals_ref, force_ref, w1, b1, w2, b2, w3,
+                 v_ref, last_goal_ref, v_out, coefs_ref, error_ref, loss_ref, inputs_ref, window_ref, terms_ref, frame_ref, buffers, rhs_ref):
+    pieces = (left, right, above, below)
+    for comp in range(2):
+        build_frame(own_ref[comp], pieces, comp, v_ref, comp)
+        build_frame(goals_ref[goals_ref.shape[0] - 1, comp], pieces, comp + 2, last_goal_ref, comp)
     keep_inputs([v_ref[0], v_ref[1]], inputs_ref)
     coefs_ref[...] = jnp.zeros_like(coefs_ref)
     network(plan, inputs_ref, (w1, b1, w2, b2, w3), coefs_ref, window_ref, terms_ref)
@@ -350,14 +423,14 @@
     loss = None
     for comp in range(2):
         v_out[comp] = result[comp]
-        error = own_part(result[comp], plan.rows, plan.cols, 0) - goal_ref[comp]
+        error = own_part(result[comp], plan.rows, plan.cols, 0) - goals_ref[0, comp]
         error_ref[comp] = error
         square = lane_sums(error * error)
         loss = square if loss is None else loss + square
-    loss_ref[...] = loss
-
-
-def second_kernel(plan, v_ref, force_ref, w1, b1, w2, b2, w3, out_ref, coefs_ref, inputs_ref, window_ref, terms_ref):
+    loss_ref[...] = loss[:, :64] + loss[:, 64:]
+
+
+def second_kernel(plan, v_ref, force_ref, w1, b1, w2, b2, w3, out_ref, low_ref, high_ref, coefs_ref, inputs_ref, window_ref, terms_ref):
     keep_inputs([v_ref[0], v_ref[1]], inputs_ref)
     coefs_ref[...] = jnp.zeros_like(coefs_ref)
     network(plan, inputs_ref, (w1, b1, w2, b2, w3), coefs_ref, window_ref, terms_ref)
@@ -365,20 +438,24 @@
     v = [v_ref[comp, low : low + tall] for comp in range(2)]
     result = advect(v, [channel(coefs_ref, number, low, tall) for number in range(6)], force_ref[...])
     for comp in range(2):
-        out_ref[comp] = own_part(result[comp], plan.rows, plan.cols, low)
-
-
-def back_kernel(plan, last, in_ref, goal_ref, extra_ref, before_ref, v_ref, coefs_ref, place_ref,
-                w1, b1, w2, b2, w1b, w2b, w3b, out_ref, sums_ref,
-                inputs_ref, taps_ref, grads_ref, window_ref, terms_ref, frame_ref, buffers, rhs_ref):
+        mine = own_part(result[comp], plan.rows, plan.cols, low)
+        out_ref[comp] = mine
+        low_ref[comp], high_ref[comp] = side_strips(mine, low_ref.shape[1])
+
+
+def back_kernel(plan, last, left, right, above, below, own_ref, goal_ref, extra_ref, before_ref, v_ref, coefs_ref,
+                place_ref, w1, b1, w2, b2, w1b, w2b, w3b, out_ref, low_ref, high_ref, sums_ref, inputs_ref, taps_ref, grads_ref, cross_ref, window_ref, terms_ref, frame_ref, buffers, rhs_ref):
     rows, cols = plan.rows, plan.cols
     sums_ref[...] = before_ref[...]
-    first, second = project(in_ref[0], in_ref[1], buffers, rhs_ref, TOP if last else 24)
+    for comp in range(2):
+        build_frame(own_ref[comp], (left, right, above, below), comp, frame_ref, comp)
+    first, second = project(frame_ref[0], frame_ref[1], buffers, rhs_ref, TOP if last else 24)
     if last:
         errors = (first - goal_ref[0], second - goal_ref[1])
         for error in errors:
             mine = own_part(error, rows, cols, 0)
-            sums_ref[111:112, :] += lane_sums(mine * mine)
+            loss = lane_sums(mine * mine)
+            sums_ref[66:67, 64:] += loss[:, :64] + loss[:, 64:]
         for comp in range(2):
             frame_ref[comp] = errors[comp]
         first, second = project(frame_ref[0], frame_ref[1], buffers, rhs_ref, 24)
@@ -396,11 +473,17 @@
     for comp in range(2):
         frame_ref[comp, low : low + tall] = result[comp]
     weight_refs = (w1, b1, w2, b2, w1b, w2b, w3b)
-    network_back(plan, inputs_ref, taps_ref, weight_refs, place_ref, grads_ref, sums_ref, window_ref, terms_ref)
+    network_back(plan, inputs_ref, taps_ref, weight_refs, place_ref, grads_ref, sums_ref, cross_ref, window_ref, terms_ref)
     for comp in range(2):
         field = frame_ref[comp, low : low + tall] + channel(grads_ref, comp, low, tall)
         total = own_part(field, rows, cols, low)
-        out_ref[comp] = total + extra_ref[comp] if last else total
+        if last:
+            total = total + extra_ref[comp]
+            low_ref[comp], high_ref[comp] = side_strips(total, low_ref.shape[1])
+        out_ref[comp] = total
+    if not last:
+        low_ref[...] = jnp.zeros_like(low_ref)
+        high_ref[...] = jnp.zeros_like(high_ref)
 
 
 def scaled(piece, count):
@@ -408,13 +491,14 @@
 
 
 def finish_kernel(loss_scale, in_ref, w1_ref, b1_ref, w2_ref, b2_ref, w3_ref, loss_ref):
-    one = jnp.concatenate([in_ref[80 + 8 * row : 86 + 8 * row, :64] for row in range(3)], axis=0)
+    one = jnp.concatenate([in_ref[8 * tap + 6 : 8 * tap + 8, :64] for tap in range(9)], axis=0)
+    three = jnp.concatenate([in_ref[8 * tap : 8 * tap + 6, :64] for tap in range(9)], axis=0)
     w1_ref[...] = scaled(one, one.size)
-    b1_ref[...] = scaled(in_ref[86:87, :64], 64)
-    b2_ref[...] = scaled(in_ref[86:87, 64:], 64)
+    b1_ref[...] = scaled(in_ref[64:65, 64:], 64)
+    b2_ref[...] = scaled(in_ref[65:66, 64:], 64)
     w2_ref[...] = scaled(in_ref[:64, 64:], 64 * 64)
-    w3_ref[...] = scaled(in_ref[:72, :64], 54 * 64)
-    loss_ref[...] = (0.5 * loss_scale) * jnp.sum(in_ref[111:112, :], axis=1, keepdims=True)
+    w3_ref[...] = scaled(three, three.size)
+    loss_ref[...] = (0.5 * loss_scale) * jnp.sum(in_ref[66:67, 64:], axis=1, keepdims=True)
 
 
 def shards(velocity, targets, weight_one, bias_one, weight_two, bias_two, weight_three):
@@ -425,16 +509,16 @@
     pair = (2,) + frame
     own_pair = (2, rows, cols)
     packed = (2, 8 * height, 128)
-    sums_shape = (112, 128)
+    sums_shape = (72, 128)
     hid = weight_two.shape[0]
     nout = weight_three.shape[3]
     near = Plan(rows, cols, 2)
     far = Plan(rows, cols, 23)
 
-    def call(kernel, outs, scratch, *args):
+    def call(kernel, outs, scratch, *args, kind=F32):
         return pl.pallas_call(
             kernel,
-            out_shape=[jax.ShapeDtypeStruct(shape, F32) for shape in outs],
+            out_shape=[jax.ShapeDtypeStruct(shape, F32 if shape[1] == 1 else kind) for shape in outs],
             scratch_shapes=[pltpu.VMEM(shape, F32) for shape in scratch],
             compiler_params=pltpu.CompilerParams(vmem_limit_bytes=60 << 20),
         )(*args)
@@ -444,17 +528,12 @@
 
     sweep_scratch = [pair, (2, 2, height + 2 * GUARD, 128), (2, height, 128)]
 
-    w1 = jnp.pad(weight_one.reshape(3, 6, hid), ((0, 1), (0, 2), (0, 0))).reshape(32, hid)
-    w1_half = (0.5 * w1.astype(F32)).astype(BF16).T
-    w2_half = (0.5 * weight_two.astype(F32)).astype(BF16).T
-    b1_half = 0.5 * bias_one[:, None]
-    b2_half = 0.5 * bias_two[:, None]
-    w3 = jnp.pad(weight_three.reshape(9, hid, nout), ((0, 0), (0, 0), (0, 8 - nout)))
-    w3_out = jnp.transpose(w3, (0, 2, 1)).reshape(72, hid)
-    w3_back = jnp.pad(jnp.transpose(w3, (1, 0, 2)).reshape(hid, 72), ((0, 0), (0, 8)))
-    w1_back = jnp.pad(weight_one.reshape(9, 2, hid), ((0, 0), (0, 6), (0, 0))).reshape(72, hid)
-    forward_weights = (w1_half, b1_half, w2_half, b2_half, w3_out)
-    backward_weights = (w1_half, b1_half, w2_half, b2_half, w1_back, weight_two, w3_back)
+    w1, b1, w2, b2, w3, w1b, w3b = call(
+        weights_kernel, [(hid, 32), (hid, 1), (hid, hid), (hid, 1), (72, hid), (72, hid), (hid, 80)], [],
+        weight_one, bias_one[None, :], weight_two, bias_two[None, :], jnp.swapaxes(weight_three, 2, 3), kind=BF16,
+    )
+    forward_weights = (w1, b1, w2, b2, w3)
+    backward_weights = (w1, b1, w2, b2, w1b, weight_two, w3b)
 
     lane = np.arange(near.chunk)
     place_row, place_col = lane // near.wide, lane % near.wide
@@ -465,31 +544,35 @@
     col_ids = lax.axis_index("gy") * cols + jnp.arange(frame[1], dtype=jnp.int32) - LEFT
     forcing = jnp.sin(col_ids.astype(F32) * (TWO_PI * FORCE_WAVES / total_cols))[None, :]
 
-    both = exchange(jnp.concatenate([velocity[0], targets[0, step_count - 1]], axis=0), 32)
-    v_first = both[:2]
-    v_second, coefs_first, error_first, loss_first = call(
+    def strips(count, rim):
+        return [(count, rim, rows)] * 2
+
+    sides = call(strips_kernel, strips(4, 32), [], velocity[0], targets[0])
+    pieces = exchange([velocity[0], targets[0, step_count - 1]], sides)
+    v_first, last_goal, v_second, coefs_first, error_first, loss_first = call(
         functools.partial(first_kernel, far),
-        [pair, packed, own_pair, (1, cols)],
+        [pair, pair, pair, packed, own_pair, (1, 64)],
         [packed] + net_scratch(far) + sweep_scratch,
-        v_first, targets[0, 0], forcing, *forward_weights,
-    )
-    provisional, coefs_second = call(
+        *pieces, velocity[0], targets[0], forcing, *forward_weights,
+    )
+    provisional, low, high, coefs_second = call(
         functools.partial(second_kernel, near),
-        [own_pair, packed],
+        [own_pair] + strips(2, 40) + [packed],
         [packed] + net_scratch(near),
         v_second, forcing, *forward_weights,
     )
-    back_scratch = [packed, packed, packed] + net_scratch(near) + sweep_scratch
-    start_sums = jnp.pad(loss_first, ((111, 0), (0, 128 - cols)))
-    framed = exchange(provisional, 40)
-    grad, sums = call(
-        functools.partial(back_kernel, near, True), [own_pair, sums_shape], back_scratch,
-        framed, both[2:], error_first, start_sums, v_second, coefs_second, place, *backward_weights,
-    )
-    framed = exchange(grad, 24)
-    grad, sums = call(
-        functools.partial(back_kernel, near, False), [own_pair, sums_shape], back_scratch,
-        framed, forcing, forcing, sums, v_first, coefs_first, place, *backward_weights,
+    back_scratch = [packed, packed, packed, (176, 192)] + net_scratch(near) + sweep_scratch
+    start_sums = jnp.pad(loss_first, ((66, 5), (64, 0)))
+    grad, low, high, sums = call(
+        functools.partial(back_kernel, near, True),
+        [own_pair] + strips(2, 24) + [sums_shape], back_scratch,
+        *exchange([provisional], (low, high)), provisional, last_goal, error_first, start_sums, v_second, coefs_second, place,
+        *backward_weights,
+    )
+    grad, _, _, sums = call(
+        functools.partial(back_kernel, near, False),
+        [own_pair] + [(1, 8, 128)] * 2 + [sums_shape], back_scratch,
+        *exchange([grad], (low, high)), grad, forcing, forcing, sums, v_first, coefs_first, place, *backward_weights,
     )
     for axis in ("ens", "gx", "gy"):
         sums = total_over(sums, axis)
@@ -497,14 +580,14 @@
     loss_scale = 1.0 / float(step_count * 2 * rows * cols * device_count)
     d1, db1, d2, db2, d3, loss = call(
         functools.partial(finish_kernel, loss_scale),
-        [(18, hid), (1, hid), (hid, hid), (1, hid), (72, hid), (1, 1)], [], sums,
+        [(18, hid), (1, hid), (hid, hid), (1, hid), (54, hid), (1, 1)], [], sums,
     )
     return (
         d1.reshape(weight_one.shape),
         db1[0],
         d2,
         db2[0],
-        d3.reshape(9, 8, hid)[:, :nout].transpose(0, 2, 1).reshape(weight_three.shape),
+        d3.reshape(3, 3, nout, hid).transpose(0, 1, 3, 2),
         loss[0, 0],
         grad[None],
     )

time: 218 us -> 202 us (0.927)
  waiting for transfers between devices: 38.9 us -> 31.4 us
  other arithmetic: 7.22 us -> 2.12 us
  local copies, waits for them, and re-layouts: 14.1 us -> 9.34 us
    ppermute x19, waiting for transfers between devices: 38.9 us -> 31.4 us  [passed_along(): return lax.ppermute(block, axis, route)]
    concatenate x4 -> x6, other arithmetic: 3.71 us -> 0.06 us  [exchange(): edges.append(passed_along(jnp.concatenate(parts, axis=1), 'gx', distance))]
    pallas_call x5 -> x7, Pallas kernels: 126 us -> 128 us  [call(): pl.pallas_call(kernel, out_shape=[jax.ShapeDtypeStruct(shape, F32 if shap...]
  transfers between devices with their start and end apart: 19 -> 19, of which waited for: 17 -> 19; matrix products, arithmetic and copies ran while one was open for 4% -> 3% of each run, Pallas kernels for 0% -> 1%
where the time goes in v3:
time: 202 us
  Pallas kernels  128 us (63%)
  waiting for transfers between devices  31.4 us (16%)
  starting transfers between devices  30.3 us (15%)
  local copies, waits for them, and re-layouts  9.34 us (5%)
  other arithmetic  2.12 us (1%)
    pallas_call x7, Pallas kernels, call(): pl.pallas_call(kernel, out_shape=[jax.ShapeDtypeStruct(shape, F32 if shap...  128 us
    ppermute x19, waiting for transfers between devices, passed_along(): return lax.ppermute(block, axis, route)  31.4 us
    ppermute x19, starting transfers between devices, passed_along(): return lax.ppermute(block, axis, route)  30.3 us
  transfers between devices with their start and end apart: 19, of which 19 were waited for; matrix products, arithmetic and copies ran while one was open for 3% of the time, Pallas kernels for 1%

profile of v3, /device:TPU:0, one launch (start us, length us, event | category | flops | bytes accessed | tf_op | source)
XLA Modules:
  0.0 201.5 jit_solution(4277955979345559969)
XLA Ops:
  0.6 2.0 shard_map.135
  2.6 3.0 %collective-permute-start = (f32[4,32,256]{2,1,0:T(8,128)}, f32[4,32,256]{2,1,0:T(8,128)S(1)}, u32[]{:S(2)}, u32[]{:S(2)}) collective-permute-start(f32[4,32,256]{2,1,0:T(8,128)} %get-tuple-element.38), channel_id=1, source_target_pairs={{0,1},{1,2},{2,3},{3,0},{4,5},{5,6},{6,7},{7,4},{8,9},{9,10},{10,1... | collective-permute-start | bytes 393224 | tf_op jit(solution)/shard_map/ppermute | solution.py:34
  5.7 2.0 %collective-permute-start.1 = (f32[4,32,256]{2,1,0:T(8,128)}, f32[4,32,256]{2,1,0:T(8,128)S(1)}, u32[]{:S(2)}, u32[]{:S(2)}) collective-permute-start(f32[4,32,256]{2,1,0:T(8,128)} %get-tuple-element.39), channel_id=1, source_target_pairs={{0,3},{1,0},{2,1},{3,2},{4,7},{5,4},{6,5},{7,6},{8,11},{9,8},{10,9... | collective-permute-start | bytes 393224 | tf_op jit(solution)/shard_map/ppermute | solution.py:34
  7.7 1.0 slice_bitcast_fusion
  8.7 0.8 fusion.2
  9.4 2.8 %collective-permute-done.left = f32[4,32,256]{2,1,0:T(8,128)S(1)} collective-permute-done((f32[4,32,256]{2,1,0:T(8,128)}, f32[4,32,256]{2,1,0:T(8,128)S(1)}, u32[]{:S(2)}, u32[]{:S(2)}) %collective-permute-start) | collective-permute-done | bytes 131104 | tf_op jit(solution)/shard_map/ppermute | solution.py:34
  12.2 1.4 collective-permute-done.1.right
  13.7 1.5 collective-permute-start.2
  15.2 1.5 collective-permute-start.3
  16.7 1.5 shard_map.136
  18.9 3.6 %collective-permute-done.2.above = f32[4,96,128]{2,1,0:T(8,128)S(1)} collective-permute-done((f32[4,96,128]{2,1,0:T(8,128)S(1)}, f32[4,96,128]{2,1,0:T(8,128)S(1)}, u32[]{:S(2)}, u32[]{:S(2)}) %collective-permute-start.2) | collective-permute-done | bytes 196640 | tf_op jit(solution)/shard_map/ppermute | solution.py:34
  22.5 2.6 %collective-permute-done.3.below = f32[4,96,128]{2,1,0:T(8,128)S(1)} collective-permute-done((f32[4,96,128]{2,1,0:T(8,128)S(1)}, f32[4,96,128]{2,1,0:T(8,128)S(1)}, u32[]{:S(2)}, u32[]{:S(2)}) %collective-permute-start.3) | collective-permute-done | bytes 196640 | tf_op jit(solution)/shard_map/ppermute | solution.py:34
  25.1 0.7 copy-done.7
  25.8 29.1 %shard_map.137 = (f32[2,336,256]{2,1,0:T(8,128)}, f32[2,336,256]{2,1,0:T(8,128)}, f32[2,336,256]{2,1,0:T(8,128)}, f32[2,2688,128]{2,1,0:T(8,128)}, f32[2,256,128]{2,1,0:T(8,128)}, /*index=5*/f32[1,64]{1,0:T(1,128)}) custom-call(f32[4,32,256]{2,1,0:T(8,128)} %copy-done, f32[4,32,256]{2,1,0:T(8,128)} %copy-done.1, f32[4,96,128]{2,1,0:T(8,128)} %copy-done.6, ...), custom_call_target="tpu_custom_call" | custom-call | tf_op jit(solution)/shard_map/pallas_call | solution.py:519
  54.8 20.0 %shard_map.138 = (f32[2,256,128]{2,1,0:T(8,128)}, f32[2,40,256]{2,1,0:T(8,128)}, f32[2,40,256]{2,1,0:T(8,128)}, f32[2,2688,128]{2,1,0:T(8,128)}) custom-call(f32[2,336,256]{2,1,0:T(8,128)} %get-tuple-element.45.v_ref, f32[1,256]{1,0:T(1,128)} %multiply_sine_fusion.force_ref.goal_ref.extra_ref, bf16[64,32]{1,0:T(8,128)(2,1)} %get-tuple-element.40.w1, ...), custom_call_target="tpu_custom_call" | custom-call | tf_op jit(solution)/shard_map/pallas_call | solution.py:519
  74.8 1.7 collective-permute-start.4
  76.5 0.8 fusion.1
  77.3 2.1 %collective-permute-start.5 = (f32[2,40,256]{2,1,0:T(8,128)}, f32[2,40,256]{2,1,0:T(8,128)S(1)}, u32[]{:S(2)}, u32[]{:S(2)}) collective-permute-start(f32[2,40,256]{2,1,0:T(8,128)} %get-tuple-element.47), channel_id=1, source_target_pairs={{0,3},{1,0},{2,1},{3,2},{4,7},{5,4},{6,5},{7,6},{8,11},{9,8},{10,9... | collective-permute-start | bytes 245768 | tf_op jit(solution)/shard_map/ppermute | solution.py:34
  79.4 1.9 collective-permute-done.4.left
  81.4 0.8 collective-permute-done.5.right
  82.2 1.5 collective-permute-start.6
  83.7 1.7 collective-permute-start.7
  85.5 1.3 pad.4.before_ref
  86.8 1.3 collective-permute-done.6.above
  88.1 0.8 collective-permute-done.7.below
  89.5 39.0 %shard_map.139 = (f32[2,256,128]{2,1,0:T(8,128)}, f32[2,24,256]{2,1,0:T(8,128)}, f32[2,24,256]{2,1,0:T(8,128)}, f32[72,128]{1,0:T(8,128)}) custom-call(f32[2,40,256]{2,1,0:T(8,128)} %copy-done.2, f32[2,40,256]{2,1,0:T(8,128)} %copy-done.3, f32[2,120,128]{2,1,0:T(8,128)} %copy-done.8, f32[2,120,128]{2,1,0:T(8,128)} %copy-done.9, ...), custom_call_target="tpu_custom_call" | custom-call | tf_op jit(solution)/shard_map/pallas_call | solution.py:519
  129.1 0.8 fusion
  129.8 3.3 %collective-permute-start.9 = (f32[2,24,256]{2,1,0:T(8,128)}, f32[2,24,256]{2,1,0:T(8,128)S(1)}, u32[]{:S(2)}, u32[]{:S(2)}) collective-permute-start(f32[2,24,256]{2,1,0:T(8,128)} %get-tuple-element.56), channel_id=1, source_target_pairs={{0,3},{1,0},{2,1},{3,2},{4,7},{5,4},{6,5},{7,6},{8,11},{9,8},{10,9... | collective-permute-start | bytes 147464 | tf_op jit(solution)/shard_map/ppermute | solution.py:34
  133.2 1.5 collective-permute-done.8.left
  135.2 1.5 collective-permute-start.10
  136.7 1.5 collective-permute-start.11
  138.2 2.3 %collective-permute-done.10.above = f32[2,72,128]{2,1,0:T(8,128)S(1)} collective-permute-done((f32[2,72,128]{2,1,0:T(8,128)S(1)}, f32[2,72,128]{2,1,0:T(8,128)S(1)}, u32[]{:S(2)}, u32[]{:S(2)}) %collective-permute-start.10) | collective-permute-done | bytes 73760 | tf_op jit(solution)/shard_map/ppermute | solution.py:34
  141.7 34.1 %shard_map.140 = (f32[2,256,128]{2,1,0:T(8,128)}, f32[1,8,128]{2,1,0:T(8,128)}, f32[1,8,128]{2,1,0:T(8,128)}, f32[72,128]{1,0:T(8,128)}) custom-call(f32[2,24,256]{2,1,0:T(8,128)} %copy-done.4, f32[2,24,256]{2,1,0:T(8,128)} %copy-done.5, f32[2,72,128]{2,1,0:T(8,128)} %copy-done.10, f32[2,72,128]{2,1,0:T(8,128)} %copy-done.11, ...), custom_call_target="tpu_custom_call" | custom-call | tf_op jit(solution)/shard_map/pallas_call | solution.py:519
  175.9 1.4 collective-permute-done.12
  177.3 0.8 add.46
  178.1 2.4 %collective-permute-start.15 = (f32[72,128]{1,0:T(8,128)S(1)}, f32[72,128]{1,0:T(8,128)S(1)}, u32[]{:S(2)}, u32[]{:S(2)}) collective-permute-start(f32[72,128]{1,0:T(8,128)S(1)} %add.46), channel_id=1, source_target_pairs={{0,12},{4,0},{8,4},{12,8},{1,13},{5,1},{9,5},{13,9},{2,14},{6,2},{... | collective-permute-start | bytes 110600 | tf_op jit(solution)/shard_map/ppermute | solution.py:34
  180.5 1.1 collective-permute-start.14
  181.6 0.7 collective-permute-done.15
  182.3 2.1 %collective-permute-done.14 = f32[72,128]{1,0:T(8,128)S(1)} collective-permute-done((f32[72,128]{1,0:T(8,128)S(1)}, f32[72,128]{1,0:T(8,128)S(1)}, u32[]{:S(2)}, u32[]{:S(2)}) %collective-permute-start.14) | collective-permute-done | bytes 36896 | tf_op jit(solution)/shard_map/ppermute | solution.py:34
  184.4 2.0 collective-permute-done.13
  186.4 4.1 %collective-permute-start.18 = (f32[72,128]{1,0:T(8,128)S(1)}, f32[72,128]{1,0:T(8,128)S(1)}, u32[]{:S(2)}, u32[]{:S(2)}) collective-permute-start(f32[72,128]{1,0:T(8,128)S(1)} %add_add_fusion.1), channel_id=1, source_target_pairs={{0,3},{1,0},{2,1},{3,2},{4,7},{5,4},{6,5},{7,6},{8,11},{9,8},{10,9... | collective-permute-start | bytes 110600 | tf_op jit(solution)/shard_map/ppermute | solution.py:34
  190.5 0.7 collective-permute-start.16
  191.2 1.0 collective-permute-done.18
  192.1 3.2 %collective-permute-done.17 = f32[72,128]{1,0:T(8,128)S(1)} collective-permute-done((f32[72,128]{1,0:T(8,128)S(1)}, f32[72,128]{1,0:T(8,128)S(1)}, u32[]{:S(2)}, u32[]{:S(2)}) %collective-permute-start.17) | collective-permute-done | bytes 36896 | tf_op jit(solution)/shard_map/ppermute | solution.py:34
  195.4 0.9 collective-permute-done.16
  196.9 2.0 shard_map.141
  198.9 1.3 reshape.39
  200.2 1.4 reshape.40
  (44 shorter events, 4.4 us)
Async XLA Ops:
  2.6 9.6 %collective-permute-start = (f32[4,32,256]{2,1,0:T(8,128)}, f32[4,32,256]{2,1,0:T(8,128)S(1)}, u32[]{:S(2)}, u32[]{:S(2)}) collective-permute-start(f32[4,32,256]{2,1,0:T(8,128)} %get-tuple-element.38), channel_id=1, source_target_pairs={{0,1},{1,2},{2,3},{3,0},{4,5},{5,6},{6,7},{7,4},{8,9},{9,10},{10,1... | collective-permute-start | bytes 393224 | tf_op jit(solution)/shard_map/ppermute | solution.py:34
  5.7 8.0 %collective-permute-start.1 = (f32[4,32,256]{2,1,0:T(8,128)}, f32[4,32,256]{2,1,0:T(8,128)S(1)}, u32[]{:S(2)}, u32[]{:S(2)}) collective-permute-start(f32[4,32,256]{2,1,0:T(8,128)} %get-tuple-element.39), channel_id=1, source_target_pairs={{0,3},{1,0},{2,1},{3,2},{4,7},{5,4},{6,5},{7,6},{8,11},{9,8},{10,9... | collective-permute-start | bytes 393224 | tf_op jit(solution)/shard_map/ppermute | solution.py:34
  12.2 12.9 %copy-start = (f32[4,32,256]{2,1,0:T(8,128)}, f32[4,32,256]{2,1,0:T(8,128)S(1)}, u32[]{:S(2)}) copy-start(f32[4,32,256]{2,1,0:T(8,128)S(1)} %collective-permute-done.left) | copy-start | bytes 393220
  13.6 11.5 %copy-start.1 = (f32[4,32,256]{2,1,0:T(8,128)}, f32[4,32,256]{2,1,0:T(8,128)S(1)}, u32[]{:S(2)}) copy-start(f32[4,32,256]{2,1,0:T(8,128)S(1)} %collective-permute-done.1.right) | copy-start | bytes 393220
  13.7 8.8 %collective-permute-start.2 = (f32[4,96,128]{2,1,0:T(8,128)S(1)}, f32[4,96,128]{2,1,0:T(8,128)S(1)}, u32[]{:S(2)}, u32[]{:S(2)}) collective-permute-start(f32[4,96,128]{2,1,0:T(8,128)S(1)} %pad_maximum_fusion), channel_id=1, source_target_pairs={{0,4},{4,8},{8,12},{12,0},{1,5},{5,9},{9,13},{13,1},{2,6},{6,10},{... | collective-permute-start | bytes 589832 | tf_op jit(solution)/shard_map/ppermute | solution.py:34
  15.2 9.9 %collective-permute-start.3 = (f32[4,96,128]{2,1,0:T(8,128)S(1)}, f32[4,96,128]{2,1,0:T(8,128)S(1)}, u32[]{:S(2)}, u32[]{:S(2)}) collective-permute-start(f32[4,96,128]{2,1,0:T(8,128)S(1)} %pad_maximum_fusion.1), channel_id=1, source_target_pairs={{0,12},{4,0},{8,4},{12,8},{1,13},{5,1},{9,5},{13,9},{2,14},{6,2},{... | collective-permute-start | bytes 589832 | tf_op jit(solution)/shard_map/ppermute | solution.py:34
  22.5 2.6 %copy-start.6 = (f32[4,96,128]{2,1,0:T(8,128)}, f32[4,96,128]{2,1,0:T(8,128)S(1)}, u32[]{:S(2)}) copy-start(f32[4,96,128]{2,1,0:T(8,128)S(1)} %collective-permute-done.2.above) | copy-start | bytes 589828
  25.1 0.7 copy-start.7
  74.8 6.5 %collective-permute-start.4 = (f32[2,40,256]{2,1,0:T(8,128)}, f32[2,40,256]{2,1,0:T(8,128)S(1)}, u32[]{:S(2)}, u32[]{:S(2)}) collective-permute-start(f32[2,40,256]{2,1,0:T(8,128)} %get-tuple-element.46), channel_id=1, source_target_pairs={{0,1},{1,2},{2,3},{3,0},{4,5},{5,6},{6,7},{7,4},{8,9},{9,10},{10,1... | collective-permute-start | bytes 245768 | tf_op jit(solution)/shard_map/ppermute | solution.py:34
  77.3 4.9 %collective-permute-start.5 = (f32[2,40,256]{2,1,0:T(8,128)}, f32[2,40,256]{2,1,0:T(8,128)S(1)}, u32[]{:S(2)}, u32[]{:S(2)}) collective-permute-start(f32[2,40,256]{2,1,0:T(8,128)} %get-tuple-element.47), channel_id=1, source_target_pairs={{0,3},{1,0},{2,1},{3,2},{4,7},{5,4},{6,5},{7,6},{8,11},{9,8},{10,9... | collective-permute-start | bytes 245768 | tf_op jit(solution)/shard_map/ppermute | solution.py:34
  81.3 7.5 %copy-start.2 = (f32[2,40,256]{2,1,0:T(8,128)}, f32[2,40,256]{2,1,0:T(8,128)S(1)}, u32[]{:S(2)}) copy-start(f32[2,40,256]{2,1,0:T(8,128)S(1)} %collective-permute-done.4.left) | copy-start | bytes 245764
  82.2 6.7 %copy-start.3 = (f32[2,40,256]{2,1,0:T(8,128)}, f32[2,40,256]{2,1,0:T(8,128)S(1)}, u32[]{:S(2)}) copy-start(f32[2,40,256]{2,1,0:T(8,128)S(1)} %collective-permute-done.5.right) | copy-start | bytes 245764
  82.2 5.8 %collective-permute-start.6 = (f32[2,120,128]{2,1,0:T(8,128)S(1)}, f32[2,120,128]{2,1,0:T(8,128)S(1)}, u32[]{:S(2)}, u32[]{:S(2)}) collective-permute-start(f32[2,120,128]{2,1,0:T(8,128)S(1)} %pad_maximum_fusion.2), channel_id=1, source_target_pairs={{0,4},{4,8},{8,12},{12,0},{1,5},{5,9},{9,13},{13,1},{2,6},{6,10},{... | collective-permute-start | bytes 368648 | tf_op jit(solution)/shard_map/ppermute | solution.py:34
  83.7 5.1 %collective-permute-start.7 = (f32[2,120,128]{2,1,0:T(8,128)S(1)}, f32[2,120,128]{2,1,0:T(8,128)S(1)}, u32[]{:S(2)}, u32[]{:S(2)}) collective-permute-start(f32[2,120,128]{2,1,0:T(8,128)S(1)} %pad_maximum_fusion.3), channel_id=1, source_target_pairs={{0,12},{4,0},{8,4},{12,8},{1,13},{5,1},{9,5},{13,9},{2,14},{6,2},{... | collective-permute-start | bytes 368648 | tf_op jit(solution)/shard_map/ppermute | solution.py:34
  88.1 0.8 copy-start.8
  88.9 0.7 copy-start.9
  128.5 6.1 %collective-permute-start.8 = (f32[2,24,256]{2,1,0:T(8,128)}, f32[2,24,256]{2,1,0:T(8,128)S(1)}, u32[]{:S(2)}, u32[]{:S(2)}) collective-permute-start(f32[2,24,256]{2,1,0:T(8,128)} %get-tuple-element.55), channel_id=1, source_target_pairs={{0,1},{1,2},{2,3},{3,0},{4,5},{5,6},{6,7},{7,4},{8,9},{9,10},{10,1... | collective-permute-start | bytes 147464 | tf_op jit(solution)/shard_map/ppermute | solution.py:34
  129.8 5.4 %collective-permute-start.9 = (f32[2,24,256]{2,1,0:T(8,128)}, f32[2,24,256]{2,1,0:T(8,128)S(1)}, u32[]{:S(2)}, u32[]{:S(2)}) collective-permute-start(f32[2,24,256]{2,1,0:T(8,128)} %get-tuple-element.56), channel_id=1, source_target_pairs={{0,3},{1,0},{2,1},{3,2},{4,7},{5,4},{6,5},{7,6},{8,11},{9,8},{10,9... | collective-permute-start | bytes 147464 | tf_op jit(solution)/shard_map/ppermute | solution.py:34
  134.7 6.4 %copy-start.4 = (f32[2,24,256]{2,1,0:T(8,128)}, f32[2,24,256]{2,1,0:T(8,128)S(1)}, u32[]{:S(2)}) copy-start(f32[2,24,256]{2,1,0:T(8,128)S(1)} %collective-permute-done.8.left) | copy-start | bytes 147460
  135.2 5.9 %copy-start.5 = (f32[2,24,256]{2,1,0:T(8,128)}, f32[2,24,256]{2,1,0:T(8,128)S(1)}, u32[]{:S(2)}) copy-start(f32[2,24,256]{2,1,0:T(8,128)S(1)} %collective-permute-done.9.right) | copy-start | bytes 147460
  135.2 5.3 %collective-permute-start.10 = (f32[2,72,128]{2,1,0:T(8,128)S(1)}, f32[2,72,128]{2,1,0:T(8,128)S(1)}, u32[]{:S(2)}, u32[]{:S(2)}) collective-permute-start(f32[2,72,128]{2,1,0:T(8,128)S(1)} %pad_maximum_fusion.4), channel_id=1, source_target_pairs={{0,4},{4,8},{8,12},{12,0},{1,5},{5,9},{9,13},{13,1},{2,6},{6,10},{... | collective-permute-start | bytes 221192 | tf_op jit(solution)/shard_map/ppermute | solution.py:34
  136.7 4.4 %collective-permute-start.11 = (f32[2,72,128]{2,1,0:T(8,128)S(1)}, f32[2,72,128]{2,1,0:T(8,128)S(1)}, u32[]{:S(2)}, u32[]{:S(2)}) collective-permute-start(f32[2,72,128]{2,1,0:T(8,128)S(1)} %pad_maximum_fusion.5), channel_id=1, source_target_pairs={{0,12},{4,0},{8,4},{12,8},{1,13},{5,1},{9,5},{13,9},{2,14},{6,2},{... | collective-permute-start | bytes 221192 | tf_op jit(solution)/shard_map/ppermute | solution.py:34
  140.5 0.6 copy-start.10
  141.1 0.6 copy-start.11
  175.8 1.5 collective-permute-start.12
  178.1 4.3 %collective-permute-start.15 = (f32[72,128]{1,0:T(8,128)S(1)}, f32[72,128]{1,0:T(8,128)S(1)}, u32[]{:S(2)}, u32[]{:S(2)}) collective-permute-start(f32[72,128]{1,0:T(8,128)S(1)} %add.46), channel_id=1, source_target_pairs={{0,12},{4,0},{8,4},{12,8},{1,13},{5,1},{9,5},{13,9},{2,14},{6,2},{... | collective-permute-start | bytes 110600 | tf_op jit(solution)/shard_map/ppermute | solution.py:34
  180.5 4.0 %collective-permute-start.14 = (f32[72,128]{1,0:T(8,128)S(1)}, f32[72,128]{1,0:T(8,128)S(1)}, u32[]{:S(2)}, u32[]{:S(2)}) collective-permute-start(f32[72,128]{1,0:T(8,128)S(1)} %add.46), channel_id=1, source_target_pairs={{0,8},{4,12},{8,0},{12,4},{1,9},{5,13},{9,1},{13,5},{2,10},{6,14},... | collective-permute-start | bytes 110600 | tf_op jit(solution)/shard_map/ppermute | solution.py:34
  181.6 4.9 %collective-permute-start.13 = (f32[72,128]{1,0:T(8,128)S(1)}, f32[72,128]{1,0:T(8,128)S(1)}, u32[]{:S(2)}, u32[]{:S(2)}) collective-permute-start(f32[72,128]{1,0:T(8,128)S(1)} %add.46), channel_id=1, source_target_pairs={{0,4},{4,8},{8,12},{12,0},{1,5},{5,9},{9,13},{13,1},{2,6},{6,10},{... | collective-permute-start | bytes 110600 | tf_op jit(solution)/shard_map/ppermute | solution.py:34
  186.4 5.7 %collective-permute-start.18 = (f32[72,128]{1,0:T(8,128)S(1)}, f32[72,128]{1,0:T(8,128)S(1)}, u32[]{:S(2)}, u32[]{:S(2)}) collective-permute-start(f32[72,128]{1,0:T(8,128)S(1)} %add_add_fusion.1), channel_id=1, source_target_pairs={{0,3},{1,0},{2,1},{3,2},{4,7},{5,4},{6,5},{7,6},{8,11},{9,8},{10,9... | collective-permute-start | bytes 110600 | tf_op jit(solution)/shard_map/ppermute | solution.py:34
  190.5 4.9 %collective-permute-start.17 = (f32[72,128]{1,0:T(8,128)S(1)}, f32[72,128]{1,0:T(8,128)S(1)}, u32[]{:S(2)}, u32[]{:S(2)}) collective-permute-start(f32[72,128]{1,0:T(8,128)S(1)} %add_add_fusion.1), channel_id=1, source_target_pairs={{0,2},{1,3},{2,0},{3,1},{4,6},{5,7},{6,4},{7,5},{8,10},{9,11},{10,... | collective-permute-start | bytes 110600 | tf_op jit(solution)/shard_map/ppermute | solution.py:34
  190.5 5.8 %collective-permute-start.16 = (f32[72,128]{1,0:T(8,128)S(1)}, f32[72,128]{1,0:T(8,128)S(1)}, u32[]{:S(2)}, u32[]{:S(2)}) collective-permute-start(f32[72,128]{1,0:T(8,128)S(1)} %add_add_fusion.1), channel_id=1, source_target_pairs={{0,1},{1,2},{2,3},{3,0},{4,5},{5,6},{6,7},{7,4},{8,9},{9,10},{10,1... | collective-permute-start | bytes 110600 | tf_op jit(solution)/shard_map/ppermute | solution.py:34

commit v4 on v3

--- a/solution.py
+++ b/solution.py
@@ -291,8 +291,8 @@
     return lax.dot_general(left, right, (((1,), (1,)), ((), ())), preferred_element_type=F32)
 
 
-def columns(plan, step, inputs_ref, window_ref):
-    lay_rows(inputs_ref, plan.in_row + CHUNK_ROWS * step, plan.in_lane, plan.wide, window_ref)
+def columns(plan, row, inputs_ref, window_ref):
+    lay_rows(inputs_ref, plan.in_row + row, plan.in_lane, plan.wide, window_ref)
     window = window_ref[...]
     parts = [shifted(window, row * plan.wide, plan.chunk) for row in range(3)]
     return jnp.concatenate(parts + [jnp.zeros((8, plan.chunk), F32)], axis=0)
@@ -306,60 +306,73 @@
     return total
 
 
-def network(plan, inputs_ref, weight_refs, coefs_ref, window_ref, terms_ref):
+def before_silu(weight_ref, inputs, bias_ref):
+    bias = jnp.concatenate([bias_ref[...]] * (inputs.shape[1] // 128), axis=1)
+    return product(weight_ref[...], inputs) + bias
+
+
+def network(plan, inputs_ref, weight_refs, coefs_ref, window_ref, terms_ref, one_ref, two_ref):
     w1_ref, b1_ref, w2_ref, b2_ref, w3_ref = weight_refs
     terms_ref[...] = jnp.zeros_like(terms_ref)
+    one_ref[...] = jnp.zeros_like(one_ref)
+    two_ref[...] = jnp.zeros_like(two_ref)
     lag = LEAD - 2 * plan.wide
 
-    def one_chunk(step, carried):
-        cols = columns(plan, step, inputs_ref, window_ref).astype(BF16)
-        half = product(w1_ref[...], cols) + b1_ref[...]
-        hidden = (half * jnp.tanh(half) + half).astype(BF16)
-        half = product(w2_ref[...], hidden) + b2_ref[...]
-        hidden = (half * jnp.tanh(half) + half).astype(BF16)
+    def one_turn(turn, carried):
+        last = jnp.maximum(turn - 2, 0)
         terms_ref[:, :LEAD] = terms_ref[:, plan.chunk :]
-        terms_ref[:, LEAD:] = product(w3_ref[...], hidden)
+        cols = columns(plan, CHUNK_ROWS * jnp.minimum(turn, plan.chunks - 1), inputs_ref, window_ref).astype(BF16)
+        terms_ref[:, LEAD:] = product(w3_ref[...], two_ref[...])
+        half = before_silu(w2_ref, one_ref[...], b2_ref)
+        two_ref[...] = (half * jnp.tanh(half) + half).astype(BF16)
+        half = before_silu(w1_ref, cols, b1_ref)
+        one_ref[...] = (half * jnp.tanh(half) + half).astype(BF16)
         total = COEF_SCALE * add_taps(terms_ref, [offset + lag for offset in plan.offsets], plan.chunk)
-        split_rows(total, coefs_ref, plan.out_row - 2 + CHUNK_ROWS * step, plan.out_lane, plan.wide)
+        split_rows(total, coefs_ref, plan.out_row - 2 + CHUNK_ROWS * last, plan.out_lane, plan.wide)
         return carried
 
-    lax.fori_loop(0, plan.chunks, one_chunk, 0)
-
-
-def network_back(plan, inputs_ref, taps_ref, weight_refs, place_ref, grads_ref, sums_ref, cross_ref, window_ref, terms_ref):
+    lax.fori_loop(0, plan.chunks + 2, one_turn, 0)
+
+
+def with_slope(half):
+    bend = jnp.tanh(half)
+    return half * bend + half, (0.5 + 0.5 * bend) * (1.0 + half * (1.0 - bend))
+
+
+def network_back(plan, inputs_ref, taps_ref, weight_refs, place_ref, grads_ref, sums_ref, net_refs):
     w1_ref, b1_ref, w2_ref, b2_ref, w1b_ref, w2b_ref, w3b_ref = weight_refs
+    cross_ref, window_ref, terms_ref = net_refs
     terms_ref[...] = jnp.zeros_like(terms_ref)
     cross_ref[...] = jnp.zeros_like(cross_ref)
 
     def one_chunk(step, carried):
-        row = place_ref[...] + CHUNK_ROWS * step
-        own = jnp.where((row >= plan.rim + 1) & (row < plan.rim + 1 + plan.rows), 1.0, 0.0)
-        mask = own.astype(BF16)
-        cols = columns(plan, step, inputs_ref, window_ref).astype(BF16)
-        half = product(w1_ref[...], cols) + b1_ref[...]
-        bend = jnp.tanh(half)
-        hidden_one = (half * bend + half).astype(BF16)
-        slope_one = (0.5 + 0.5 * bend) * (1.0 + half * (1.0 - bend))
-        half = product(w2_ref[...], hidden_one) + b2_ref[...]
-        bend = jnp.tanh(half)
-        hidden_two = (half * bend + half).astype(BF16)
-        slope_two = (0.5 + 0.5 * bend) * (1.0 + half * (1.0 - bend))
-        lay_rows(taps_ref, plan.out_row - 2 + CHUNK_ROWS * step, plan.out_lane, plan.wide, window_ref)
+        row = CHUNK_ROWS * step
+        place = place_ref[...] + row
+        own = jnp.where((place >= plan.rim + 1) & (place < plan.rim + 1 + plan.rows), 1.0, 0.0).astype(BF16)
+        own = jnp.concatenate([own] * 4, axis=0)
+        cols = columns(plan, row, inputs_ref, window_ref).astype(BF16)
+        hidden, slope_one = with_slope(before_silu(w1_ref, cols, b1_ref))
+        hidden_one = hidden.astype(BF16)
+        hidden, slope_two = with_slope(before_silu(w2_ref, hidden_one, b2_ref))
+        hidden_two = hidden.astype(BF16)
+        lay_rows(taps_ref, plan.out_row - 2 + row, plan.out_lane, plan.wide, window_ref)
         window = window_ref[...]
         parts = [shifted(window, 2 * plan.wide - offset, plan.chunk) for offset in plan.offsets]
         spread = jnp.concatenate(parts + [jnp.zeros((8, plan.chunk), F32)], axis=0).astype(BF16)
         grad_two = (product(w3b_ref[...], spread) * slope_two).astype(BF16)
         grad_one = (product(w2b_ref[...], grad_two) * slope_one).astype(BF16)
         left = jnp.concatenate([spread, hidden_one, cols], axis=0)
-        right = jnp.concatenate([hidden_two * mask, grad_two * mask, grad_one * mask], axis=0)
+        right = jnp.concatenate([hidden_two * own, grad_two * own, grad_one * own], axis=0)
         cross_ref[...] += product_over_cells(left, right)
         terms_ref[:, :LEAD] = terms_ref[:, plan.chunk :]
         terms_ref[:, LEAD:] = product(w1b_ref[...], grad_one)
         total = add_taps(terms_ref, [LEAD - offset for offset in plan.offsets], plan.chunk)
-        split_rows(total, grads_ref, plan.in_row + CHUNK_ROWS * step, plan.in_lane, plan.wide)
+        split_rows(total, grads_ref, plan.in_row + row, plan.in_lane, plan.wide)
         return carried
 
-    lax.fori_loop(0, plan.chunks, one_chunk, 0)
+    lax.fori_loop(0, plan.chunks // 2, lambda pair, carried: one_chunk(2 * pair + 1, one_chunk(2 * pair, carried)), 0)
+    if plan.chunks % 2:
+        one_chunk(plan.chunks - 1, 0)
     for tap in range(9):
         taken = 144 + 8 * (tap // 3) + 2 * (tap % 3)
         sums_ref[8 * tap : 8 * tap + 6, :64] += cross_ref[8 * tap : 8 * tap + 6, :64]
@@ -401,18 +414,18 @@
     w3[...] = back.astype(BF16)
     w3b[...] = jnp.concatenate([back, jnp.zeros((8, hid), F32)], axis=0).T.astype(BF16)
     for source, target in ((b1_in, b1), (b2_in, b2)):
-        target[...] = jnp.broadcast_to(0.5 * source[...], (8, hid)).T[:, :1]
+        target[...] = jnp.broadcast_to(0.5 * source[...], (128, hid)).T
 
 
 def first_kernel(plan, left, right, above, below, own_ref, goals_ref, force_ref, w1, b1, w2, b2, w3,
-                 v_ref, last_goal_ref, v_out, coefs_ref, error_ref, loss_ref, inputs_ref, window_ref, terms_ref, frame_ref, buffers, rhs_ref):
+                 v_ref, last_goal_ref, v_out, coefs_ref, error_ref, loss_ref, inputs_ref, window_ref, terms_ref, one_ref, two_ref, frame_ref, buffers, rhs_ref):
     pieces = (left, right, above, below)
     for comp in range(2):
         build_frame(own_ref[comp], pieces, comp, v_ref, comp)
         build_frame(goals_ref[goals_ref.shape[0] - 1, comp], pieces, comp + 2, last_goal_ref, comp)
     keep_inputs([v_ref[0], v_ref[1]], inputs_ref)
     coefs_ref[...] = jnp.zeros_like(coefs_ref)
-    network(plan, inputs_ref, (w1, b1, w2, b2, w3), coefs_ref, window_ref, terms_ref)
+    network(plan, inputs_ref, (w1, b1, w2, b2, w3), coefs_ref, window_ref, terms_ref, one_ref, two_ref)
     height = v_ref.shape[1]
     result = advect(
         [v_ref[0], v_ref[1]], [channel(coefs_ref, number, 0, height) for number in range(6)], force_ref[...]
@@ -430,10 +443,11 @@
     loss_ref[...] = loss[:, :64] + loss[:, 64:]
 
 
-def second_kernel(plan, v_ref, force_ref, w1, b1, w2, b2, w3, out_ref, low_ref, high_ref, coefs_ref, inputs_ref, window_ref, terms_ref):
+def second_kernel(plan, v_ref, force_ref, w1, b1, w2, b2, w3, out_ref, low_ref, high_ref, coefs_ref, inputs_ref, window_ref,
+                  terms_ref, one_ref, two_ref):
     keep_inputs([v_ref[0], v_ref[1]], inputs_ref)
     coefs_ref[...] = jnp.zeros_like(coefs_ref)
-    network(plan, inputs_ref, (w1, b1, w2, b2, w3), coefs_ref, window_ref, terms_ref)
+    network(plan, inputs_ref, (w1, b1, w2, b2, w3), coefs_ref, window_ref, terms_ref, one_ref, two_ref)
     low, tall = TOP - 8, plan.rows + 16
     v = [v_ref[comp, low : low + tall] for comp in range(2)]
     result = advect(v, [channel(coefs_ref, number, low, tall) for number in range(6)], force_ref[...])
@@ -444,7 +458,7 @@
 
 
 def back_kernel(plan, last, left, right, above, below, own_ref, goal_ref, extra_ref, before_ref, v_ref, coefs_ref,
-                place_ref, w1, b1, w2, b2, w1b, w2b, w3b, out_ref, low_ref, high_ref, sums_ref, inputs_ref, taps_ref, grads_ref, cross_ref, window_ref, terms_ref, frame_ref, buffers, rhs_ref):
+                place_ref, w1, b1, w2, b2, w1b, w2b, w3b, out_ref, low_ref, high_ref, sums_ref, inputs_ref, taps_ref, grads_ref, frame_ref, buffers, rhs_ref, *net_refs):
     rows, cols = plan.rows, plan.cols
     sums_ref[...] = before_ref[...]
     for comp in range(2):
@@ -473,7 +487,7 @@
     for comp in range(2):
         frame_ref[comp, low : low + tall] = result[comp]
     weight_refs = (w1, b1, w2, b2, w1b, w2b, w3b)
-    network_back(plan, inputs_ref, taps_ref, weight_refs, place_ref, grads_ref, sums_ref, cross_ref, window_ref, terms_ref)
+    network_back(plan, inputs_ref, taps_ref, weight_refs, place_ref, grads_ref, sums_ref, net_refs)
     for comp in range(2):
         field = frame_ref[comp, low : low + tall] + channel(grads_ref, comp, low, tall)
         total = own_part(field, rows, cols, low)
@@ -518,18 +532,21 @@
     def call(kernel, outs, scratch, *args, kind=F32):
         return pl.pallas_call(
             kernel,
-            out_shape=[jax.ShapeDtypeStruct(shape, F32 if shape[1] == 1 else kind) for shape in outs],
-            scratch_shapes=[pltpu.VMEM(shape, F32) for shape in scratch],
+            out_shape=[jax.ShapeDtypeStruct(shape, F32 if shape[1] == 128 else kind) for shape in outs],
+            scratch_shapes=[pltpu.VMEM(item, F32) if isinstance(item, tuple) else item for item in scratch],
             compiler_params=pltpu.CompilerParams(vmem_limit_bytes=60 << 20),
         )(*args)
 
     def net_scratch(plan):
         return [(8, plan.window), (72, plan.chunk + LEAD)]
 
+    def layers(plan):
+        return [pltpu.VMEM((hid, plan.chunk), BF16)] * 2
+
     sweep_scratch = [pair, (2, 2, height + 2 * GUARD, 128), (2, height, 128)]
 
     w1, b1, w2, b2, w3, w1b, w3b = call(
-        weights_kernel, [(hid, 32), (hid, 1), (hid, hid), (hid, 1), (72, hid), (72, hid), (hid, 80)], [],
+        weights_kernel, [(hid, 32), (hid, 128), (hid, hid), (hid, 128), (72, hid), (72, hid), (hid, 80)], [],
         weight_one, bias_one[None, :], weight_two, bias_two[None, :], jnp.swapaxes(weight_three, 2, 3), kind=BF16,
     )
     forward_weights = (w1, b1, w2, b2, w3)
@@ -538,7 +555,7 @@
     lane = np.arange(near.chunk)
     place_row, place_col = lane // near.wide, lane % near.wide
     mine = (place_col >= near.rim + 1) & (place_col < near.rim + 1 + cols)
-    place = jnp.asarray(np.where(mine, place_row, -10 * height)[None, :], jnp.int32)
+    place = jnp.asarray(np.tile(np.where(mine, place_row, -10 * height), (16, 1)), jnp.int32)
 
     total_cols = cols * lax.axis_size("gy")
     col_ids = lax.axis_index("gy") * cols + jnp.arange(frame[1], dtype=jnp.int32) - LEFT
@@ -552,16 +569,16 @@
     v_first, last_goal, v_second, coefs_first, error_first, loss_first = call(
         functools.partial(first_kernel, far),
         [pair, pair, pair, packed, own_pair, (1, 64)],
-        [packed] + net_scratch(far) + sweep_scratch,
+        [packed] + net_scratch(far) + layers(far) + sweep_scratch,
         *pieces, velocity[0], targets[0], forcing, *forward_weights,
     )
     provisional, low, high, coefs_second = call(
         functools.partial(second_kernel, near),
         [own_pair] + strips(2, 40) + [packed],
-        [packed] + net_scratch(near),
+        [packed] + net_scratch(near) + layers(near),
         v_second, forcing, *forward_weights,
     )
-    back_scratch = [packed, packed, packed, (176, 192)] + net_scratch(near) + sweep_scratch
+    back_scratch = [packed, packed, packed] + sweep_scratch + [(176, 192)] + net_scratch(near)
     start_sums = jnp.pad(loss_first, ((66, 5), (64, 0)))
     grad, low, high, sums = call(
         functools.partial(back_kernel, near, True),

time: 202 us -> 179 us (0.89)
  Pallas kernels: 128 us -> 104 us
    pallas_call x7, Pallas kernels: 128 us -> 104 us  [call(): pl.pallas_call(kernel, out_shape=[jax.ShapeDtypeStruct(shape, F32 if shap...]
where the time goes in v4:
time: 179 us; the launch traced here: 178 us
  Pallas kernels  104 us (58%)
  waiting for transfers between devices  31.4 us (18%)
  starting transfers between devices  30.3 us (17%)
  local copies, waits for them, and re-layouts  9.34 us (5%)
  other arithmetic  2.12 us (1%)
    pallas_call x7, Pallas kernels, call(): pl.pallas_call(kernel, out_shape=[jax.ShapeDtypeStruct(shape, F32 if shap...  104 us
    ppermute x19, waiting for transfers between devices, passed_along(): return lax.ppermute(block, axis, route)  31.4 us
    ppermute x19, starting transfers between devices, passed_along(): return lax.ppermute(block, axis, route)  30.3 us
  transfers between devices with their start and end apart: 19, of which 19 were waited for; matrix products, arithmetic and copies ran while one was open for 3% of the time, Pallas kernels for 1%

profile of v4, /device:TPU:0, one launch (start us, length us, event | category | flops | bytes accessed | tf_op | source)
XLA Modules:
  0.0 178.0 jit_solution(2208766300967056259)
XLA Ops:
  0.6 2.0 %shard_map.135 = (f32[4,32,256]{2,1,0:T(8,128)}, f32[4,32,256]{2,1,0:T(8,128)}) custom-call(f32[2,256,128]{2,1,0:T(8,128)} %bitcast.14, f32[2,2,256,128]{3,2,1,0:T(8,128)} %bitcast.12), custom_call_target="tpu_custom_call" | custom-call | tf_op jit(solution)/shard_map/pallas_call | solution.py:533
  2.6 3.0 %collective-permute-start = (f32[4,32,256]{2,1,0:T(8,128)}, f32[4,32,256]{2,1,0:T(8,128)S(1)}, u32[]{:S(2)}, u32[]{:S(2)}) collective-permute-start(f32[4,32,256]{2,1,0:T(8,128)} %get-tuple-element.38), channel_id=1, source_target_pairs={{0,1},{1,2},{2,3},{3,0},{4,5},{5,6},{6,7},{7,4},{8,9},{9,10},{10,1... | collective-permute-start | bytes 393224 | tf_op jit(solution)/shard_map/ppermute | solution.py:34
  5.7 2.0 %collective-permute-start.1 = (f32[4,32,256]{2,1,0:T(8,128)}, f32[4,32,256]{2,1,0:T(8,128)S(1)}, u32[]{:S(2)}, u32[]{:S(2)}) collective-permute-start(f32[4,32,256]{2,1,0:T(8,128)} %get-tuple-element.39), channel_id=1, source_target_pairs={{0,3},{1,0},{2,1},{3,2},{4,7},{5,4},{6,5},{7,6},{8,11},{9,8},{10,9... | collective-permute-start | bytes 393224 | tf_op jit(solution)/shard_map/ppermute | solution.py:34
  7.7 1.0 slice_bitcast_fusion
  8.7 0.8 fusion.2
  9.4 2.8 %collective-permute-done.left = f32[4,32,256]{2,1,0:T(8,128)S(1)} collective-permute-done((f32[4,32,256]{2,1,0:T(8,128)}, f32[4,32,256]{2,1,0:T(8,128)S(1)}, u32[]{:S(2)}, u32[]{:S(2)}) %collective-permute-start) | collective-permute-done | bytes 131104 | tf_op jit(solution)/shard_map/ppermute | solution.py:34
  12.2 1.4 collective-permute-done.1.right
  13.7 1.5 collective-permute-start.2
  15.2 1.5 collective-permute-start.3
  16.7 1.5 shard_map.136
  18.9 3.6 %collective-permute-done.2.above = f32[4,96,128]{2,1,0:T(8,128)S(1)} collective-permute-done((f32[4,96,128]{2,1,0:T(8,128)S(1)}, f32[4,96,128]{2,1,0:T(8,128)S(1)}, u32[]{:S(2)}, u32[]{:S(2)}) %collective-permute-start.2) | collective-permute-done | bytes 196640 | tf_op jit(solution)/shard_map/ppermute | solution.py:34
  22.5 2.6 %collective-permute-done.3.below = f32[4,96,128]{2,1,0:T(8,128)S(1)} collective-permute-done((f32[4,96,128]{2,1,0:T(8,128)S(1)}, f32[4,96,128]{2,1,0:T(8,128)S(1)}, u32[]{:S(2)}, u32[]{:S(2)}) %collective-permute-start.3) | collective-permute-done | bytes 196640 | tf_op jit(solution)/shard_map/ppermute | solution.py:34
  25.1 0.7 copy-done.7
  25.8 21.8 %shard_map.137 = (f32[2,336,256]{2,1,0:T(8,128)}, f32[2,336,256]{2,1,0:T(8,128)}, f32[2,336,256]{2,1,0:T(8,128)}, f32[2,2688,128]{2,1,0:T(8,128)}, f32[2,256,128]{2,1,0:T(8,128)}, /*index=5*/f32[1,64]{1,0:T(1,128)}) custom-call(f32[4,32,256]{2,1,0:T(8,128)} %copy-done, f32[4,32,256]{2,1,0:T(8,128)} %copy-done.1, f32[4,96,128]{2,1,0:T(8,128)} %copy-done.6, ...), custom_call_target="tpu_custom_call" | custom-call | tf_op jit(solution)/shard_map/pallas_call | solution.py:533
  47.5 13.0 %shard_map.138 = (f32[2,256,128]{2,1,0:T(8,128)}, f32[2,40,256]{2,1,0:T(8,128)}, f32[2,40,256]{2,1,0:T(8,128)}, f32[2,2688,128]{2,1,0:T(8,128)}) custom-call(f32[2,336,256]{2,1,0:T(8,128)} %get-tuple-element.45.v_ref, f32[1,256]{1,0:T(1,128)} %multiply_sine_fusion.force_ref.goal_ref.extra_ref, bf16[64,32]{1,0:T(8,128)(2,1)} %get-tuple-element.40.w1, ...), custom_call_target="tpu_custom_call" | custom-call | tf_op jit(solution)/shard_map/pallas_call | solution.py:533
  60.5 1.7 collective-permute-start.4
  62.3 0.8 fusion.1
  63.1 2.1 %collective-permute-start.5 = (f32[2,40,256]{2,1,0:T(8,128)}, f32[2,40,256]{2,1,0:T(8,128)S(1)}, u32[]{:S(2)}, u32[]{:S(2)}) collective-permute-start(f32[2,40,256]{2,1,0:T(8,128)} %get-tuple-element.47), channel_id=1, source_target_pairs={{0,3},{1,0},{2,1},{3,2},{4,7},{5,4},{6,5},{7,6},{8,11},{9,8},{10,9... | collective-permute-start | bytes 245768 | tf_op jit(solution)/shard_map/ppermute | solution.py:34
  65.1 1.9 %collective-permute-done.4.left = f32[2,40,256]{2,1,0:T(8,128)S(1)} collective-permute-done((f32[2,40,256]{2,1,0:T(8,128)}, f32[2,40,256]{2,1,0:T(8,128)S(1)}, u32[]{:S(2)}, u32[]{:S(2)}) %collective-permute-start.4) | collective-permute-done | bytes 81952 | tf_op jit(solution)/shard_map/ppermute | solution.py:34
  67.0 0.8 collective-permute-done.5.right
  67.9 1.6 collective-permute-start.6
  69.5 1.7 collective-permute-start.7
  71.2 1.3 pad.4.before_ref
  72.5 1.3 collective-permute-done.6.above
  73.8 0.8 collective-permute-done.7.below
  75.3 34.3 %shard_map.139 = (f32[2,256,128]{2,1,0:T(8,128)}, f32[2,24,256]{2,1,0:T(8,128)}, f32[2,24,256]{2,1,0:T(8,128)}, f32[72,128]{1,0:T(8,128)}) custom-call(f32[2,40,256]{2,1,0:T(8,128)} %copy-done.2, f32[2,40,256]{2,1,0:T(8,128)} %copy-done.3, f32[2,120,128]{2,1,0:T(8,128)} %copy-done.8, f32[2,120,128]{2,1,0:T(8,128)} %copy-done.9, ...), custom_call_target="tpu_custom_call" | custom-call | tf_op jit(solution)/shard_map/pallas_call | solution.py:533
  110.1 0.8 fusion
  110.9 3.3 %collective-permute-start.9 = (f32[2,24,256]{2,1,0:T(8,128)}, f32[2,24,256]{2,1,0:T(8,128)S(1)}, u32[]{:S(2)}, u32[]{:S(2)}) collective-permute-start(f32[2,24,256]{2,1,0:T(8,128)} %get-tuple-element.56), channel_id=1, source_target_pairs={{0,3},{1,0},{2,1},{3,2},{4,7},{5,4},{6,5},{7,6},{8,11},{9,8},{10,9... | collective-permute-start | bytes 147464 | tf_op jit(solution)/shard_map/ppermute | solution.py:34
  114.2 1.5 collective-permute-done.8.left
  116.3 1.4 collective-permute-start.10
  117.7 1.6 collective-permute-start.11
  119.3 2.3 %collective-permute-done.10.above = f32[2,72,128]{2,1,0:T(8,128)S(1)} collective-permute-done((f32[2,72,128]{2,1,0:T(8,128)S(1)}, f32[2,72,128]{2,1,0:T(8,128)S(1)}, u32[]{:S(2)}, u32[]{:S(2)}) %collective-permute-start.10) | collective-permute-done | bytes 73760 | tf_op jit(solution)/shard_map/ppermute | solution.py:34
  122.7 29.5 %shard_map.140 = (f32[2,256,128]{2,1,0:T(8,128)}, f32[1,8,128]{2,1,0:T(8,128)}, f32[1,8,128]{2,1,0:T(8,128)}, f32[72,128]{1,0:T(8,128)}) custom-call(f32[2,24,256]{2,1,0:T(8,128)} %copy-done.4, f32[2,24,256]{2,1,0:T(8,128)} %copy-done.5, f32[2,72,128]{2,1,0:T(8,128)} %copy-done.10, f32[2,72,128]{2,1,0:T(8,128)} %copy-done.11, ...), custom_call_target="tpu_custom_call" | custom-call | tf_op jit(solution)/shard_map/pallas_call | solution.py:533
  152.3 1.4 collective-permute-done.12
  153.7 0.8 add.46
  154.5 2.5 %collective-permute-start.15 = (f32[72,128]{1,0:T(8,128)S(1)}, f32[72,128]{1,0:T(8,128)S(1)}, u32[]{:S(2)}, u32[]{:S(2)}) collective-permute-start(f32[72,128]{1,0:T(8,128)S(1)} %add.46), channel_id=1, source_target_pairs={{0,12},{4,0},{8,4},{12,8},{1,13},{5,1},{9,5},{13,9},{2,14},{6,2},{... | collective-permute-start | bytes 110600 | tf_op jit(solution)/shard_map/ppermute | solution.py:34
  157.0 1.0 collective-permute-start.14
  158.1 0.7 collective-permute-done.15
  158.8 2.1 %collective-permute-done.14 = f32[72,128]{1,0:T(8,128)S(1)} collective-permute-done((f32[72,128]{1,0:T(8,128)S(1)}, f32[72,128]{1,0:T(8,128)S(1)}, u32[]{:S(2)}, u32[]{:S(2)}) %collective-permute-start.14) | collective-permute-done | bytes 36896 | tf_op jit(solution)/shard_map/ppermute | solution.py:34
  160.9 1.9 %collective-permute-done.13 = f32[72,128]{1,0:T(8,128)S(1)} collective-permute-done((f32[72,128]{1,0:T(8,128)S(1)}, f32[72,128]{1,0:T(8,128)S(1)}, u32[]{:S(2)}, u32[]{:S(2)}) %collective-permute-start.13) | collective-permute-done | bytes 36896 | tf_op jit(solution)/shard_map/ppermute | solution.py:34
  162.9 4.1 %collective-permute-start.18 = (f32[72,128]{1,0:T(8,128)S(1)}, f32[72,128]{1,0:T(8,128)S(1)}, u32[]{:S(2)}, u32[]{:S(2)}) collective-permute-start(f32[72,128]{1,0:T(8,128)S(1)} %add_add_fusion.1), channel_id=1, source_target_pairs={{0,3},{1,0},{2,1},{3,2},{4,7},{5,4},{6,5},{7,6},{8,11},{9,8},{10,9... | collective-permute-start | bytes 110600 | tf_op jit(solution)/shard_map/ppermute | solution.py:34
  167.0 0.7 collective-permute-start.16
  167.6 1.0 collective-permute-done.18
  168.6 3.2 %collective-permute-done.17 = f32[72,128]{1,0:T(8,128)S(1)} collective-permute-done((f32[72,128]{1,0:T(8,128)S(1)}, f32[72,128]{1,0:T(8,128)S(1)}, u32[]{:S(2)}, u32[]{:S(2)}) %collective-permute-start.17) | collective-permute-done | bytes 36896 | tf_op jit(solution)/shard_map/ppermute | solution.py:34
  171.8 0.9 collective-permute-done.16
  173.3 2.0 %shard_map.141 = (f32[18,64]{1,0:T(8,128)}, f32[1,64]{1,0:T(1,128)}, f32[64,64]{1,0:T(8,128)}, f32[1,64]{1,0:T(1,128)}, f32[54,64]{1,0:T(8,128)}, /*index=5*/f32[1,1]{1,0:T(1,128)}) custom-call(f32[72,128]{1,0:T(8,128)} %add_add_fusion.in_ref), custom_call_target="tpu_custom_call" | custom-call | tf_op jit(solution)/shard_map/pallas_call | solution.py:533
  175.3 1.3 reshape.39
  176.6 1.4 reshape.40
  (44 shorter events, 4.4 us)
Async XLA Ops:
  2.6 9.6 %collective-permute-start = (f32[4,32,256]{2,1,0:T(8,128)}, f32[4,32,256]{2,1,0:T(8,128)S(1)}, u32[]{:S(2)}, u32[]{:S(2)}) collective-permute-start(f32[4,32,256]{2,1,0:T(8,128)} %get-tuple-element.38), channel_id=1, source_target_pairs={{0,1},{1,2},{2,3},{3,0},{4,5},{5,6},{6,7},{7,4},{8,9},{9,10},{10,1... | collective-permute-start | bytes 393224 | tf_op jit(solution)/shard_map/ppermute | solution.py:34
  5.7 8.0 %collective-permute-start.1 = (f32[4,32,256]{2,1,0:T(8,128)}, f32[4,32,256]{2,1,0:T(8,128)S(1)}, u32[]{:S(2)}, u32[]{:S(2)}) collective-permute-start(f32[4,32,256]{2,1,0:T(8,128)} %get-tuple-element.39), channel_id=1, source_target_pairs={{0,3},{1,0},{2,1},{3,2},{4,7},{5,4},{6,5},{7,6},{8,11},{9,8},{10,9... | collective-permute-start | bytes 393224 | tf_op jit(solution)/shard_map/ppermute | solution.py:34
  12.2 12.9 %copy-start = (f32[4,32,256]{2,1,0:T(8,128)}, f32[4,32,256]{2,1,0:T(8,128)S(1)}, u32[]{:S(2)}) copy-start(f32[4,32,256]{2,1,0:T(8,128)S(1)} %collective-permute-done.left) | copy-start | bytes 393220
  13.6 11.5 %copy-start.1 = (f32[4,32,256]{2,1,0:T(8,128)}, f32[4,32,256]{2,1,0:T(8,128)S(1)}, u32[]{:S(2)}) copy-start(f32[4,32,256]{2,1,0:T(8,128)S(1)} %collective-permute-done.1.right) | copy-start | bytes 393220
  13.7 8.8 %collective-permute-start.2 = (f32[4,96,128]{2,1,0:T(8,128)S(1)}, f32[4,96,128]{2,1,0:T(8,128)S(1)}, u32[]{:S(2)}, u32[]{:S(2)}) collective-permute-start(f32[4,96,128]{2,1,0:T(8,128)S(1)} %pad_maximum_fusion), channel_id=1, source_target_pairs={{0,4},{4,8},{8,12},{12,0},{1,5},{5,9},{9,13},{13,1},{2,6},{6,10},{... | collective-permute-start | bytes 589832 | tf_op jit(solution)/shard_map/ppermute | solution.py:34
  15.2 9.9 %collective-permute-start.3 = (f32[4,96,128]{2,1,0:T(8,128)S(1)}, f32[4,96,128]{2,1,0:T(8,128)S(1)}, u32[]{:S(2)}, u32[]{:S(2)}) collective-permute-start(f32[4,96,128]{2,1,0:T(8,128)S(1)} %pad_maximum_fusion.1), channel_id=1, source_target_pairs={{0,12},{4,0},{8,4},{12,8},{1,13},{5,1},{9,5},{13,9},{2,14},{6,2},{... | collective-permute-start | bytes 589832 | tf_op jit(solution)/shard_map/ppermute | solution.py:34
  22.5 2.6 %copy-start.6 = (f32[4,96,128]{2,1,0:T(8,128)}, f32[4,96,128]{2,1,0:T(8,128)S(1)}, u32[]{:S(2)}) copy-start(f32[4,96,128]{2,1,0:T(8,128)S(1)} %collective-permute-done.2.above) | copy-start | bytes 589828
  25.1 0.7 copy-start.7
  60.5 6.5 %collective-permute-start.4 = (f32[2,40,256]{2,1,0:T(8,128)}, f32[2,40,256]{2,1,0:T(8,128)S(1)}, u32[]{:S(2)}, u32[]{:S(2)}) collective-permute-start(f32[2,40,256]{2,1,0:T(8,128)} %get-tuple-element.46), channel_id=1, source_target_pairs={{0,1},{1,2},{2,3},{3,0},{4,5},{5,6},{6,7},{7,4},{8,9},{9,10},{10,1... | collective-permute-start | bytes 245768 | tf_op jit(solution)/shard_map/ppermute | solution.py:34
  63.1 4.8 %collective-permute-start.5 = (f32[2,40,256]{2,1,0:T(8,128)}, f32[2,40,256]{2,1,0:T(8,128)S(1)}, u32[]{:S(2)}, u32[]{:S(2)}) collective-permute-start(f32[2,40,256]{2,1,0:T(8,128)} %get-tuple-element.47), channel_id=1, source_target_pairs={{0,3},{1,0},{2,1},{3,2},{4,7},{5,4},{6,5},{7,6},{8,11},{9,8},{10,9... | collective-permute-start | bytes 245768 | tf_op jit(solution)/shard_map/ppermute | solution.py:34
  67.0 7.6 %copy-start.2 = (f32[2,40,256]{2,1,0:T(8,128)}, f32[2,40,256]{2,1,0:T(8,128)S(1)}, u32[]{:S(2)}) copy-start(f32[2,40,256]{2,1,0:T(8,128)S(1)} %collective-permute-done.4.left) | copy-start | bytes 245764
  67.9 6.7 %copy-start.3 = (f32[2,40,256]{2,1,0:T(8,128)}, f32[2,40,256]{2,1,0:T(8,128)S(1)}, u32[]{:S(2)}) copy-start(f32[2,40,256]{2,1,0:T(8,128)S(1)} %collective-permute-done.5.right) | copy-start | bytes 245764
  67.9 5.8 %collective-permute-start.6 = (f32[2,120,128]{2,1,0:T(8,128)S(1)}, f32[2,120,128]{2,1,0:T(8,128)S(1)}, u32[]{:S(2)}, u32[]{:S(2)}) collective-permute-start(f32[2,120,128]{2,1,0:T(8,128)S(1)} %pad_maximum_fusion.2), channel_id=1, source_target_pairs={{0,4},{4,8},{8,12},{12,0},{1,5},{5,9},{9,13},{13,1},{2,6},{6,10},{... | collective-permute-start | bytes 368648 | tf_op jit(solution)/shard_map/ppermute | solution.py:34
  69.5 5.1 %collective-permute-start.7 = (f32[2,120,128]{2,1,0:T(8,128)S(1)}, f32[2,120,128]{2,1,0:T(8,128)S(1)}, u32[]{:S(2)}, u32[]{:S(2)}) collective-permute-start(f32[2,120,128]{2,1,0:T(8,128)S(1)} %pad_maximum_fusion.3), channel_id=1, source_target_pairs={{0,12},{4,0},{8,4},{12,8},{1,13},{5,1},{9,5},{13,9},{2,14},{6,2},{... | collective-permute-start | bytes 368648 | tf_op jit(solution)/shard_map/ppermute | solution.py:34
  73.8 0.9 copy-start.8
  74.6 0.7 copy-start.9
  109.6 6.1 %collective-permute-start.8 = (f32[2,24,256]{2,1,0:T(8,128)}, f32[2,24,256]{2,1,0:T(8,128)S(1)}, u32[]{:S(2)}, u32[]{:S(2)}) collective-permute-start(f32[2,24,256]{2,1,0:T(8,128)} %get-tuple-element.55), channel_id=1, source_target_pairs={{0,1},{1,2},{2,3},{3,0},{4,5},{5,6},{6,7},{7,4},{8,9},{9,10},{10,1... | collective-permute-start | bytes 147464 | tf_op jit(solution)/shard_map/ppermute | solution.py:34
  110.9 5.4 %collective-permute-start.9 = (f32[2,24,256]{2,1,0:T(8,128)}, f32[2,24,256]{2,1,0:T(8,128)S(1)}, u32[]{:S(2)}, u32[]{:S(2)}) collective-permute-start(f32[2,24,256]{2,1,0:T(8,128)} %get-tuple-element.56), channel_id=1, source_target_pairs={{0,3},{1,0},{2,1},{3,2},{4,7},{5,4},{6,5},{7,6},{8,11},{9,8},{10,9... | collective-permute-start | bytes 147464 | tf_op jit(solution)/shard_map/ppermute | solution.py:34
  115.7 6.4 %copy-start.4 = (f32[2,24,256]{2,1,0:T(8,128)}, f32[2,24,256]{2,1,0:T(8,128)S(1)}, u32[]{:S(2)}) copy-start(f32[2,24,256]{2,1,0:T(8,128)S(1)} %collective-permute-done.8.left) | copy-start | bytes 147460
  116.3 5.8 %copy-start.5 = (f32[2,24,256]{2,1,0:T(8,128)}, f32[2,24,256]{2,1,0:T(8,128)S(1)}, u32[]{:S(2)}) copy-start(f32[2,24,256]{2,1,0:T(8,128)S(1)} %collective-permute-done.9.right) | copy-start | bytes 147460
  116.3 5.3 %collective-permute-start.10 = (f32[2,72,128]{2,1,0:T(8,128)S(1)}, f32[2,72,128]{2,1,0:T(8,128)S(1)}, u32[]{:S(2)}, u32[]{:S(2)}) collective-permute-start(f32[2,72,128]{2,1,0:T(8,128)S(1)} %pad_maximum_fusion.4), channel_id=1, source_target_pairs={{0,4},{4,8},{8,12},{12,0},{1,5},{5,9},{9,13},{13,1},{2,6},{6,10},{... | collective-permute-start | bytes 221192 | tf_op jit(solution)/shard_map/ppermute | solution.py:34
  117.7 4.4 %collective-permute-start.11 = (f32[2,72,128]{2,1,0:T(8,128)S(1)}, f32[2,72,128]{2,1,0:T(8,128)S(1)}, u32[]{:S(2)}, u32[]{:S(2)}) collective-permute-start(f32[2,72,128]{2,1,0:T(8,128)S(1)} %pad_maximum_fusion.5), channel_id=1, source_target_pairs={{0,12},{4,0},{8,4},{12,8},{1,13},{5,1},{9,5},{13,9},{2,14},{6,2},{... | collective-permute-start | bytes 221192 | tf_op jit(solution)/shard_map/ppermute | solution.py:34
  121.6 0.6 copy-start.10
  122.1 0.6 copy-start.11
  152.2 1.5 collective-permute-start.12
  154.5 4.3 %collective-permute-start.15 = (f32[72,128]{1,0:T(8,128)S(1)}, f32[72,128]{1,0:T(8,128)S(1)}, u32[]{:S(2)}, u32[]{:S(2)}) collective-permute-start(f32[72,128]{1,0:T(8,128)S(1)} %add.46), channel_id=1, source_target_pairs={{0,12},{4,0},{8,4},{12,8},{1,13},{5,1},{9,5},{13,9},{2,14},{6,2},{... | collective-permute-start | bytes 110600 | tf_op jit(solution)/shard_map/ppermute | solution.py:34
  157.0 4.0 %collective-permute-start.14 = (f32[72,128]{1,0:T(8,128)S(1)}, f32[72,128]{1,0:T(8,128)S(1)}, u32[]{:S(2)}, u32[]{:S(2)}) collective-permute-start(f32[72,128]{1,0:T(8,128)S(1)} %add.46), channel_id=1, source_target_pairs={{0,8},{4,12},{8,0},{12,4},{1,9},{5,13},{9,1},{13,5},{2,10},{6,14},... | collective-permute-start | bytes 110600 | tf_op jit(solution)/shard_map/ppermute | solution.py:34
  158.0 4.9 %collective-permute-start.13 = (f32[72,128]{1,0:T(8,128)S(1)}, f32[72,128]{1,0:T(8,128)S(1)}, u32[]{:S(2)}, u32[]{:S(2)}) collective-permute-start(f32[72,128]{1,0:T(8,128)S(1)} %add.46), channel_id=1, source_target_pairs={{0,4},{4,8},{8,12},{12,0},{1,5},{5,9},{9,13},{13,1},{2,6},{6,10},{... | collective-permute-start | bytes 110600 | tf_op jit(solution)/shard_map/ppermute | solution.py:34
  162.9 5.7 %collective-permute-start.18 = (f32[72,128]{1,0:T(8,128)S(1)}, f32[72,128]{1,0:T(8,128)S(1)}, u32[]{:S(2)}, u32[]{:S(2)}) collective-permute-start(f32[72,128]{1,0:T(8,128)S(1)} %add_add_fusion.1), channel_id=1, source_target_pairs={{0,3},{1,0},{2,1},{3,2},{4,7},{5,4},{6,5},{7,6},{8,11},{9,8},{10,9... | collective-permute-start | bytes 110600 | tf_op jit(solution)/shard_map/ppermute | solution.py:34
  167.0 4.9 %collective-permute-start.17 = (f32[72,128]{1,0:T(8,128)S(1)}, f32[72,128]{1,0:T(8,128)S(1)}, u32[]{:S(2)}, u32[]{:S(2)}) collective-permute-start(f32[72,128]{1,0:T(8,128)S(1)} %add_add_fusion.1), channel_id=1, source_target_pairs={{0,2},{1,3},{2,0},{3,1},{4,6},{5,7},{6,4},{7,5},{8,10},{9,11},{10,... | collective-permute-start | bytes 110600 | tf_op jit(solution)/shard_map/ppermute | solution.py:34
  167.0 5.8 %collective-permute-start.16 = (f32[72,128]{1,0:T(8,128)S(1)}, f32[72,128]{1,0:T(8,128)S(1)}, u32[]{:S(2)}, u32[]{:S(2)}) collective-permute-start(f32[72,128]{1,0:T(8,128)S(1)} %add_add_fusion.1), channel_id=1, source_target_pairs={{0,1},{1,2},{2,3},{3,0},{4,5},{5,6},{6,7},{7,4},{8,9},{9,10},{10,1... | collective-permute-start | bytes 110600 | tf_op jit(solution)/shard_map/ppermute | solution.py:34

commit v5 on v4

--- a/solution.py
+++ b/solution.py
@@ -24,6 +24,7 @@
 CHUNK_ROWS = 16
 LEAD = 384
 GUARD = 8
+VMEM_BYTES = 40 << 20
 BF16 = jnp.bfloat16
 F32 = jnp.float32
 
@@ -460,7 +461,11 @@
 def back_kernel(plan, last, left, right, above, below, own_ref, goal_ref, extra_ref, before_ref, v_ref, coefs_ref,
                 place_ref, w1, b1, w2, b2, w1b, w2b, w3b, out_ref, low_ref, high_ref, sums_ref, inputs_ref, taps_ref, grads_ref, frame_ref, buffers, rhs_ref, *net_refs):
     rows, cols = plan.rows, plan.cols
-    sums_ref[...] = before_ref[...]
+    if last:
+        sums_ref[...] = jnp.zeros_like(sums_ref)
+        sums_ref[66:67, 64:] = before_ref[...]
+    else:
+        sums_ref[...] = before_ref[...]
     for comp in range(2):
         build_frame(own_ref[comp], (left, right, above, below), comp, frame_ref, comp)
     first, second = project(frame_ref[0], frame_ref[1], buffers, rhs_ref, TOP if last else 24)
@@ -507,11 +512,13 @@
 def finish_kernel(loss_scale, in_ref, w1_ref, b1_ref, w2_ref, b2_ref, w3_ref, loss_ref):
     one = jnp.concatenate([in_ref[8 * tap + 6 : 8 * tap + 8, :64] for tap in range(9)], axis=0)
     three = jnp.concatenate([in_ref[8 * tap : 8 * tap + 6, :64] for tap in range(9)], axis=0)
-    w1_ref[...] = scaled(one, one.size)
+    one, three = scaled(one, one.size), scaled(three, three.size)
+    for tap in range(9):
+        w1_ref[tap // 3, tap % 3] = one[2 * tap : 2 * tap + 2]
+        w3_ref[tap // 3, tap % 3] = three[6 * tap : 6 * tap + 6]
     b1_ref[...] = scaled(in_ref[64:65, 64:], 64)
     b2_ref[...] = scaled(in_ref[65:66, 64:], 64)
     w2_ref[...] = scaled(in_ref[:64, 64:], 64 * 64)
-    w3_ref[...] = scaled(three, three.size)
     loss_ref[...] = (0.5 * loss_scale) * jnp.sum(in_ref[66:67, 64:], axis=1, keepdims=True)
 
 
@@ -534,7 +541,7 @@
             kernel,
             out_shape=[jax.ShapeDtypeStruct(shape, F32 if shape[1] == 128 else kind) for shape in outs],
             scratch_shapes=[pltpu.VMEM(item, F32) if isinstance(item, tuple) else item for item in scratch],
-            compiler_params=pltpu.CompilerParams(vmem_limit_bytes=60 << 20),
+            compiler_params=pltpu.CompilerParams(vmem_limit_bytes=VMEM_BYTES),
         )(*args)
 
     def net_scratch(plan):
@@ -579,11 +586,10 @@
         v_second, forcing, *forward_weights,
     )
     back_scratch = [packed, packed, packed] + sweep_scratch + [(176, 192)] + net_scratch(near)
-    start_sums = jnp.pad(loss_first, ((66, 5), (64, 0)))
     grad, low, high, sums = call(
         functools.partial(back_kernel, near, True),
         [own_pair] + strips(2, 24) + [sums_shape], back_scratch,
-        *exchange([provisional], (low, high)), provisional, last_goal, error_first, start_sums, v_second, coefs_second, place,
+        *exchange([provisional], (low, high)), provisional, last_goal, error_first, loss_first, v_second, coefs_second, place,
         *backward_weights,
     )
     grad, _, _, sums = call(
@@ -597,14 +603,14 @@
     loss_scale = 1.0 / float(step_count * 2 * rows * cols * device_count)
     d1, db1, d2, db2, d3, loss = call(
         functools.partial(finish_kernel, loss_scale),
-        [(18, hid), (1, hid), (hid, hid), (1, hid), (54, hid), (1, 1)], [], sums,
+        [(3, 3, 2, hid), (1, hid), (hid, hid), (1, hid), (3, 3, nout, hid), (1, 1)], [], sums,
     )
     return (
-        d1.reshape(weight_one.shape),
+        d1,
         db1[0],
         d2,
         db2[0],
-        d3.reshape(3, 3, nout, hid).transpose(0, 1, 3, 2),
+        jnp.swapaxes(d3, 2, 3),
         loss[0, 0],
         grad[None],
     )

time: 179 us -> 161 us (0.90)
  Pallas kernels: 104 us -> 90.8 us
  local copies, waits for them, and re-layouts: 9.34 us -> 2.11 us
  waiting for transfers between devices: 31.4 us -> 36.6 us
  other arithmetic: 2.12 us -> 0.15 us
    pallas_call x7, Pallas kernels: 104 us -> 90.8 us  [call(): pl.pallas_call(kernel, out_shape=[jax.ShapeDtypeStruct(shape, F32 if shap...]
    ppermute x19, waiting for transfers between devices: 31.4 us -> 36.6 us  [passed_along(): return lax.ppermute(block, axis, route)]
    reshape x2 -> x0, local copies, waits for them, and re-layouts: 2.68 us -> none  [the longest x1 1.37 us: shards(): d3.reshape(3, 3, nout, hid).transpose(0, 1, 3, 2)]
    slice x3, local copies, waits for them, and re-layouts: 2.36 us -> 0.02 us  [exchange(): mine = jnp.concatenate([own[:, first:first + rim] for own in owns], axis=0)]
  transfers between devices with their start and end apart: 19 -> 19, of which waited for: 19 -> 18; matrix products, arithmetic and copies ran while one was open for 3% -> 0% of each run, Pallas kernels for 1% -> 0%
where the time goes in v5:
time: 161 us
  Pallas kernels  90.8 us (56%)
  waiting for transfers between devices  36.6 us (23%)
  starting transfers between devices  30.1 us (19%)
  local copies, waits for them, and re-layouts  2.11 us (1%)
    pallas_call x7, Pallas kernels, call(): pl.pallas_call(kernel, out_shape=[jax.ShapeDtypeStruct(shape, F32 if shap...  90.8 us
    ppermute x19, waiting for transfers between devices, passed_along(): return lax.ppermute(block, axis, route)  36.6 us
    ppermute x19, starting transfers between devices, passed_along(): return lax.ppermute(block, axis, route)  30.1 us
  transfers between devices with their start and end apart: 19, of which 18 were waited for; matrix products, arithmetic and copies ran while one was open for 0% of the time, Pallas kernels for 0%

profile of v5, /device:TPU:0, one launch (start us, length us, event | category | flops | bytes accessed | tf_op | source)
XLA Modules:
  0.0 160.5 jit_solution(4188881710134451318)
XLA Ops:
  0.7 1.0 copy-done
  1.7 0.9 copy-done.2
  2.7 0.2 shard_map.135
  2.9 3.1 %collective-permute-start = (f32[4,32,256]{2,1,0:T(8,128)S(1)}, f32[4,32,256]{2,1,0:T(8,128)S(1)}, u32[]{:S(2)}, u32[]{:S(2)}) collective-permute-start(f32[4,32,256]{2,1,0:T(8,128)S(1)} %get-tuple-element.38), channel_id=1, source_target_pairs={{0,1},{1,2},{2,3},{3,0},{4,5},{5,6},{6,7},{7,4},{8,9},{9,10},{10,1... | collective-permute-start | bytes 393224 | tf_op jit(solution)/shard_map/ppermute | solution.py:35
  6.0 2.1 %collective-permute-start.1 = (f32[4,32,256]{2,1,0:T(8,128)S(1)}, f32[4,32,256]{2,1,0:T(8,128)S(1)}, u32[]{:S(2)}, u32[]{:S(2)}) collective-permute-start(f32[4,32,256]{2,1,0:T(8,128)S(1)} %get-tuple-element.39), channel_id=1, source_target_pairs={{0,3},{1,0},{2,1},{3,2},{4,7},{5,4},{6,5},{7,6},{8,11},{9,8},{10,9... | collective-permute-start | bytes 393224 | tf_op jit(solution)/shard_map/ppermute | solution.py:35
  8.1 4.2 %collective-permute-done.left = f32[4,32,256]{2,1,0:T(8,128)S(1)} collective-permute-done((f32[4,32,256]{2,1,0:T(8,128)S(1)}, f32[4,32,256]{2,1,0:T(8,128)S(1)}, u32[]{:S(2)}, u32[]{:S(2)}) %collective-permute-start) | collective-permute-done | bytes 131104 | tf_op jit(solution)/shard_map/ppermute | solution.py:35
  12.3 1.4 collective-permute-done.1.right
  13.8 1.5 collective-permute-start.2
  15.3 1.5 collective-permute-start.3
  16.8 0.1 shard_map.136
  17.0 0.1 multiply_sine_fusion.force_ref.goal_ref.extra_ref
  17.0 5.5 %collective-permute-done.2.above = f32[4,96,128]{2,1,0:T(8,128)S(1)} collective-permute-done((f32[4,96,128]{2,1,0:T(8,128)S(1)}, f32[4,96,128]{2,1,0:T(8,128)S(1)}, u32[]{:S(2)}, u32[]{:S(2)}) %collective-permute-start.2) | collective-permute-done | bytes 196640 | tf_op jit(solution)/shard_map/ppermute | solution.py:35
  22.6 2.6 %collective-permute-done.3.below = f32[4,96,128]{2,1,0:T(8,128)S(1)} collective-permute-done((f32[4,96,128]{2,1,0:T(8,128)S(1)}, f32[4,96,128]{2,1,0:T(8,128)S(1)}, u32[]{:S(2)}, u32[]{:S(2)}) %collective-permute-start.3) | collective-permute-done | bytes 196640 | tf_op jit(solution)/shard_map/ppermute | solution.py:35
  25.2 19.2 %shard_map.137 = (f32[2,336,256]{2,1,0:T(8,128)S(1)}, f32[2,336,256]{2,1,0:T(8,128)S(1)}, f32[2,336,256]{2,1,0:T(8,128)S(1)}, f32[2,2688,128]{2,1,0:T(8,128)S(1)...) custom-call(f32[4,32,256]{2,1,0:T(8,128)S(1)} %collective-permute-done.left, ...), custom_call_target="tpu_custom_call" | custom-call | tf_op jit(solution)/shard_map/pallas_call | solution.py:540
  44.4 11.2 %shard_map.138 = (f32[2,256,128]{2,1,0:T(8,128)S(1)}, f32[2,40,256]{2,1,0:T(8,128)S(1)}, f32[2,40,256]{2,1,0:T(8,128)S(1)}, f32[2,2688,128]{2,1,0:T(8,128)S(1)}) custom-call(f32[2,336,256]{2,1,0:T(8,128)S(1)} %get-tuple-element.45.v_ref, f32[1,256]{1,0:T(1,128)S(1)} %multiply_sine_fusion.force_ref.goal_ref.extra_ref, ...), custom_call_target="tpu_custom_call" | custom-call | tf_op jit(solution)/shard_map/pallas_call | solution.py:540
  55.6 1.8 %collective-permute-start.4 = (f32[2,40,256]{2,1,0:T(8,128)S(1)}, f32[2,40,256]{2,1,0:T(8,128)S(1)}, u32[]{:S(2)}, u32[]{:S(2)}) collective-permute-start(f32[2,40,256]{2,1,0:T(8,128)S(1)} %get-tuple-element.46), channel_id=1, source_target_pairs={{0,1},{1,2},{2,3},{3,0},{4,5},{5,6},{6,7},{7,4},{8,9},{9,10},{10,1... | collective-permute-start | bytes 245768 | tf_op jit(solution)/shard_map/ppermute | solution.py:35
  57.4 2.1 %collective-permute-start.5 = (f32[2,40,256]{2,1,0:T(8,128)S(1)}, f32[2,40,256]{2,1,0:T(8,128)S(1)}, u32[]{:S(2)}, u32[]{:S(2)}) collective-permute-start(f32[2,40,256]{2,1,0:T(8,128)S(1)} %get-tuple-element.47), channel_id=1, source_target_pairs={{0,3},{1,0},{2,1},{3,2},{4,7},{5,4},{6,5},{7,6},{8,11},{9,8},{10,9... | collective-permute-start | bytes 245768 | tf_op jit(solution)/shard_map/ppermute | solution.py:35
  59.4 2.6 %collective-permute-done.4.left = f32[2,40,256]{2,1,0:T(8,128)S(1)} collective-permute-done((f32[2,40,256]{2,1,0:T(8,128)S(1)}, f32[2,40,256]{2,1,0:T(8,128)S(1)}, u32[]{:S(2)}, u32[]{:S(2)}) %collective-permute-start.4) | collective-permute-done | bytes 81952 | tf_op jit(solution)/shard_map/ppermute | solution.py:35
  62.0 0.7 collective-permute-done.5.right
  62.7 1.5 collective-permute-start.6
  64.3 1.7 %collective-permute-start.7 = (f32[2,120,128]{2,1,0:T(8,128)S(1)}, f32[2,120,128]{2,1,0:T(8,128)S(1)}, u32[]{:S(2)}, u32[]{:S(2)}) collective-permute-start(f32[2,120,128]{2,1,0:T(8,128)S(1)} %pad_maximum_fusion.3), channel_id=1, source_target_pairs={{0,12},{4,0},{8,4},{12,8},{1,13},{5,1},{9,5},{13,9},{2,14},{6,2},{... | collective-permute-start | bytes 368648 | tf_op jit(solution)/shard_map/ppermute | solution.py:35
  65.9 2.6 %collective-permute-done.6.above = f32[2,120,128]{2,1,0:T(8,128)S(1)} collective-permute-done((f32[2,120,128]{2,1,0:T(8,128)S(1)}, f32[2,120,128]{2,1,0:T(8,128)S(1)}, u32[]{:S(2)}, u32[]{:S(2)}) %collective-permute-start.6) | collective-permute-done | bytes 122912 | tf_op jit(solution)/shard_map/ppermute | solution.py:35
  68.5 0.8 collective-permute-done.7.below
  69.4 31.4 %shard_map.139 = (f32[2,256,128]{2,1,0:T(8,128)S(1)}, f32[2,24,256]{2,1,0:T(8,128)S(1)}, f32[2,24,256]{2,1,0:T(8,128)S(1)}, f32[72,128]{1,0:T(8,128)S(1)}) custom-call(f32[2,40,256]{2,1,0:T(8,128)S(1)} %collective-permute-done.4.left, f32[2,40,256]{2,1,0:T(8,128)S(1)} %collective-permute-done.5.right, f32[2,120,128]{2,1,0:T(8,128)S(1)} %collective-permute-done.6.above, ...), custom_call_target="tpu_custom_call" | custom-call | tf_op jit(solution)/shard_map/pallas_call | solution.py:540
  100.7 0.1 collective-permute-start.8
  100.9 3.7 %collective-permute-start.9 = (f32[2,24,256]{2,1,0:T(8,128)S(1)}, f32[2,24,256]{2,1,0:T(8,128)S(1)}, u32[]{:S(2)}, u32[]{:S(2)}) collective-permute-start(f32[2,24,256]{2,1,0:T(8,128)S(1)} %get-tuple-element.56), channel_id=1, source_target_pairs={{0,3},{1,0},{2,1},{3,2},{4,7},{5,4},{6,5},{7,6},{8,11},{9,8},{10,9... | collective-permute-start | bytes 147464 | tf_op jit(solution)/shard_map/ppermute | solution.py:35
  104.6 2.2 %collective-permute-done.8.left = f32[2,24,256]{2,1,0:T(8,128)S(1)} collective-permute-done((f32[2,24,256]{2,1,0:T(8,128)S(1)}, f32[2,24,256]{2,1,0:T(8,128)S(1)}, u32[]{:S(2)}, u32[]{:S(2)}) %collective-permute-start.8) | collective-permute-done | bytes 49184 | tf_op jit(solution)/shard_map/ppermute | solution.py:35
  106.8 0.0 collective-permute-done.9.right
  106.8 1.4 collective-permute-start.10
  108.3 1.5 collective-permute-start.11
  109.8 2.3 %collective-permute-done.10.above = f32[2,72,128]{2,1,0:T(8,128)S(1)} collective-permute-done((f32[2,72,128]{2,1,0:T(8,128)S(1)}, f32[2,72,128]{2,1,0:T(8,128)S(1)}, u32[]{:S(2)}, u32[]{:S(2)}) %collective-permute-start.10) | collective-permute-done | bytes 73760 | tf_op jit(solution)/shard_map/ppermute | solution.py:35
  112.1 0.5 collective-permute-done.11.below
  112.6 27.5 %shard_map.140 = (f32[2,256,128]{2,1,0:T(8,128)}, f32[1,8,128]{2,1,0:T(8,128)}, f32[1,8,128]{2,1,0:T(8,128)}, f32[72,128]{1,0:T(8,128)S(1)}) custom-call(f32[2,24,256]{2,1,0:T(8,128)S(1)} %collective-permute-done.8.left, f32[2,24,256]{2,1,0:T(8,128)S(1)} %collective-permute-done.9.right, f32[2,72,128]{2,1,0:T(8,128)S(1)} %collective-permute-done.10.above, ...), custom_call_target="tpu_custom_call" | custom-call | tf_op jit(solution)/shard_map/pallas_call | solution.py:540
  140.2 0.0 collective-permute-start.12
  140.2 1.2 collective-permute-done.12
  141.4 2.4 %collective-permute-start.15 = (f32[72,128]{1,0:T(8,128)S(1)}, f32[72,128]{1,0:T(8,128)S(1)}, u32[]{:S(2)}, u32[]{:S(2)}) collective-permute-start(f32[72,128]{1,0:T(8,128)S(1)} %add.44), channel_id=1, source_target_pairs={{0,12},{4,0},{8,4},{12,8},{1,13},{5,1},{9,5},{13,9},{2,14},{6,2},{... | collective-permute-start | bytes 110600 | tf_op jit(solution)/shard_map/ppermute | solution.py:35
  143.8 1.0 collective-permute-start.14
  144.9 0.1 collective-permute-start.13
  144.9 0.8 collective-permute-done.15
  145.7 2.1 %collective-permute-done.14 = f32[72,128]{1,0:T(8,128)S(1)} collective-permute-done((f32[72,128]{1,0:T(8,128)S(1)}, f32[72,128]{1,0:T(8,128)S(1)}, u32[]{:S(2)}, u32[]{:S(2)}) %collective-permute-start.14) | collective-permute-done | bytes 36896 | tf_op jit(solution)/shard_map/ppermute | solution.py:35
  147.8 1.9 %collective-permute-done.13 = f32[72,128]{1,0:T(8,128)S(1)} collective-permute-done((f32[72,128]{1,0:T(8,128)S(1)}, f32[72,128]{1,0:T(8,128)S(1)}, u32[]{:S(2)}, u32[]{:S(2)}) %collective-permute-start.13) | collective-permute-done | bytes 36896 | tf_op jit(solution)/shard_map/ppermute | solution.py:35
  149.7 3.7 %collective-permute-start.18 = (f32[72,128]{1,0:T(8,128)S(1)}, f32[72,128]{1,0:T(8,128)S(1)}, u32[]{:S(2)}, u32[]{:S(2)}) collective-permute-start(f32[72,128]{1,0:T(8,128)S(1)} %add_add_fusion.1), channel_id=1, source_target_pairs={{0,3},{1,0},{2,1},{3,2},{4,7},{5,4},{6,5},{7,6},{8,11},{9,8},{10,9... | collective-permute-start | bytes 110600 | tf_op jit(solution)/shard_map/ppermute | solution.py:35
  153.5 0.0 collective-permute-start.17
  153.5 0.6 collective-permute-start.16
  154.1 1.0 collective-permute-done.18
  155.1 3.2 %collective-permute-done.17 = f32[72,128]{1,0:T(8,128)S(1)} collective-permute-done((f32[72,128]{1,0:T(8,128)S(1)}, f32[72,128]{1,0:T(8,128)S(1)}, u32[]{:S(2)}, u32[]{:S(2)}) %collective-permute-start.17) | collective-permute-done | bytes 36896 | tf_op jit(solution)/shard_map/ppermute | solution.py:35
  158.4 0.9 collective-permute-done.16
  159.3 1.2 shard_map.141
  (37 shorter events, 0.2 us)
Async XLA Ops:
  0.6 16.2 %copy-start.9 = (f32[64]{0:T(128)S(1)}, f32[64]{0:T(128)}, u32[]{:S(2)}) copy-start(f32[64]{0:T(128)} %param.13) | copy-start | bytes 772
  0.6 16.2 %copy-start.8 = (f32[64]{0:T(128)S(1)}, f32[64]{0:T(128)}, u32[]{:S(2)}) copy-start(f32[64]{0:T(128)} %param.11) | copy-start | bytes 772
  0.7 1.1 copy-start
  1.7 0.9 copy-start.2
  2.7 14.2 %copy-start.5 = (bf16[64,64]{1,0:T(8,128)(2,1)S(1)}, bf16[64,64]{1,0:T(8,128)(2,1)}, u32[]{:S(2)}) copy-start(bf16[64,64]{1,0:T(8,128)(2,1)} %w2b.3) | copy-start | bytes 24580
  2.7 14.2 %copy-start.6 = (bf16[3,3,64,6]{2,3,1,0:T(8,128)(2,1)S(1)}, bf16[3,3,64,6]{2,3,1,0:T(8,128)(2,1)}, u32[]{:S(2)}) copy-start(bf16[3,3,64,6]{2,3,1,0:T(8,128)(2,1)} %param.14) | copy-start | bytes 20740
  2.7 14.2 %copy-start.7 = (bf16[3,3,2,64]{3,2,1,0:T(2,128)(2,1)S(1)}, bf16[3,3,2,64]{3,2,1,0:T(2,128)(2,1)}, u32[]{:S(2)}) copy-start(bf16[3,3,2,64]{3,2,1,0:T(2,128)(2,1)} %w1_in.1) | copy-start | bytes 6916
  2.7 22.5 %copy-start.1 = (f32[1,2,2,256,128]{4,3,2,1,0:T(8,128)S(1)}, f32[1,2,2,256,128]{4,3,2,1,0:T(8,128)}, u32[]{:S(2)}) copy-start(f32[1,2,2,256,128]{4,3,2,1,0:T(8,128)} %param.9) | copy-start | bytes 1572868
  2.7 22.5 %copy-start.3 = (f32[1,2,256,128]{3,2,1,0:T(8,128)S(1)}, f32[1,2,256,128]{3,2,1,0:T(8,128)}, u32[]{:S(2)}) copy-start(f32[1,2,256,128]{3,2,1,0:T(8,128)} %param.8) | copy-start | bytes 786436
  2.9 9.4 %collective-permute-start = (f32[4,32,256]{2,1,0:T(8,128)S(1)}, f32[4,32,256]{2,1,0:T(8,128)S(1)}, u32[]{:S(2)}, u32[]{:S(2)}) collective-permute-start(f32[4,32,256]{2,1,0:T(8,128)S(1)} %get-tuple-element.38), channel_id=1, source_target_pairs={{0,1},{1,2},{2,3},{3,0},{4,5},{5,6},{6,7},{7,4},{8,9},{9,10},{10,1... | collective-permute-start | bytes 393224 | tf_op jit(solution)/shard_map/ppermute | solution.py:35
  6.0 63.4 %copy-start.4 = (s32[16,2176]{1,0:T(8,128)S(1)}, s32[16,2176]{1,0:T(8,128)}, u32[]{:S(2)}) copy-start(s32[16,2176]{1,0:T(8,128)} %constant.13.clone.place_ref) | copy-start | bytes 417796
  6.0 7.8 %collective-permute-start.1 = (f32[4,32,256]{2,1,0:T(8,128)S(1)}, f32[4,32,256]{2,1,0:T(8,128)S(1)}, u32[]{:S(2)}, u32[]{:S(2)}) collective-permute-start(f32[4,32,256]{2,1,0:T(8,128)S(1)} %get-tuple-element.39), channel_id=1, source_target_pairs={{0,3},{1,0},{2,1},{3,2},{4,7},{5,4},{6,5},{7,6},{8,11},{9,8},{10,9... | collective-permute-start | bytes 393224 | tf_op jit(solution)/shard_map/ppermute | solution.py:35
  13.8 8.8 %collective-permute-start.2 = (f32[4,96,128]{2,1,0:T(8,128)S(1)}, f32[4,96,128]{2,1,0:T(8,128)S(1)}, u32[]{:S(2)}, u32[]{:S(2)}) collective-permute-start(f32[4,96,128]{2,1,0:T(8,128)S(1)} %pad_maximum_fusion), channel_id=1, source_target_pairs={{0,4},{4,8},{8,12},{12,0},{1,5},{5,9},{9,13},{13,1},{2,6},{6,10},{... | collective-permute-start | bytes 589832 | tf_op jit(solution)/shard_map/ppermute | solution.py:35
  15.3 9.9 %collective-permute-start.3 = (f32[4,96,128]{2,1,0:T(8,128)S(1)}, f32[4,96,128]{2,1,0:T(8,128)S(1)}, u32[]{:S(2)}, u32[]{:S(2)}) collective-permute-start(f32[4,96,128]{2,1,0:T(8,128)S(1)} %pad_maximum_fusion.1), channel_id=1, source_target_pairs={{0,12},{4,0},{8,4},{12,8},{1,13},{5,1},{9,5},{13,9},{2,14},{6,2},{... | collective-permute-start | bytes 589832 | tf_op jit(solution)/shard_map/ppermute | solution.py:35
  55.6 6.5 %collective-permute-start.4 = (f32[2,40,256]{2,1,0:T(8,128)S(1)}, f32[2,40,256]{2,1,0:T(8,128)S(1)}, u32[]{:S(2)}, u32[]{:S(2)}) collective-permute-start(f32[2,40,256]{2,1,0:T(8,128)S(1)} %get-tuple-element.46), channel_id=1, source_target_pairs={{0,1},{1,2},{2,3},{3,0},{4,5},{5,6},{6,7},{7,4},{8,9},{9,10},{10,1... | collective-permute-start | bytes 245768 | tf_op jit(solution)/shard_map/ppermute | solution.py:35
  57.4 5.3 %collective-permute-start.5 = (f32[2,40,256]{2,1,0:T(8,128)S(1)}, f32[2,40,256]{2,1,0:T(8,128)S(1)}, u32[]{:S(2)}, u32[]{:S(2)}) collective-permute-start(f32[2,40,256]{2,1,0:T(8,128)S(1)} %get-tuple-element.47), channel_id=1, source_target_pairs={{0,3},{1,0},{2,1},{3,2},{4,7},{5,4},{6,5},{7,6},{8,11},{9,8},{10,9... | collective-permute-start | bytes 245768 | tf_op jit(solution)/shard_map/ppermute | solution.py:35
  62.7 5.8 %collective-permute-start.6 = (f32[2,120,128]{2,1,0:T(8,128)S(1)}, f32[2,120,128]{2,1,0:T(8,128)S(1)}, u32[]{:S(2)}, u32[]{:S(2)}) collective-permute-start(f32[2,120,128]{2,1,0:T(8,128)S(1)} %pad_maximum_fusion.2), channel_id=1, source_target_pairs={{0,4},{4,8},{8,12},{12,0},{1,5},{5,9},{9,13},{13,1},{2,6},{6,10},{... | collective-permute-start | bytes 368648 | tf_op jit(solution)/shard_map/ppermute | solution.py:35
  64.3 5.1 %collective-permute-start.7 = (f32[2,120,128]{2,1,0:T(8,128)S(1)}, f32[2,120,128]{2,1,0:T(8,128)S(1)}, u32[]{:S(2)}, u32[]{:S(2)}) collective-permute-start(f32[2,120,128]{2,1,0:T(8,128)S(1)} %pad_maximum_fusion.3), channel_id=1, source_target_pairs={{0,12},{4,0},{8,4},{12,8},{1,13},{5,1},{9,5},{13,9},{2,14},{6,2},{... | collective-permute-start | bytes 368648 | tf_op jit(solution)/shard_map/ppermute | solution.py:35
  100.7 6.0 %collective-permute-start.8 = (f32[2,24,256]{2,1,0:T(8,128)S(1)}, f32[2,24,256]{2,1,0:T(8,128)S(1)}, u32[]{:S(2)}, u32[]{:S(2)}) collective-permute-start(f32[2,24,256]{2,1,0:T(8,128)S(1)} %get-tuple-element.55), channel_id=1, source_target_pairs={{0,1},{1,2},{2,3},{3,0},{4,5},{5,6},{6,7},{7,4},{8,9},{9,10},{10,1... | collective-permute-start | bytes 147464 | tf_op jit(solution)/shard_map/ppermute | solution.py:35
  100.9 5.9 %collective-permute-start.9 = (f32[2,24,256]{2,1,0:T(8,128)S(1)}, f32[2,24,256]{2,1,0:T(8,128)S(1)}, u32[]{:S(2)}, u32[]{:S(2)}) collective-permute-start(f32[2,24,256]{2,1,0:T(8,128)S(1)} %get-tuple-element.56), channel_id=1, source_target_pairs={{0,3},{1,0},{2,1},{3,2},{4,7},{5,4},{6,5},{7,6},{8,11},{9,8},{10,9... | collective-permute-start | bytes 147464 | tf_op jit(solution)/shard_map/ppermute | solution.py:35
  106.8 5.3 %collective-permute-start.10 = (f32[2,72,128]{2,1,0:T(8,128)S(1)}, f32[2,72,128]{2,1,0:T(8,128)S(1)}, u32[]{:S(2)}, u32[]{:S(2)}) collective-permute-start(f32[2,72,128]{2,1,0:T(8,128)S(1)} %pad_maximum_fusion.4), channel_id=1, source_target_pairs={{0,4},{4,8},{8,12},{12,0},{1,5},{5,9},{9,13},{13,1},{2,6},{6,10},{... | collective-permute-start | bytes 221192 | tf_op jit(solution)/shard_map/ppermute | solution.py:35
  108.3 4.4 %collective-permute-start.11 = (f32[2,72,128]{2,1,0:T(8,128)S(1)}, f32[2,72,128]{2,1,0:T(8,128)S(1)}, u32[]{:S(2)}, u32[]{:S(2)}) collective-permute-start(f32[2,72,128]{2,1,0:T(8,128)S(1)} %pad_maximum_fusion.5), channel_id=1, source_target_pairs={{0,12},{4,0},{8,4},{12,8},{1,13},{5,1},{9,5},{13,9},{2,14},{6,2},{... | collective-permute-start | bytes 221192 | tf_op jit(solution)/shard_map/ppermute | solution.py:35
  140.2 1.2 collective-permute-start.12
  141.4 4.3 %collective-permute-start.15 = (f32[72,128]{1,0:T(8,128)S(1)}, f32[72,128]{1,0:T(8,128)S(1)}, u32[]{:S(2)}, u32[]{:S(2)}) collective-permute-start(f32[72,128]{1,0:T(8,128)S(1)} %add.44), channel_id=1, source_target_pairs={{0,12},{4,0},{8,4},{12,8},{1,13},{5,1},{9,5},{13,9},{2,14},{6,2},{... | collective-permute-start | bytes 110600 | tf_op jit(solution)/shard_map/ppermute | solution.py:35
  143.8 4.0 %collective-permute-start.14 = (f32[72,128]{1,0:T(8,128)S(1)}, f32[72,128]{1,0:T(8,128)S(1)}, u32[]{:S(2)}, u32[]{:S(2)}) collective-permute-start(f32[72,128]{1,0:T(8,128)S(1)} %add.44), channel_id=1, source_target_pairs={{0,8},{4,12},{8,0},{12,4},{1,9},{5,13},{9,1},{13,5},{2,10},{6,14},... | collective-permute-start | bytes 110600 | tf_op jit(solution)/shard_map/ppermute | solution.py:35
  144.9 4.9 %collective-permute-start.13 = (f32[72,128]{1,0:T(8,128)S(1)}, f32[72,128]{1,0:T(8,128)S(1)}, u32[]{:S(2)}, u32[]{:S(2)}) collective-permute-start(f32[72,128]{1,0:T(8,128)S(1)} %add.44), channel_id=1, source_target_pairs={{0,4},{4,8},{8,12},{12,0},{1,5},{5,9},{9,13},{13,1},{2,6},{6,10},{... | collective-permute-start | bytes 110600 | tf_op jit(solution)/shard_map/ppermute | solution.py:35
  149.7 5.4 %collective-permute-start.18 = (f32[72,128]{1,0:T(8,128)S(1)}, f32[72,128]{1,0:T(8,128)S(1)}, u32[]{:S(2)}, u32[]{:S(2)}) collective-permute-start(f32[72,128]{1,0:T(8,128)S(1)} %add_add_fusion.1), channel_id=1, source_target_pairs={{0,3},{1,0},{2,1},{3,2},{4,7},{5,4},{6,5},{7,6},{8,11},{9,8},{10,9... | collective-permute-start | bytes 110600 | tf_op jit(solution)/shard_map/ppermute | solution.py:35
  153.5 4.9 %collective-permute-start.17 = (f32[72,128]{1,0:T(8,128)S(1)}, f32[72,128]{1,0:T(8,128)S(1)}, u32[]{:S(2)}, u32[]{:S(2)}) collective-permute-start(f32[72,128]{1,0:T(8,128)S(1)} %add_add_fusion.1), channel_id=1, source_target_pairs={{0,2},{1,3},{2,0},{3,1},{4,6},{5,7},{6,4},{7,5},{8,10},{9,11},{10,... | collective-permute-start | bytes 110600 | tf_op jit(solution)/shard_map/ppermute | solution.py:35
  153.5 5.8 %collective-permute-start.16 = (f32[72,128]{1,0:T(8,128)S(1)}, f32[72,128]{1,0:T(8,128)S(1)}, u32[]{:S(2)}, u32[]{:S(2)}) collective-permute-start(f32[72,128]{1,0:T(8,128)S(1)} %add_add_fusion.1), channel_id=1, source_target_pairs={{0,1},{1,2},{2,3},{3,0},{4,5},{5,6},{6,7},{7,4},{8,9},{9,10},{10,1... | collective-permute-start | bytes 110600 | tf_op jit(solution)/shard_map/ppermute | solution.py:35

commit v6 on v5

--- a/solution.py
+++ b/solution.py
@@ -24,6 +24,7 @@
 CHUNK_ROWS = 16
 LEAD = 384
 GUARD = 8
+GROUP = 4
 VMEM_BYTES = 40 << 20
 BF16 = jnp.bfloat16
 F32 = jnp.float32
@@ -371,9 +372,14 @@
         split_rows(total, grads_ref, plan.in_row + row, plan.in_lane, plan.wide)
         return carried
 
-    lax.fori_loop(0, plan.chunks // 2, lambda pair, carried: one_chunk(2 * pair + 1, one_chunk(2 * pair, carried)), 0)
-    if plan.chunks % 2:
-        one_chunk(plan.chunks - 1, 0)
+    def one_group(group, carried):
+        for number in range(GROUP):
+            one_chunk(GROUP * group + number, carried)
+        return carried
+
+    lax.fori_loop(0, plan.chunks // GROUP, one_group, 0)
+    for number in range(plan.chunks // GROUP * GROUP, plan.chunks):
+        one_chunk(number, 0)
     for tap in range(9):
         taken = 144 + 8 * (tap // 3) + 2 * (tap % 3)
         sums_ref[8 * tap : 8 * tap + 6, :64] += cross_ref[8 * tap : 8 * tap + 6, :64]

time: 161 us -> 158 us (0.981)
  Pallas kernels: 90.8 us -> 88.3 us
    pallas_call x7, Pallas kernels: 90.8 us -> 88.3 us  [call(): pl.pallas_call(kernel, out_shape=[jax.ShapeDtypeStruct(shape, F32 if shap...]
where the time goes in v6:
time: 158 us
  Pallas kernels  88.3 us (56%)
  waiting for transfers between devices  36.5 us (23%)
  starting transfers between devices  30.1 us (19%)
  local copies, waits for them, and re-layouts  2.11 us (1%)
    pallas_call x7, Pallas kernels, call(): pl.pallas_call(kernel, out_shape=[jax.ShapeDtypeStruct(shape, F32 if shap...  88.3 us
    ppermute x19, waiting for transfers between devices, passed_along(): return lax.ppermute(block, axis, route)  36.5 us
    ppermute x19, starting transfers between devices, passed_along(): return lax.ppermute(block, axis, route)  30.1 us
  transfers between devices with their start and end apart: 19, of which 18 were waited for; matrix products, arithmetic and copies ran while one was open for 0% of the time, Pallas kernels for 0%

profile of v6, /device:TPU:0, one launch (start us, length us, event | category | flops | bytes accessed | tf_op | source)
XLA Modules:
  0.0 158.0 jit_solution(3297376695126904403)
XLA Ops:
  0.7 1.0 copy-done
  1.7 0.9 copy-done.2
  2.7 0.2 shard_map.135
  2.9 3.1 %collective-permute-start = (f32[4,32,256]{2,1,0:T(8,128)S(1)}, f32[4,32,256]{2,1,0:T(8,128)S(1)}, u32[]{:S(2)}, u32[]{:S(2)}) collective-permute-start(f32[4,32,256]{2,1,0:T(8,128)S(1)} %get-tuple-element.38), channel_id=1, source_target_pairs={{0,1},{1,2},{2,3},{3,0},{4,5},{5,6},{6,7},{7,4},{8,9},{9,10},{10,1... | collective-permute-start | bytes 393224 | tf_op jit(solution)/shard_map/ppermute | solution.py:36
  6.0 2.1 %collective-permute-start.1 = (f32[4,32,256]{2,1,0:T(8,128)S(1)}, f32[4,32,256]{2,1,0:T(8,128)S(1)}, u32[]{:S(2)}, u32[]{:S(2)}) collective-permute-start(f32[4,32,256]{2,1,0:T(8,128)S(1)} %get-tuple-element.39), channel_id=1, source_target_pairs={{0,3},{1,0},{2,1},{3,2},{4,7},{5,4},{6,5},{7,6},{8,11},{9,8},{10,9... | collective-permute-start | bytes 393224 | tf_op jit(solution)/shard_map/ppermute | solution.py:36
  8.1 4.2 %collective-permute-done.left = f32[4,32,256]{2,1,0:T(8,128)S(1)} collective-permute-done((f32[4,32,256]{2,1,0:T(8,128)S(1)}, f32[4,32,256]{2,1,0:T(8,128)S(1)}, u32[]{:S(2)}, u32[]{:S(2)}) %collective-permute-start) | collective-permute-done | bytes 131104 | tf_op jit(solution)/shard_map/ppermute | solution.py:36
  12.3 1.4 collective-permute-done.1.right
  13.8 1.5 collective-permute-start.2
  15.3 1.5 collective-permute-start.3
  16.8 0.1 shard_map.136
  17.0 0.1 multiply_sine_fusion.force_ref.goal_ref.extra_ref
  17.0 5.5 %collective-permute-done.2.above = f32[4,96,128]{2,1,0:T(8,128)S(1)} collective-permute-done((f32[4,96,128]{2,1,0:T(8,128)S(1)}, f32[4,96,128]{2,1,0:T(8,128)S(1)}, u32[]{:S(2)}, u32[]{:S(2)}) %collective-permute-start.2) | collective-permute-done | bytes 196640 | tf_op jit(solution)/shard_map/ppermute | solution.py:36
  22.6 2.6 %collective-permute-done.3.below = f32[4,96,128]{2,1,0:T(8,128)S(1)} collective-permute-done((f32[4,96,128]{2,1,0:T(8,128)S(1)}, f32[4,96,128]{2,1,0:T(8,128)S(1)}, u32[]{:S(2)}, u32[]{:S(2)}) %collective-permute-start.3) | collective-permute-done | bytes 196640 | tf_op jit(solution)/shard_map/ppermute | solution.py:36
  25.2 19.2 %shard_map.137 = (f32[2,336,256]{2,1,0:T(8,128)S(1)}, f32[2,336,256]{2,1,0:T(8,128)S(1)}, f32[2,336,256]{2,1,0:T(8,128)S(1)}, f32[2,2688,128]{2,1,0:T(8,128)S(1)...) custom-call(f32[4,32,256]{2,1,0:T(8,128)S(1)} %collective-permute-done.left, ...), custom_call_target="tpu_custom_call" | custom-call | tf_op jit(solution)/shard_map/pallas_call | solution.py:546
  44.4 11.2 %shard_map.138 = (f32[2,256,128]{2,1,0:T(8,128)S(1)}, f32[2,40,256]{2,1,0:T(8,128)S(1)}, f32[2,40,256]{2,1,0:T(8,128)S(1)}, f32[2,2688,128]{2,1,0:T(8,128)S(1)}) custom-call(f32[2,336,256]{2,1,0:T(8,128)S(1)} %get-tuple-element.45.v_ref, f32[1,256]{1,0:T(1,128)S(1)} %multiply_sine_fusion.force_ref.goal_ref.extra_ref, ...), custom_call_target="tpu_custom_call" | custom-call | tf_op jit(solution)/shard_map/pallas_call | solution.py:546
  55.6 1.8 %collective-permute-start.4 = (f32[2,40,256]{2,1,0:T(8,128)S(1)}, f32[2,40,256]{2,1,0:T(8,128)S(1)}, u32[]{:S(2)}, u32[]{:S(2)}) collective-permute-start(f32[2,40,256]{2,1,0:T(8,128)S(1)} %get-tuple-element.46), channel_id=1, source_target_pairs={{0,1},{1,2},{2,3},{3,0},{4,5},{5,6},{6,7},{7,4},{8,9},{9,10},{10,1... | collective-permute-start | bytes 245768 | tf_op jit(solution)/shard_map/ppermute | solution.py:36
  57.4 2.1 %collective-permute-start.5 = (f32[2,40,256]{2,1,0:T(8,128)S(1)}, f32[2,40,256]{2,1,0:T(8,128)S(1)}, u32[]{:S(2)}, u32[]{:S(2)}) collective-permute-start(f32[2,40,256]{2,1,0:T(8,128)S(1)} %get-tuple-element.47), channel_id=1, source_target_pairs={{0,3},{1,0},{2,1},{3,2},{4,7},{5,4},{6,5},{7,6},{8,11},{9,8},{10,9... | collective-permute-start | bytes 245768 | tf_op jit(solution)/shard_map/ppermute | solution.py:36
  59.4 2.6 %collective-permute-done.4.left = f32[2,40,256]{2,1,0:T(8,128)S(1)} collective-permute-done((f32[2,40,256]{2,1,0:T(8,128)S(1)}, f32[2,40,256]{2,1,0:T(8,128)S(1)}, u32[]{:S(2)}, u32[]{:S(2)}) %collective-permute-start.4) | collective-permute-done | bytes 81952 | tf_op jit(solution)/shard_map/ppermute | solution.py:36
  62.0 0.7 collective-permute-done.5.right
  62.7 1.5 collective-permute-start.6
  64.3 1.7 %collective-permute-start.7 = (f32[2,120,128]{2,1,0:T(8,128)S(1)}, f32[2,120,128]{2,1,0:T(8,128)S(1)}, u32[]{:S(2)}, u32[]{:S(2)}) collective-permute-start(f32[2,120,128]{2,1,0:T(8,128)S(1)} %pad_maximum_fusion.3), channel_id=1, source_target_pairs={{0,12},{4,0},{8,4},{12,8},{1,13},{5,1},{9,5},{13,9},{2,14},{6,2},{... | collective-permute-start | bytes 368648 | tf_op jit(solution)/shard_map/ppermute | solution.py:36
  65.9 2.6 %collective-permute-done.6.above = f32[2,120,128]{2,1,0:T(8,128)S(1)} collective-permute-done((f32[2,120,128]{2,1,0:T(8,128)S(1)}, f32[2,120,128]{2,1,0:T(8,128)S(1)}, u32[]{:S(2)}, u32[]{:S(2)}) %collective-permute-start.6) | collective-permute-done | bytes 122912 | tf_op jit(solution)/shard_map/ppermute | solution.py:36
  68.5 0.8 collective-permute-done.7.below
  69.4 30.1 %shard_map.139 = (f32[2,256,128]{2,1,0:T(8,128)S(1)}, f32[2,24,256]{2,1,0:T(8,128)S(1)}, f32[2,24,256]{2,1,0:T(8,128)S(1)}, f32[72,128]{1,0:T(8,128)S(1)}) custom-call(f32[2,40,256]{2,1,0:T(8,128)S(1)} %collective-permute-done.4.left, f32[2,40,256]{2,1,0:T(8,128)S(1)} %collective-permute-done.5.right, f32[2,120,128]{2,1,0:T(8,128)S(1)} %collective-permute-done.6.above, ...), custom_call_target="tpu_custom_call" | custom-call | tf_op jit(solution)/shard_map/pallas_call | solution.py:546
  99.5 0.1 collective-permute-start.8
  99.6 3.8 %collective-permute-start.9 = (f32[2,24,256]{2,1,0:T(8,128)S(1)}, f32[2,24,256]{2,1,0:T(8,128)S(1)}, u32[]{:S(2)}, u32[]{:S(2)}) collective-permute-start(f32[2,24,256]{2,1,0:T(8,128)S(1)} %get-tuple-element.56), channel_id=1, source_target_pairs={{0,3},{1,0},{2,1},{3,2},{4,7},{5,4},{6,5},{7,6},{8,11},{9,8},{10,9... | collective-permute-start | bytes 147464 | tf_op jit(solution)/shard_map/ppermute | solution.py:36
  103.3 2.2 %collective-permute-done.8.left = f32[2,24,256]{2,1,0:T(8,128)S(1)} collective-permute-done((f32[2,24,256]{2,1,0:T(8,128)S(1)}, f32[2,24,256]{2,1,0:T(8,128)S(1)}, u32[]{:S(2)}, u32[]{:S(2)}) %collective-permute-start.8) | collective-permute-done | bytes 49184 | tf_op jit(solution)/shard_map/ppermute | solution.py:36
  105.5 0.0 collective-permute-done.9.right
  105.6 1.4 collective-permute-start.10
  107.0 1.5 collective-permute-start.11
  108.5 2.3 %collective-permute-done.10.above = f32[2,72,128]{2,1,0:T(8,128)S(1)} collective-permute-done((f32[2,72,128]{2,1,0:T(8,128)S(1)}, f32[2,72,128]{2,1,0:T(8,128)S(1)}, u32[]{:S(2)}, u32[]{:S(2)}) %collective-permute-start.10) | collective-permute-done | bytes 73760 | tf_op jit(solution)/shard_map/ppermute | solution.py:36
  110.9 0.5 collective-permute-done.11.below
  111.3 26.3 %shard_map.140 = (f32[2,256,128]{2,1,0:T(8,128)}, f32[1,8,128]{2,1,0:T(8,128)}, f32[1,8,128]{2,1,0:T(8,128)}, f32[72,128]{1,0:T(8,128)S(1)}) custom-call(f32[2,24,256]{2,1,0:T(8,128)S(1)} %collective-permute-done.8.left, f32[2,24,256]{2,1,0:T(8,128)S(1)} %collective-permute-done.9.right, f32[2,72,128]{2,1,0:T(8,128)S(1)} %collective-permute-done.10.above, ...), custom_call_target="tpu_custom_call" | custom-call | tf_op jit(solution)/shard_map/pallas_call | solution.py:546
  137.7 0.0 collective-permute-start.12
  137.7 1.2 collective-permute-done.12
  138.9 2.4 %collective-permute-start.15 = (f32[72,128]{1,0:T(8,128)S(1)}, f32[72,128]{1,0:T(8,128)S(1)}, u32[]{:S(2)}, u32[]{:S(2)}) collective-permute-start(f32[72,128]{1,0:T(8,128)S(1)} %add.44), channel_id=1, source_target_pairs={{0,12},{4,0},{8,4},{12,8},{1,13},{5,1},{9,5},{13,9},{2,14},{6,2},{... | collective-permute-start | bytes 110600 | tf_op jit(solution)/shard_map/ppermute | solution.py:36
  141.3 1.0 collective-permute-start.14
  142.4 0.1 collective-permute-start.13
  142.4 0.7 collective-permute-done.15
  143.2 2.1 %collective-permute-done.14 = f32[72,128]{1,0:T(8,128)S(1)} collective-permute-done((f32[72,128]{1,0:T(8,128)S(1)}, f32[72,128]{1,0:T(8,128)S(1)}, u32[]{:S(2)}, u32[]{:S(2)}) %collective-permute-start.14) | collective-permute-done | bytes 36896 | tf_op jit(solution)/shard_map/ppermute | solution.py:36
  145.3 1.9 %collective-permute-done.13 = f32[72,128]{1,0:T(8,128)S(1)} collective-permute-done((f32[72,128]{1,0:T(8,128)S(1)}, f32[72,128]{1,0:T(8,128)S(1)}, u32[]{:S(2)}, u32[]{:S(2)}) %collective-permute-start.13) | collective-permute-done | bytes 36896 | tf_op jit(solution)/shard_map/ppermute | solution.py:36
  147.2 3.7 %collective-permute-start.18 = (f32[72,128]{1,0:T(8,128)S(1)}, f32[72,128]{1,0:T(8,128)S(1)}, u32[]{:S(2)}, u32[]{:S(2)}) collective-permute-start(f32[72,128]{1,0:T(8,128)S(1)} %add_add_fusion.1), channel_id=1, source_target_pairs={{0,3},{1,0},{2,1},{3,2},{4,7},{5,4},{6,5},{7,6},{8,11},{9,8},{10,9... | collective-permute-start | bytes 110600 | tf_op jit(solution)/shard_map/ppermute | solution.py:36
  151.0 0.0 collective-permute-start.17
  151.0 0.6 collective-permute-start.16
  151.6 1.0 collective-permute-done.18
  152.6 3.2 %collective-permute-done.17 = f32[72,128]{1,0:T(8,128)S(1)} collective-permute-done((f32[72,128]{1,0:T(8,128)S(1)}, f32[72,128]{1,0:T(8,128)S(1)}, u32[]{:S(2)}, u32[]{:S(2)}) %collective-permute-start.17) | collective-permute-done | bytes 36896 | tf_op jit(solution)/shard_map/ppermute | solution.py:36
  155.8 0.9 collective-permute-done.16
  156.8 1.2 shard_map.141
  (37 shorter events, 0.2 us)
Async XLA Ops:
  0.6 16.2 %copy-start.9 = (f32[64]{0:T(128)S(1)}, f32[64]{0:T(128)}, u32[]{:S(2)}) copy-start(f32[64]{0:T(128)} %param.13) | copy-start | bytes 772
  0.6 16.2 %copy-start.8 = (f32[64]{0:T(128)S(1)}, f32[64]{0:T(128)}, u32[]{:S(2)}) copy-start(f32[64]{0:T(128)} %param.11) | copy-start | bytes 772
  0.7 1.1 copy-start
  1.7 0.9 copy-start.2
  2.7 14.2 %copy-start.5 = (bf16[64,64]{1,0:T(8,128)(2,1)S(1)}, bf16[64,64]{1,0:T(8,128)(2,1)}, u32[]{:S(2)}) copy-start(bf16[64,64]{1,0:T(8,128)(2,1)} %w2b.3) | copy-start | bytes 24580
  2.7 14.2 %copy-start.6 = (bf16[3,3,64,6]{2,3,1,0:T(8,128)(2,1)S(1)}, bf16[3,3,64,6]{2,3,1,0:T(8,128)(2,1)}, u32[]{:S(2)}) copy-start(bf16[3,3,64,6]{2,3,1,0:T(8,128)(2,1)} %param.14) | copy-start | bytes 20740
  2.7 14.2 %copy-start.7 = (bf16[3,3,2,64]{3,2,1,0:T(2,128)(2,1)S(1)}, bf16[3,3,2,64]{3,2,1,0:T(2,128)(2,1)}, u32[]{:S(2)}) copy-start(bf16[3,3,2,64]{3,2,1,0:T(2,128)(2,1)} %w1_in.1) | copy-start | bytes 6916
  2.7 22.5 %copy-start.1 = (f32[1,2,2,256,128]{4,3,2,1,0:T(8,128)S(1)}, f32[1,2,2,256,128]{4,3,2,1,0:T(8,128)}, u32[]{:S(2)}) copy-start(f32[1,2,2,256,128]{4,3,2,1,0:T(8,128)} %param.9) | copy-start | bytes 1572868
  2.7 22.5 %copy-start.3 = (f32[1,2,256,128]{3,2,1,0:T(8,128)S(1)}, f32[1,2,256,128]{3,2,1,0:T(8,128)}, u32[]{:S(2)}) copy-start(f32[1,2,256,128]{3,2,1,0:T(8,128)} %param.8) | copy-start | bytes 786436
  2.9 9.4 %collective-permute-start = (f32[4,32,256]{2,1,0:T(8,128)S(1)}, f32[4,32,256]{2,1,0:T(8,128)S(1)}, u32[]{:S(2)}, u32[]{:S(2)}) collective-permute-start(f32[4,32,256]{2,1,0:T(8,128)S(1)} %get-tuple-element.38), channel_id=1, source_target_pairs={{0,1},{1,2},{2,3},{3,0},{4,5},{5,6},{6,7},{7,4},{8,9},{9,10},{10,1... | collective-permute-start | bytes 393224 | tf_op jit(solution)/shard_map/ppermute | solution.py:36
  6.0 63.4 %copy-start.4 = (s32[16,2176]{1,0:T(8,128)S(1)}, s32[16,2176]{1,0:T(8,128)}, u32[]{:S(2)}) copy-start(s32[16,2176]{1,0:T(8,128)} %constant.13.clone.place_ref) | copy-start | bytes 417796
  6.0 7.8 %collective-permute-start.1 = (f32[4,32,256]{2,1,0:T(8,128)S(1)}, f32[4,32,256]{2,1,0:T(8,128)S(1)}, u32[]{:S(2)}, u32[]{:S(2)}) collective-permute-start(f32[4,32,256]{2,1,0:T(8,128)S(1)} %get-tuple-element.39), channel_id=1, source_target_pairs={{0,3},{1,0},{2,1},{3,2},{4,7},{5,4},{6,5},{7,6},{8,11},{9,8},{10,9... | collective-permute-start | bytes 393224 | tf_op jit(solution)/shard_map/ppermute | solution.py:36
  13.8 8.8 %collective-permute-start.2 = (f32[4,96,128]{2,1,0:T(8,128)S(1)}, f32[4,96,128]{2,1,0:T(8,128)S(1)}, u32[]{:S(2)}, u32[]{:S(2)}) collective-permute-start(f32[4,96,128]{2,1,0:T(8,128)S(1)} %pad_maximum_fusion), channel_id=1, source_target_pairs={{0,4},{4,8},{8,12},{12,0},{1,5},{5,9},{9,13},{13,1},{2,6},{6,10},{... | collective-permute-start | bytes 589832 | tf_op jit(solution)/shard_map/ppermute | solution.py:36
  15.3 9.9 %collective-permute-start.3 = (f32[4,96,128]{2,1,0:T(8,128)S(1)}, f32[4,96,128]{2,1,0:T(8,128)S(1)}, u32[]{:S(2)}, u32[]{:S(2)}) collective-permute-start(f32[4,96,128]{2,1,0:T(8,128)S(1)} %pad_maximum_fusion.1), channel_id=1, source_target_pairs={{0,12},{4,0},{8,4},{12,8},{1,13},{5,1},{9,5},{13,9},{2,14},{6,2},{... | collective-permute-start | bytes 589832 | tf_op jit(solution)/shard_map/ppermute | solution.py:36
  55.6 6.5 %collective-permute-start.4 = (f32[2,40,256]{2,1,0:T(8,128)S(1)}, f32[2,40,256]{2,1,0:T(8,128)S(1)}, u32[]{:S(2)}, u32[]{:S(2)}) collective-permute-start(f32[2,40,256]{2,1,0:T(8,128)S(1)} %get-tuple-element.46), channel_id=1, source_target_pairs={{0,1},{1,2},{2,3},{3,0},{4,5},{5,6},{6,7},{7,4},{8,9},{9,10},{10,1... | collective-permute-start | bytes 245768 | tf_op jit(solution)/shard_map/ppermute | solution.py:36
  57.4 5.3 %collective-permute-start.5 = (f32[2,40,256]{2,1,0:T(8,128)S(1)}, f32[2,40,256]{2,1,0:T(8,128)S(1)}, u32[]{:S(2)}, u32[]{:S(2)}) collective-permute-start(f32[2,40,256]{2,1,0:T(8,128)S(1)} %get-tuple-element.47), channel_id=1, source_target_pairs={{0,3},{1,0},{2,1},{3,2},{4,7},{5,4},{6,5},{7,6},{8,11},{9,8},{10,9... | collective-permute-start | bytes 245768 | tf_op jit(solution)/shard_map/ppermute | solution.py:36
  62.7 5.8 %collective-permute-start.6 = (f32[2,120,128]{2,1,0:T(8,128)S(1)}, f32[2,120,128]{2,1,0:T(8,128)S(1)}, u32[]{:S(2)}, u32[]{:S(2)}) collective-permute-start(f32[2,120,128]{2,1,0:T(8,128)S(1)} %pad_maximum_fusion.2), channel_id=1, source_target_pairs={{0,4},{4,8},{8,12},{12,0},{1,5},{5,9},{9,13},{13,1},{2,6},{6,10},{... | collective-permute-start | bytes 368648 | tf_op jit(solution)/shard_map/ppermute | solution.py:36
  64.3 5.1 %collective-permute-start.7 = (f32[2,120,128]{2,1,0:T(8,128)S(1)}, f32[2,120,128]{2,1,0:T(8,128)S(1)}, u32[]{:S(2)}, u32[]{:S(2)}) collective-permute-start(f32[2,120,128]{2,1,0:T(8,128)S(1)} %pad_maximum_fusion.3), channel_id=1, source_target_pairs={{0,12},{4,0},{8,4},{12,8},{1,13},{5,1},{9,5},{13,9},{2,14},{6,2},{... | collective-permute-start | bytes 368648 | tf_op jit(solution)/shard_map/ppermute | solution.py:36
  99.5 6.0 %collective-permute-start.8 = (f32[2,24,256]{2,1,0:T(8,128)S(1)}, f32[2,24,256]{2,1,0:T(8,128)S(1)}, u32[]{:S(2)}, u32[]{:S(2)}) collective-permute-start(f32[2,24,256]{2,1,0:T(8,128)S(1)} %get-tuple-element.55), channel_id=1, source_target_pairs={{0,1},{1,2},{2,3},{3,0},{4,5},{5,6},{6,7},{7,4},{8,9},{9,10},{10,1... | collective-permute-start | bytes 147464 | tf_op jit(solution)/shard_map/ppermute | solution.py:36
  99.6 5.9 %collective-permute-start.9 = (f32[2,24,256]{2,1,0:T(8,128)S(1)}, f32[2,24,256]{2,1,0:T(8,128)S(1)}, u32[]{:S(2)}, u32[]{:S(2)}) collective-permute-start(f32[2,24,256]{2,1,0:T(8,128)S(1)} %get-tuple-element.56), channel_id=1, source_target_pairs={{0,3},{1,0},{2,1},{3,2},{4,7},{5,4},{6,5},{7,6},{8,11},{9,8},{10,9... | collective-permute-start | bytes 147464 | tf_op jit(solution)/shard_map/ppermute | solution.py:36
  105.6 5.3 %collective-permute-start.10 = (f32[2,72,128]{2,1,0:T(8,128)S(1)}, f32[2,72,128]{2,1,0:T(8,128)S(1)}, u32[]{:S(2)}, u32[]{:S(2)}) collective-permute-start(f32[2,72,128]{2,1,0:T(8,128)S(1)} %pad_maximum_fusion.4), channel_id=1, source_target_pairs={{0,4},{4,8},{8,12},{12,0},{1,5},{5,9},{9,13},{13,1},{2,6},{6,10},{... | collective-permute-start | bytes 221192 | tf_op jit(solution)/shard_map/ppermute | solution.py:36
  107.0 4.4 %collective-permute-start.11 = (f32[2,72,128]{2,1,0:T(8,128)S(1)}, f32[2,72,128]{2,1,0:T(8,128)S(1)}, u32[]{:S(2)}, u32[]{:S(2)}) collective-permute-start(f32[2,72,128]{2,1,0:T(8,128)S(1)} %pad_maximum_fusion.5), channel_id=1, source_target_pairs={{0,12},{4,0},{8,4},{12,8},{1,13},{5,1},{9,5},{13,9},{2,14},{6,2},{... | collective-permute-start | bytes 221192 | tf_op jit(solution)/shard_map/ppermute | solution.py:36
  137.7 1.2 collective-permute-start.12
  138.9 4.3 %collective-permute-start.15 = (f32[72,128]{1,0:T(8,128)S(1)}, f32[72,128]{1,0:T(8,128)S(1)}, u32[]{:S(2)}, u32[]{:S(2)}) collective-permute-start(f32[72,128]{1,0:T(8,128)S(1)} %add.44), channel_id=1, source_target_pairs={{0,12},{4,0},{8,4},{12,8},{1,13},{5,1},{9,5},{13,9},{2,14},{6,2},{... | collective-permute-start | bytes 110600 | tf_op jit(solution)/shard_map/ppermute | solution.py:36
  141.3 4.0 %collective-permute-start.14 = (f32[72,128]{1,0:T(8,128)S(1)}, f32[72,128]{1,0:T(8,128)S(1)}, u32[]{:S(2)}, u32[]{:S(2)}) collective-permute-start(f32[72,128]{1,0:T(8,128)S(1)} %add.44), channel_id=1, source_target_pairs={{0,8},{4,12},{8,0},{12,4},{1,9},{5,13},{9,1},{13,5},{2,10},{6,14},... | collective-permute-start | bytes 110600 | tf_op jit(solution)/shard_map/ppermute | solution.py:36
  142.4 4.9 %collective-permute-start.13 = (f32[72,128]{1,0:T(8,128)S(1)}, f32[72,128]{1,0:T(8,128)S(1)}, u32[]{:S(2)}, u32[]{:S(2)}) collective-permute-start(f32[72,128]{1,0:T(8,128)S(1)} %add.44), channel_id=1, source_target_pairs={{0,4},{4,8},{8,12},{12,0},{1,5},{5,9},{9,13},{13,1},{2,6},{6,10},{... | collective-permute-start | bytes 110600 | tf_op jit(solution)/shard_map/ppermute | solution.py:36
  147.2 5.4 %collective-permute-start.18 = (f32[72,128]{1,0:T(8,128)S(1)}, f32[72,128]{1,0:T(8,128)S(1)}, u32[]{:S(2)}, u32[]{:S(2)}) collective-permute-start(f32[72,128]{1,0:T(8,128)S(1)} %add_add_fusion.1), channel_id=1, source_target_pairs={{0,3},{1,0},{2,1},{3,2},{4,7},{5,4},{6,5},{7,6},{8,11},{9,8},{10,9... | collective-permute-start | bytes 110600 | tf_op jit(solution)/shard_map/ppermute | solution.py:36
  151.0 4.9 %collective-permute-start.17 = (f32[72,128]{1,0:T(8,128)S(1)}, f32[72,128]{1,0:T(8,128)S(1)}, u32[]{:S(2)}, u32[]{:S(2)}) collective-permute-start(f32[72,128]{1,0:T(8,128)S(1)} %add_add_fusion.1), channel_id=1, source_target_pairs={{0,2},{1,3},{2,0},{3,1},{4,6},{5,7},{6,4},{7,5},{8,10},{9,11},{10,... | collective-permute-start | bytes 110600 | tf_op jit(solution)/shard_map/ppermute | solution.py:36
  151.0 5.8 %collective-permute-start.16 = (f32[72,128]{1,0:T(8,128)S(1)}, f32[72,128]{1,0:T(8,128)S(1)}, u32[]{:S(2)}, u32[]{:S(2)}) collective-permute-start(f32[72,128]{1,0:T(8,128)S(1)} %add_add_fusion.1), channel_id=1, source_target_pairs={{0,1},{1,2},{2,3},{3,0},{4,5},{5,6},{6,7},{7,4},{8,9},{9,10},{10,1... | collective-permute-start | bytes 110600 | tf_op jit(solution)/shard_map/ppermute | solution.py:36

commit v7 on v6

--- a/solution.py
+++ b/solution.py
@@ -453,7 +453,6 @@
 def second_kernel(plan, v_ref, force_ref, w1, b1, w2, b2, w3, out_ref, low_ref, high_ref, coefs_ref, inputs_ref, window_ref,
                   terms_ref, one_ref, two_ref):
     keep_inputs([v_ref[0], v_ref[1]], inputs_ref)
-    coefs_ref[...] = jnp.zeros_like(coefs_ref)
     network(plan, inputs_ref, (w1, b1, w2, b2, w3), coefs_ref, window_ref, terms_ref, one_ref, two_ref)
     low, tall = TOP - 8, plan.rows + 16
     v = [v_ref[comp, low : low + tall] for comp in range(2)]

time: 158 us -> 158 us (level)
  no operation moved by 1% of the time
where the time goes in v7:
time: 158 us
  Pallas kernels  88.1 us (56%)
  waiting for transfers between devices  36.6 us (23%)
  starting transfers between devices  30.1 us (19%)
  local copies, waits for them, and re-layouts  2.11 us (1%)
    pallas_call x7, Pallas kernels, call(): pl.pallas_call(kernel, out_shape=[jax.ShapeDtypeStruct(shape, F32 if shap...  88.1 us
    ppermute x19, waiting for transfers between devices, passed_along(): return lax.ppermute(block, axis, route)  36.6 us
    ppermute x19, starting transfers between devices, passed_along(): return lax.ppermute(block, axis, route)  30.1 us
  transfers between devices with their start and end apart: 19, of which 18 were waited for; matrix products, arithmetic and copies ran while one was open for 0% of the time, Pallas kernels for 0%

profile of v7, /device:TPU:0, one launch (start us, length us, event | category | flops | bytes accessed | tf_op | source)
XLA Modules:
  0.0 157.8 jit_solution(11408776516081644785)
XLA Ops:
  0.7 1.0 copy-done
  1.7 0.9 copy-done.2
  2.7 0.2 shard_map.135
  2.9 3.1 %collective-permute-start = (f32[4,32,256]{2,1,0:T(8,128)S(1)}, f32[4,32,256]{2,1,0:T(8,128)S(1)}, u32[]{:S(2)}, u32[]{:S(2)}) collective-permute-start(f32[4,32,256]{2,1,0:T(8,128)S(1)} %get-tuple-element.38), channel_id=1, source_target_pairs={{0,1},{1,2},{2,3},{3,0},{4,5},{5,6},{6,7},{7,4},{8,9},{9,10},{10,1... | collective-permute-start | bytes 393224 | tf_op jit(solution)/shard_map/ppermute | solution.py:36
  6.0 2.1 %collective-permute-start.1 = (f32[4,32,256]{2,1,0:T(8,128)S(1)}, f32[4,32,256]{2,1,0:T(8,128)S(1)}, u32[]{:S(2)}, u32[]{:S(2)}) collective-permute-start(f32[4,32,256]{2,1,0:T(8,128)S(1)} %get-tuple-element.39), channel_id=1, source_target_pairs={{0,3},{1,0},{2,1},{3,2},{4,7},{5,4},{6,5},{7,6},{8,11},{9,8},{10,9... | collective-permute-start | bytes 393224 | tf_op jit(solution)/shard_map/ppermute | solution.py:36
  8.1 4.2 %collective-permute-done.left = f32[4,32,256]{2,1,0:T(8,128)S(1)} collective-permute-done((f32[4,32,256]{2,1,0:T(8,128)S(1)}, f32[4,32,256]{2,1,0:T(8,128)S(1)}, u32[]{:S(2)}, u32[]{:S(2)}) %collective-permute-start) | collective-permute-done | bytes 131104 | tf_op jit(solution)/shard_map/ppermute | solution.py:36
  12.3 1.4 collective-permute-done.1.right
  13.8 1.5 collective-permute-start.2
  15.3 1.5 collective-permute-start.3
  16.8 0.1 shard_map.136
  17.0 0.1 multiply_sine_fusion.force_ref.goal_ref.extra_ref
  17.0 5.5 %collective-permute-done.2.above = f32[4,96,128]{2,1,0:T(8,128)S(1)} collective-permute-done((f32[4,96,128]{2,1,0:T(8,128)S(1)}, f32[4,96,128]{2,1,0:T(8,128)S(1)}, u32[]{:S(2)}, u32[]{:S(2)}) %collective-permute-start.2) | collective-permute-done | bytes 196640 | tf_op jit(solution)/shard_map/ppermute | solution.py:36
  22.6 2.6 %collective-permute-done.3.below = f32[4,96,128]{2,1,0:T(8,128)S(1)} collective-permute-done((f32[4,96,128]{2,1,0:T(8,128)S(1)}, f32[4,96,128]{2,1,0:T(8,128)S(1)}, u32[]{:S(2)}, u32[]{:S(2)}) %collective-permute-start.3) | collective-permute-done | bytes 196640 | tf_op jit(solution)/shard_map/ppermute | solution.py:36
  25.2 19.2 %shard_map.137 = (f32[2,336,256]{2,1,0:T(8,128)S(1)}, f32[2,336,256]{2,1,0:T(8,128)S(1)}, f32[2,336,256]{2,1,0:T(8,128)S(1)}, f32[2,2688,128]{2,1,0:T(8,128)S(1)...) custom-call(f32[4,32,256]{2,1,0:T(8,128)S(1)} %collective-permute-done.left, ...), custom_call_target="tpu_custom_call" | custom-call | tf_op jit(solution)/shard_map/pallas_call | solution.py:545
  44.4 11.0 %shard_map.138 = (f32[2,256,128]{2,1,0:T(8,128)S(1)}, f32[2,40,256]{2,1,0:T(8,128)S(1)}, f32[2,40,256]{2,1,0:T(8,128)S(1)}, f32[2,2688,128]{2,1,0:T(8,128)S(1)}) custom-call(f32[2,336,256]{2,1,0:T(8,128)S(1)} %get-tuple-element.45.v_ref, f32[1,256]{1,0:T(1,128)S(1)} %multiply_sine_fusion.force_ref.goal_ref.extra_ref, ...), custom_call_target="tpu_custom_call" | custom-call | tf_op jit(solution)/shard_map/pallas_call | solution.py:545
  55.4 1.8 %collective-permute-start.4 = (f32[2,40,256]{2,1,0:T(8,128)S(1)}, f32[2,40,256]{2,1,0:T(8,128)S(1)}, u32[]{:S(2)}, u32[]{:S(2)}) collective-permute-start(f32[2,40,256]{2,1,0:T(8,128)S(1)} %get-tuple-element.46), channel_id=1, source_target_pairs={{0,1},{1,2},{2,3},{3,0},{4,5},{5,6},{6,7},{7,4},{8,9},{9,10},{10,1... | collective-permute-start | bytes 245768 | tf_op jit(solution)/shard_map/ppermute | solution.py:36
  57.2 2.1 %collective-permute-start.5 = (f32[2,40,256]{2,1,0:T(8,128)S(1)}, f32[2,40,256]{2,1,0:T(8,128)S(1)}, u32[]{:S(2)}, u32[]{:S(2)}) collective-permute-start(f32[2,40,256]{2,1,0:T(8,128)S(1)} %get-tuple-element.47), channel_id=1, source_target_pairs={{0,3},{1,0},{2,1},{3,2},{4,7},{5,4},{6,5},{7,6},{8,11},{9,8},{10,9... | collective-permute-start | bytes 245768 | tf_op jit(solution)/shard_map/ppermute | solution.py:36
  59.3 2.6 %collective-permute-done.4.left = f32[2,40,256]{2,1,0:T(8,128)S(1)} collective-permute-done((f32[2,40,256]{2,1,0:T(8,128)S(1)}, f32[2,40,256]{2,1,0:T(8,128)S(1)}, u32[]{:S(2)}, u32[]{:S(2)}) %collective-permute-start.4) | collective-permute-done | bytes 81952 | tf_op jit(solution)/shard_map/ppermute | solution.py:36
  61.8 0.7 collective-permute-done.5.right
  62.5 1.5 collective-permute-start.6
  64.1 1.7 %collective-permute-start.7 = (f32[2,120,128]{2,1,0:T(8,128)S(1)}, f32[2,120,128]{2,1,0:T(8,128)S(1)}, u32[]{:S(2)}, u32[]{:S(2)}) collective-permute-start(f32[2,120,128]{2,1,0:T(8,128)S(1)} %pad_maximum_fusion.3), channel_id=1, source_target_pairs={{0,12},{4,0},{8,4},{12,8},{1,13},{5,1},{9,5},{13,9},{2,14},{6,2},{... | collective-permute-start | bytes 368648 | tf_op jit(solution)/shard_map/ppermute | solution.py:36
  65.8 2.6 %collective-permute-done.6.above = f32[2,120,128]{2,1,0:T(8,128)S(1)} collective-permute-done((f32[2,120,128]{2,1,0:T(8,128)S(1)}, f32[2,120,128]{2,1,0:T(8,128)S(1)}, u32[]{:S(2)}, u32[]{:S(2)}) %collective-permute-start.6) | collective-permute-done | bytes 122912 | tf_op jit(solution)/shard_map/ppermute | solution.py:36
  68.4 0.8 collective-permute-done.7.below
  69.2 30.1 %shard_map.139 = (f32[2,256,128]{2,1,0:T(8,128)S(1)}, f32[2,24,256]{2,1,0:T(8,128)S(1)}, f32[2,24,256]{2,1,0:T(8,128)S(1)}, f32[72,128]{1,0:T(8,128)S(1)}) custom-call(f32[2,40,256]{2,1,0:T(8,128)S(1)} %collective-permute-done.4.left, f32[2,40,256]{2,1,0:T(8,128)S(1)} %collective-permute-done.5.right, f32[2,120,128]{2,1,0:T(8,128)S(1)} %collective-permute-done.6.above, ...), custom_call_target="tpu_custom_call" | custom-call | tf_op jit(solution)/shard_map/pallas_call | solution.py:545
  99.3 0.1 collective-permute-start.8
  99.4 3.7 %collective-permute-start.9 = (f32[2,24,256]{2,1,0:T(8,128)S(1)}, f32[2,24,256]{2,1,0:T(8,128)S(1)}, u32[]{:S(2)}, u32[]{:S(2)}) collective-permute-start(f32[2,24,256]{2,1,0:T(8,128)S(1)} %get-tuple-element.56), channel_id=1, source_target_pairs={{0,3},{1,0},{2,1},{3,2},{4,7},{5,4},{6,5},{7,6},{8,11},{9,8},{10,9... | collective-permute-start | bytes 147464 | tf_op jit(solution)/shard_map/ppermute | solution.py:36
  103.2 2.2 %collective-permute-done.8.left = f32[2,24,256]{2,1,0:T(8,128)S(1)} collective-permute-done((f32[2,24,256]{2,1,0:T(8,128)S(1)}, f32[2,24,256]{2,1,0:T(8,128)S(1)}, u32[]{:S(2)}, u32[]{:S(2)}) %collective-permute-start.8) | collective-permute-done | bytes 49184 | tf_op jit(solution)/shard_map/ppermute | solution.py:36
  105.3 0.0 collective-permute-done.9.right
  105.4 1.4 collective-permute-start.10
  106.8 1.6 collective-permute-start.11
  108.4 2.3 %collective-permute-done.10.above = f32[2,72,128]{2,1,0:T(8,128)S(1)} collective-permute-done((f32[2,72,128]{2,1,0:T(8,128)S(1)}, f32[2,72,128]{2,1,0:T(8,128)S(1)}, u32[]{:S(2)}, u32[]{:S(2)}) %collective-permute-start.10) | collective-permute-done | bytes 73760 | tf_op jit(solution)/shard_map/ppermute | solution.py:36
  110.7 0.5 collective-permute-done.11.below
  111.2 26.3 %shard_map.140 = (f32[2,256,128]{2,1,0:T(8,128)}, f32[1,8,128]{2,1,0:T(8,128)}, f32[1,8,128]{2,1,0:T(8,128)}, f32[72,128]{1,0:T(8,128)S(1)}) custom-call(f32[2,24,256]{2,1,0:T(8,128)S(1)} %collective-permute-done.8.left, f32[2,24,256]{2,1,0:T(8,128)S(1)} %collective-permute-done.9.right, f32[2,72,128]{2,1,0:T(8,128)S(1)} %collective-permute-done.10.above, ...), custom_call_target="tpu_custom_call" | custom-call | tf_op jit(solution)/shard_map/pallas_call | solution.py:545
  137.5 0.0 collective-permute-start.12
  137.5 1.2 collective-permute-done.12
  138.7 2.5 %collective-permute-start.15 = (f32[72,128]{1,0:T(8,128)S(1)}, f32[72,128]{1,0:T(8,128)S(1)}, u32[]{:S(2)}, u32[]{:S(2)}) collective-permute-start(f32[72,128]{1,0:T(8,128)S(1)} %add.44), channel_id=1, source_target_pairs={{0,12},{4,0},{8,4},{12,8},{1,13},{5,1},{9,5},{13,9},{2,14},{6,2},{... | collective-permute-start | bytes 110600 | tf_op jit(solution)/shard_map/ppermute | solution.py:36
  141.2 1.0 collective-permute-start.14
  142.2 0.0 collective-permute-start.13
  142.2 0.8 collective-permute-done.15
  143.0 2.1 %collective-permute-done.14 = f32[72,128]{1,0:T(8,128)S(1)} collective-permute-done((f32[72,128]{1,0:T(8,128)S(1)}, f32[72,128]{1,0:T(8,128)S(1)}, u32[]{:S(2)}, u32[]{:S(2)}) %collective-permute-start.14) | collective-permute-done | bytes 36896 | tf_op jit(solution)/shard_map/ppermute | solution.py:36
  145.1 1.9 %collective-permute-done.13 = f32[72,128]{1,0:T(8,128)S(1)} collective-permute-done((f32[72,128]{1,0:T(8,128)S(1)}, f32[72,128]{1,0:T(8,128)S(1)}, u32[]{:S(2)}, u32[]{:S(2)}) %collective-permute-start.13) | collective-permute-done | bytes 36896 | tf_op jit(solution)/shard_map/ppermute | solution.py:36
  147.1 3.7 %collective-permute-start.18 = (f32[72,128]{1,0:T(8,128)S(1)}, f32[72,128]{1,0:T(8,128)S(1)}, u32[]{:S(2)}, u32[]{:S(2)}) collective-permute-start(f32[72,128]{1,0:T(8,128)S(1)} %add_add_fusion.1), channel_id=1, source_target_pairs={{0,3},{1,0},{2,1},{3,2},{4,7},{5,4},{6,5},{7,6},{8,11},{9,8},{10,9... | collective-permute-start | bytes 110600 | tf_op jit(solution)/shard_map/ppermute | solution.py:36
  150.8 0.0 collective-permute-start.17
  150.8 0.6 collective-permute-start.16
  151.5 1.0 collective-permute-done.18
  152.5 3.2 %collective-permute-done.17 = f32[72,128]{1,0:T(8,128)S(1)} collective-permute-done((f32[72,128]{1,0:T(8,128)S(1)}, f32[72,128]{1,0:T(8,128)S(1)}, u32[]{:S(2)}, u32[]{:S(2)}) %collective-permute-start.17) | collective-permute-done | bytes 36896 | tf_op jit(solution)/shard_map/ppermute | solution.py:36
  155.7 0.9 collective-permute-done.16
  156.6 1.2 shard_map.141
  (37 shorter events, 0.2 us)
Async XLA Ops:
  0.6 16.2 %copy-start.9 = (f32[64]{0:T(128)S(1)}, f32[64]{0:T(128)}, u32[]{:S(2)}) copy-start(f32[64]{0:T(128)} %param.13) | copy-start | bytes 772
  0.6 16.2 %copy-start.8 = (f32[64]{0:T(128)S(1)}, f32[64]{0:T(128)}, u32[]{:S(2)}) copy-start(f32[64]{0:T(128)} %param.11) | copy-start | bytes 772
  0.7 1.1 copy-start
  1.7 0.9 copy-start.2
  2.7 14.2 %copy-start.5 = (bf16[64,64]{1,0:T(8,128)(2,1)S(1)}, bf16[64,64]{1,0:T(8,128)(2,1)}, u32[]{:S(2)}) copy-start(bf16[64,64]{1,0:T(8,128)(2,1)} %w2b.3) | copy-start | bytes 24580
  2.7 14.2 %copy-start.6 = (bf16[3,3,64,6]{2,3,1,0:T(8,128)(2,1)S(1)}, bf16[3,3,64,6]{2,3,1,0:T(8,128)(2,1)}, u32[]{:S(2)}) copy-start(bf16[3,3,64,6]{2,3,1,0:T(8,128)(2,1)} %param.14) | copy-start | bytes 20740
  2.7 14.2 %copy-start.7 = (bf16[3,3,2,64]{3,2,1,0:T(2,128)(2,1)S(1)}, bf16[3,3,2,64]{3,2,1,0:T(2,128)(2,1)}, u32[]{:S(2)}) copy-start(bf16[3,3,2,64]{3,2,1,0:T(2,128)(2,1)} %w1_in.1) | copy-start | bytes 6916
  2.7 22.5 %copy-start.1 = (f32[1,2,2,256,128]{4,3,2,1,0:T(8,128)S(1)}, f32[1,2,2,256,128]{4,3,2,1,0:T(8,128)}, u32[]{:S(2)}) copy-start(f32[1,2,2,256,128]{4,3,2,1,0:T(8,128)} %param.9) | copy-start | bytes 1572868
  2.7 22.5 %copy-start.3 = (f32[1,2,256,128]{3,2,1,0:T(8,128)S(1)}, f32[1,2,256,128]{3,2,1,0:T(8,128)}, u32[]{:S(2)}) copy-start(f32[1,2,256,128]{3,2,1,0:T(8,128)} %param.8) | copy-start | bytes 786436
  2.9 9.4 %collective-permute-start = (f32[4,32,256]{2,1,0:T(8,128)S(1)}, f32[4,32,256]{2,1,0:T(8,128)S(1)}, u32[]{:S(2)}, u32[]{:S(2)}) collective-permute-start(f32[4,32,256]{2,1,0:T(8,128)S(1)} %get-tuple-element.38), channel_id=1, source_target_pairs={{0,1},{1,2},{2,3},{3,0},{4,5},{5,6},{6,7},{7,4},{8,9},{9,10},{10,1... | collective-permute-start | bytes 393224 | tf_op jit(solution)/shard_map/ppermute | solution.py:36
  6.0 63.2 %copy-start.4 = (s32[16,2176]{1,0:T(8,128)S(1)}, s32[16,2176]{1,0:T(8,128)}, u32[]{:S(2)}) copy-start(s32[16,2176]{1,0:T(8,128)} %constant.13.clone.place_ref) | copy-start | bytes 417796
  6.0 7.8 %collective-permute-start.1 = (f32[4,32,256]{2,1,0:T(8,128)S(1)}, f32[4,32,256]{2,1,0:T(8,128)S(1)}, u32[]{:S(2)}, u32[]{:S(2)}) collective-permute-start(f32[4,32,256]{2,1,0:T(8,128)S(1)} %get-tuple-element.39), channel_id=1, source_target_pairs={{0,3},{1,0},{2,1},{3,2},{4,7},{5,4},{6,5},{7,6},{8,11},{9,8},{10,9... | collective-permute-start | bytes 393224 | tf_op jit(solution)/shard_map/ppermute | solution.py:36
  13.8 8.8 %collective-permute-start.2 = (f32[4,96,128]{2,1,0:T(8,128)S(1)}, f32[4,96,128]{2,1,0:T(8,128)S(1)}, u32[]{:S(2)}, u32[]{:S(2)}) collective-permute-start(f32[4,96,128]{2,1,0:T(8,128)S(1)} %pad_maximum_fusion), channel_id=1, source_target_pairs={{0,4},{4,8},{8,12},{12,0},{1,5},{5,9},{9,13},{13,1},{2,6},{6,10},{... | collective-permute-start | bytes 589832 | tf_op jit(solution)/shard_map/ppermute | solution.py:36
  15.3 9.9 %collective-permute-start.3 = (f32[4,96,128]{2,1,0:T(8,128)S(1)}, f32[4,96,128]{2,1,0:T(8,128)S(1)}, u32[]{:S(2)}, u32[]{:S(2)}) collective-permute-start(f32[4,96,128]{2,1,0:T(8,128)S(1)} %pad_maximum_fusion.1), channel_id=1, source_target_pairs={{0,12},{4,0},{8,4},{12,8},{1,13},{5,1},{9,5},{13,9},{2,14},{6,2},{... | collective-permute-start | bytes 589832 | tf_op jit(solution)/shard_map/ppermute | solution.py:36
  55.4 6.5 %collective-permute-start.4 = (f32[2,40,256]{2,1,0:T(8,128)S(1)}, f32[2,40,256]{2,1,0:T(8,128)S(1)}, u32[]{:S(2)}, u32[]{:S(2)}) collective-permute-start(f32[2,40,256]{2,1,0:T(8,128)S(1)} %get-tuple-element.46), channel_id=1, source_target_pairs={{0,1},{1,2},{2,3},{3,0},{4,5},{5,6},{6,7},{7,4},{8,9},{9,10},{10,1... | collective-permute-start | bytes 245768 | tf_op jit(solution)/shard_map/ppermute | solution.py:36
  57.2 5.3 %collective-permute-start.5 = (f32[2,40,256]{2,1,0:T(8,128)S(1)}, f32[2,40,256]{2,1,0:T(8,128)S(1)}, u32[]{:S(2)}, u32[]{:S(2)}) collective-permute-start(f32[2,40,256]{2,1,0:T(8,128)S(1)} %get-tuple-element.47), channel_id=1, source_target_pairs={{0,3},{1,0},{2,1},{3,2},{4,7},{5,4},{6,5},{7,6},{8,11},{9,8},{10,9... | collective-permute-start | bytes 245768 | tf_op jit(solution)/shard_map/ppermute | solution.py:36
  62.5 5.8 %collective-permute-start.6 = (f32[2,120,128]{2,1,0:T(8,128)S(1)}, f32[2,120,128]{2,1,0:T(8,128)S(1)}, u32[]{:S(2)}, u32[]{:S(2)}) collective-permute-start(f32[2,120,128]{2,1,0:T(8,128)S(1)} %pad_maximum_fusion.2), channel_id=1, source_target_pairs={{0,4},{4,8},{8,12},{12,0},{1,5},{5,9},{9,13},{13,1},{2,6},{6,10},{... | collective-permute-start | bytes 368648 | tf_op jit(solution)/shard_map/ppermute | solution.py:36
  64.1 5.1 %collective-permute-start.7 = (f32[2,120,128]{2,1,0:T(8,128)S(1)}, f32[2,120,128]{2,1,0:T(8,128)S(1)}, u32[]{:S(2)}, u32[]{:S(2)}) collective-permute-start(f32[2,120,128]{2,1,0:T(8,128)S(1)} %pad_maximum_fusion.3), channel_id=1, source_target_pairs={{0,12},{4,0},{8,4},{12,8},{1,13},{5,1},{9,5},{13,9},{2,14},{6,2},{... | collective-permute-start | bytes 368648 | tf_op jit(solution)/shard_map/ppermute | solution.py:36
  99.3 6.0 %collective-permute-start.8 = (f32[2,24,256]{2,1,0:T(8,128)S(1)}, f32[2,24,256]{2,1,0:T(8,128)S(1)}, u32[]{:S(2)}, u32[]{:S(2)}) collective-permute-start(f32[2,24,256]{2,1,0:T(8,128)S(1)} %get-tuple-element.55), channel_id=1, source_target_pairs={{0,1},{1,2},{2,3},{3,0},{4,5},{5,6},{6,7},{7,4},{8,9},{9,10},{10,1... | collective-permute-start | bytes 147464 | tf_op jit(solution)/shard_map/ppermute | solution.py:36
  99.4 5.9 %collective-permute-start.9 = (f32[2,24,256]{2,1,0:T(8,128)S(1)}, f32[2,24,256]{2,1,0:T(8,128)S(1)}, u32[]{:S(2)}, u32[]{:S(2)}) collective-permute-start(f32[2,24,256]{2,1,0:T(8,128)S(1)} %get-tuple-element.56), channel_id=1, source_target_pairs={{0,3},{1,0},{2,1},{3,2},{4,7},{5,4},{6,5},{7,6},{8,11},{9,8},{10,9... | collective-permute-start | bytes 147464 | tf_op jit(solution)/shard_map/ppermute | solution.py:36
  105.4 5.3 %collective-permute-start.10 = (f32[2,72,128]{2,1,0:T(8,128)S(1)}, f32[2,72,128]{2,1,0:T(8,128)S(1)}, u32[]{:S(2)}, u32[]{:S(2)}) collective-permute-start(f32[2,72,128]{2,1,0:T(8,128)S(1)} %pad_maximum_fusion.4), channel_id=1, source_target_pairs={{0,4},{4,8},{8,12},{12,0},{1,5},{5,9},{9,13},{13,1},{2,6},{6,10},{... | collective-permute-start | bytes 221192 | tf_op jit(solution)/shard_map/ppermute | solution.py:36
  106.8 4.4 %collective-permute-start.11 = (f32[2,72,128]{2,1,0:T(8,128)S(1)}, f32[2,72,128]{2,1,0:T(8,128)S(1)}, u32[]{:S(2)}, u32[]{:S(2)}) collective-permute-start(f32[2,72,128]{2,1,0:T(8,128)S(1)} %pad_maximum_fusion.5), channel_id=1, source_target_pairs={{0,12},{4,0},{8,4},{12,8},{1,13},{5,1},{9,5},{13,9},{2,14},{6,2},{... | collective-permute-start | bytes 221192 | tf_op jit(solution)/shard_map/ppermute | solution.py:36
  137.5 1.2 collective-permute-start.12
  138.7 4.3 %collective-permute-start.15 = (f32[72,128]{1,0:T(8,128)S(1)}, f32[72,128]{1,0:T(8,128)S(1)}, u32[]{:S(2)}, u32[]{:S(2)}) collective-permute-start(f32[72,128]{1,0:T(8,128)S(1)} %add.44), channel_id=1, source_target_pairs={{0,12},{4,0},{8,4},{12,8},{1,13},{5,1},{9,5},{13,9},{2,14},{6,2},{... | collective-permute-start | bytes 110600 | tf_op jit(solution)/shard_map/ppermute | solution.py:36
  141.2 4.0 %collective-permute-start.14 = (f32[72,128]{1,0:T(8,128)S(1)}, f32[72,128]{1,0:T(8,128)S(1)}, u32[]{:S(2)}, u32[]{:S(2)}) collective-permute-start(f32[72,128]{1,0:T(8,128)S(1)} %add.44), channel_id=1, source_target_pairs={{0,8},{4,12},{8,0},{12,4},{1,9},{5,13},{9,1},{13,5},{2,10},{6,14},... | collective-permute-start | bytes 110600 | tf_op jit(solution)/shard_map/ppermute | solution.py:36
  142.2 4.9 %collective-permute-start.13 = (f32[72,128]{1,0:T(8,128)S(1)}, f32[72,128]{1,0:T(8,128)S(1)}, u32[]{:S(2)}, u32[]{:S(2)}) collective-permute-start(f32[72,128]{1,0:T(8,128)S(1)} %add.44), channel_id=1, source_target_pairs={{0,4},{4,8},{8,12},{12,0},{1,5},{5,9},{9,13},{13,1},{2,6},{6,10},{... | collective-permute-start | bytes 110600 | tf_op jit(solution)/shard_map/ppermute | solution.py:36
  147.1 5.4 %collective-permute-start.18 = (f32[72,128]{1,0:T(8,128)S(1)}, f32[72,128]{1,0:T(8,128)S(1)}, u32[]{:S(2)}, u32[]{:S(2)}) collective-permute-start(f32[72,128]{1,0:T(8,128)S(1)} %add_add_fusion.1), channel_id=1, source_target_pairs={{0,3},{1,0},{2,1},{3,2},{4,7},{5,4},{6,5},{7,6},{8,11},{9,8},{10,9... | collective-permute-start | bytes 110600 | tf_op jit(solution)/shard_map/ppermute | solution.py:36
  150.8 4.9 %collective-permute-start.17 = (f32[72,128]{1,0:T(8,128)S(1)}, f32[72,128]{1,0:T(8,128)S(1)}, u32[]{:S(2)}, u32[]{:S(2)}) collective-permute-start(f32[72,128]{1,0:T(8,128)S(1)} %add_add_fusion.1), channel_id=1, source_target_pairs={{0,2},{1,3},{2,0},{3,1},{4,6},{5,7},{6,4},{7,5},{8,10},{9,11},{10,... | collective-permute-start | bytes 110600 | tf_op jit(solution)/shard_map/ppermute | solution.py:36
  150.8 5.8 %collective-permute-start.16 = (f32[72,128]{1,0:T(8,128)S(1)}, f32[72,128]{1,0:T(8,128)S(1)}, u32[]{:S(2)}, u32[]{:S(2)}) collective-permute-start(f32[72,128]{1,0:T(8,128)S(1)} %add_add_fusion.1), channel_id=1, source_target_pairs={{0,1},{1,2},{2,3},{3,0},{4,5},{5,6},{6,7},{7,4},{8,9},{9,10},{10,1... | collective-permute-start | bytes 110600 | tf_op jit(solution)/shard_map/ppermute | solution.py:36
